TPU v7x, 128 devices: a whole 4x4x4 slice. The times are simulated.
128 devices in a mesh: tm: 32 (over x, y, core), col: 4 (over z).
Axes of the slice: x: 4, y: 4, z: 4, core: 2. Of those that a mesh axis runs over, the one named last changes fastest.
Arguments:
- blocks: float32 [128, 512, 512], P('tm', None, 'col'), as said below
- upper: float32 [128, 512, 512], P('tm', None, 'col'), as said below
- arrow: float32 [128, 64, 512], P('tm', None, 'col'), as said below
- tip: float32 [64, 64], replicated, as said below
- rhs: float32 [128, 512], P('tm'), may hold values from -1 to 1
- rhs_fixed: float32 [64], replicated, may hold values from -6 to 6
Outputs:
- solution: float32 [128, 512], P('tm', 'col')
- solution_fixed: float32 [64], replicated
- mean_log_det: float32 [], replicated
Inputs may be any that keep to these rules, and one draw needn't show every extreme that they name: blocks[t] is symmetric for every t, and the matrix Q assembled from blocks, upper, arrow and tip is positive definite. `upper`: Q assembled with these couplings is positive definite. `arrow`: Q assembled with these couplings is positive definite. tip is symmetric, and Q assembled with it is positive definite.
All inputs are finite; a program needn't handle non-finite values.
Results may differ from a plain program's by a relative error of at most 0.0003.
Values sent between devices are 32-bit elements; how exact they have to be, the bound alone decides.
No kernel may reach another device: no remote copies, remote signals or barrier semaphores. Data moves between devices by JAX's collectives and lax.ppermute only.
A program may use at most 192 MiB of HBM per device.

v0:
```python
import jax
import jax.numpy as jnp
from jax import lax
from jax.sharding import PartitionSpec as P


def copy_for_each(x, axis):
    copies = jnp.broadcast_to(x, (lax.axis_size(axis), *x.shape))
    return lax.all_to_all(copies, axis, split_axis=0, concat_axis=0, tiled=True)


def in_order(parts, dim):
    parts = jnp.moveaxis(parts, 0, dim)
    dims = parts.shape
    return parts.reshape(*dims[:dim], dims[dim] * dims[dim + 1], *dims[dim + 2 :])


def collect(x, axis, dim):
    parts = copy_for_each(x, axis)
    return in_order(parts, dim)


def sent_together(arrays, axis, dim, along):
    widths = [a.shape[along] for a in arrays]
    both = jnp.concatenate(arrays, axis=along)
    whole = collect(both, axis, dim)
    return tuple(jnp.split(whole, [sum(widths[:k]) for k in range(1, len(widths))], axis=along))


def shifted(block, axis, distance):
    devices = range(lax.axis_size(axis))
    route = [(i - distance, i) for i in devices if i - distance in devices]
    return lax.ppermute(block, axis, route)


def in_one_piece(arrays, axis, dim, along):
    both = jnp.concatenate(arrays, axis=along)
    whole, at, gathered = (lax.all_gather(both, axis, axis=dim, tiled=True), 0, [])
    for a in arrays:
        gathered.append(lax.slice_in_dim(whole, at, at + a.shape[along], axis=along))
        at += a.shape[along]
    return tuple(gathered)


def taken_together(x, axis):
    everything = copy_for_each(x, axis)
    return jnp.sum(everything, axis=0)


def in_one(arrays, axis):
    line, at, gathered = (jnp.concatenate([a.reshape(-1) for a in arrays]), 0, [])
    running = taken_together(line, axis)
    for a in arrays:
        gathered.append(running[at : at + a.size].reshape(a.shape))
        at += a.size
    return tuple(gathered)


def lower_solve(factor, right_side):
    return lax.linalg.triangular_solve(factor, right_side, left_side=True, lower=True)


def upper_solve(factor, right_side):
    return lax.linalg.triangular_solve(
        factor, right_side, left_side=True, lower=True, transpose_a=True
    )


def cross_product(first_operand, second_operand):
    return lax.dot_general(
        first_operand,
        second_operand,
        (((0,), (0,)), ((), ())),
        precision=lax.Precision.HIGHEST,
        preferred_element_type=jnp.float32,
    )


def apply_matrix(matrix, vector):
    return jnp.dot(
        matrix, vector, precision=lax.Precision.HIGHEST, preferred_element_type=jnp.float32
    )


def blocked_cholesky(matrix):
    order = matrix.shape[0]
    if order <= 128:
        return jnp.linalg.cholesky(matrix)
    half = order // 2
    top_factor = blocked_cholesky(matrix[:half, :half])
    panel = lax.linalg.triangular_solve(
        top_factor, matrix[half:, :half], left_side=False, lower=True, transpose_a=True
    )
    trailing = matrix[half:, half:] - lax.dot_general(
        panel,
        panel,
        (((1,), (1,)), ((), ())),
        precision=lax.Precision.HIGHEST,
        preferred_element_type=jnp.float32,
    )
    bottom_factor = blocked_cholesky(trailing)
    upper_rows = jnp.concatenate([top_factor, jnp.zeros((half, order - half), jnp.float32)], axis=1)
    lower_rows = jnp.concatenate([panel, bottom_factor], axis=1)
    return jnp.concatenate([upper_rows, lower_rows], axis=0)


def log_pivots(factor):
    return 2.0 * jnp.sum(jnp.log(jnp.diagonal(factor)))


def arrow_solve(factor, side_part, right_part):
    solved = lower_solve(factor, jnp.concatenate([side_part.T, right_part[:, None]], axis=1))
    return (solved[:, :-1], solved[:, -1])


def back_value(factor, right_solved, terms):
    return upper_solve(factor, (right_solved - terms)[:, None])[:, 0]


def transposed_coupling(local_part):
    flipped = local_part.T
    return flipped


def whole_panels(low_local, high_local):
    low_whole, high_whole = (low_local, high_local)
    return (low_whole, high_whole)


def per_device(blocks, upper, arrow, tip, rhs, rhs_fixed):
    step_count, node_count, slab_width = blocks.shape
    effect_count = tip.shape[0]
    part_count = lax.axis_size("tm")
    level_count = part_count.bit_length() - 1
    part_index = lax.axis_index("tm")
    offset = lax.axis_index("col") * slab_width
    zero_value = jnp.zeros((), jnp.float32)
    arrows = collect(arrow, "col", 2)
    received = lax.all_to_all(upper[0], "col", split_axis=0, concat_axis=1, tiled=True)
    coupling = received.T * (part_index > 0).astype(jnp.float32)
    diagonal = blocks[0]
    side_part = arrows[0]
    right_part = rhs[0]
    sent_diag = jnp.zeros((node_count, slab_width), jnp.float32)
    sent_side = jnp.zeros((effect_count, node_count), jnp.float32)
    sent_right = jnp.zeros((node_count,), jnp.float32)
    inner_tip = jnp.zeros((effect_count, effect_count), jnp.float32)
    inner_fixed = jnp.zeros((effect_count,), jnp.float32)
    inner_log = zero_value
    stored_rows = []
    for step_index in range(step_count - 1):
        whole_diag = collect(diagonal, "col", 1)
        factor = blocked_cholesky(whole_diag)
        inner_log = inner_log + log_pivots(factor)
        panels = lower_solve(factor, jnp.concatenate([coupling, upper[step_index + 1]], axis=1))
        fill_local = panels[:, :slab_width]
        next_local = panels[:, slab_width:]
        side_solved, right_solved = arrow_solve(factor, side_part, right_part)
        fill_whole, next_whole = sent_together((fill_local, next_local), "col", 1, 0)
        sent_diag = sent_diag + cross_product(fill_whole, fill_local)
        sent_side = sent_side + cross_product(side_solved, fill_whole)
        sent_right = sent_right + cross_product(fill_whole, right_solved)
        inner_tip = inner_tip + cross_product(side_solved, side_solved)
        inner_fixed = inner_fixed + cross_product(side_solved, right_solved)
        diagonal = blocks[step_index + 1] - cross_product(next_whole, next_local)
        coupling = -cross_product(next_whole, fill_local)
        side_part = arrows[step_index + 1] - cross_product(side_solved, next_whole)
        right_part = rhs[step_index + 1] - cross_product(next_whole, right_solved)
        stored_rows.append((factor, fill_whole, next_whole, side_solved, right_solved))
    got_diag, got_side, got_right = shifted((sent_diag, sent_side, sent_right), "tm", -1)
    diagonal = diagonal - got_diag
    side_part = side_part - got_side
    right_part = right_part - got_right
    tree_diag, tree_coupling = in_one_piece((diagonal, coupling), "col", 1, 0)
    tree_sums = (
        jnp.zeros((effect_count, effect_count), jnp.float32),
        jnp.zeros((effect_count,), jnp.float32),
        zero_value,
    )
    for level_index in range(level_count):
        stride = 1 << level_index
        position = (part_index + 1) % (2 * stride)
        leaving = position == stride
        from_upper = shifted(transposed_coupling(tree_coupling), "tm", -stride)
        factor = blocked_cholesky(tree_diag)
        column_count = tree_coupling.shape[1]
        panels = lower_solve(factor, jnp.concatenate([tree_coupling, from_upper], axis=1))
        low_local = panels[:, :column_count]
        high_local = panels[:, column_count:]
        side_solved, right_solved = arrow_solve(factor, side_part, right_part)
        low_whole, high_whole = whole_panels(low_local, high_local)
        own_tip = cross_product(side_solved, side_solved)
        own_fixed = cross_product(side_solved, right_solved)
        own_log = log_pivots(factor)
        downward = (
            cross_product(low_whole, low_local),
            cross_product(side_solved, low_whole),
            cross_product(low_whole, right_solved),
        )
        upward = (
            cross_product(high_whole, high_local),
            -cross_product(high_whole, low_local),
            cross_product(side_solved, high_whole),
            cross_product(high_whole, right_solved),
        )
        from_above = shifted((downward[0], downward[1], downward[2]), "tm", -stride)
        from_below = shifted((upward[0], upward[1], upward[2], upward[3]), "tm", stride)
        tree_diag = tree_diag - from_above[0] - from_below[0]
        tree_coupling = from_below[1]
        side_part = side_part - from_above[1] - from_below[2]
        right_part = right_part - from_above[2] - from_below[3]
        tree_sums = (
            tree_sums[0] + jnp.where(leaving, own_tip, 0.0),
            tree_sums[1] + jnp.where(leaving, own_fixed, 0.0),
            tree_sums[2] + jnp.where(leaving, own_log, 0.0),
        )
    is_root = part_index == part_count - 1
    factor = blocked_cholesky(tree_diag)
    side_solved, right_solved = arrow_solve(factor, side_part, right_part)
    root_tip = cross_product(side_solved, side_solved)
    root_fixed = cross_product(side_solved, right_solved)
    root_log = log_pivots(factor)
    order_total = step_count * part_count * node_count + effect_count
    total_tip, total_fixed, total_log = in_one(
        (
            inner_tip + tree_sums[0] + jnp.where(is_root, root_tip, 0.0),
            inner_fixed + tree_sums[1] + jnp.where(is_root, root_fixed, 0.0),
            inner_log + tree_sums[2] + jnp.where(is_root, root_log, 0.0),
        ),
        "tm",
    )
    fixed_factor = jnp.linalg.cholesky(tip - total_tip)
    solution_fixed = upper_solve(
        fixed_factor, lower_solve(fixed_factor, (rhs_fixed - total_fixed)[:, None])
    )[:, 0]
    log_total = total_log + log_pivots(fixed_factor)
    mean_log_det = log_total / order_total
    boundary_value = back_value(factor, right_solved, apply_matrix(side_solved, solution_fixed))
    prior_value = shifted(boundary_value, "tm", 1)
    solved_rows = [boundary_value]
    following = boundary_value
    for step_index in reversed(range(step_count - 1)):
        factor, fill_whole, next_whole, side_solved, right_solved = stored_rows[step_index]
        terms = (
            apply_matrix(fill_whole, prior_value)
            + apply_matrix(next_whole, following)
            + apply_matrix(side_solved, solution_fixed)
        )
        following = back_value(factor, right_solved, terms)
        solved_rows.insert(0, following)
    whole_rows = jnp.stack(solved_rows)
    solution = lax.dynamic_slice_in_dim(whole_rows, offset, slab_width, 1)
    return (solution, solution_fixed, mean_log_det)


def solution(mesh):
    placed = (
        P("tm", None, "col"),
        P("tm", None, "col"),
        P("tm", None, "col"),
        P(),
        P("tm", None),
        P(),
    )
    return jax.shard_map(
        per_device,
        mesh=mesh,
        in_specs=placed,
        out_specs=(P("tm", "col"), P(), P()),
        check_vma=False,
    )
```

profile of v0, /device:TPU:6, one launch (start us, length us, event | category | flops | bytes accessed | tf_op | source)
XLA Modules:
  0.0 2266.2 jit_solution(6952045541354148446)
XLA Ops:
  51.6 11.7 cholesky.586
  75.2 11.7 cholesky.597
  93.3 20.1 custom-call.92
  115.1 11.7 cholesky.608
  139.3 11.7 cholesky.619
  162.0 40.4 %custom-call.138 = f32[4,128,128]{1,2,0:T(8,128)S(1)} custom-call(f32[4,128,128]{2,1,0:T(8,128)} %copy-done.106), custom_call_target="InvertDiagBlocksLowerTriangular" | custom-call | tf_op jit(solution)/shard_map/triangular_solve/custom-call.9 | solution.py:64
  287.1 11.9 cholesky.641
  305.1 19.7 custom-call.97
  329.2 11.7 cholesky.652
  352.7 11.7 cholesky.663
  386.7 39.3 %custom-call.99 = f32[4,128,128]{1,2,0:T(8,128)S(1)} custom-call(f32[4,128,128]{2,1,0:T(8,128)S(1)} %get-tuple-element.204), custom_call_target="InvertDiagBlocksLowerTriangular" | custom-call | tf_op jit(solution)/shard_map/triangular_solve/custom-call.5 | solution.py:60
  514.9 12.5 cholesky.685
  537.6 20.7 custom-call.101
  570.1 13.2 cholesky.696
  604.8 13.2 cholesky.707
  624.4 14.0 while.64
  638.4 40.9 %custom-call.103 = f32[4,128,128]{1,2,0:T(8,128)} custom-call(f32[4,128,128]{2,1,0:T(8,128)} %get-tuple-element.206), custom_call_target="InvertDiagBlocksLowerTriangular" | custom-call | tf_op jit(solution)/shard_map/triangular_solve/custom-call.5 | solution.py:60
  788.9 11.7 cholesky.729
  806.7 19.9 custom-call.105
  831.0 11.7 cholesky.740
  855.2 11.7 cholesky.751
  889.3 14.0 while.66
  903.3 40.8 %custom-call.107 = f32[4,128,128]{1,2,0:T(8,128)} custom-call(f32[4,128,128]{2,1,0:T(8,128)} %get-tuple-element.208), custom_call_target="InvertDiagBlocksLowerTriangular" | custom-call | tf_op jit(solution)/shard_map/triangular_solve/custom-call.6 | solution.py:60
  1002.6 11.7 cholesky.762
  1030.3 12.5 cholesky.773
  1053.0 20.7 custom-call.109
  1107.6 11.7 cholesky.795
  1145.6 39.3 %custom-call.111 = f32[4,128,128]{1,2,0:T(8,128)S(1)} custom-call(f32[4,128,128]{2,1,0:T(8,128)S(1)} %get-tuple-element.210), custom_call_target="InvertDiagBlocksLowerTriangular" | custom-call | tf_op jit(solution)/shard_map/triangular_solve/custom-call.6 | solution.py:60
  1239.7 11.7 cholesky.806
  1263.9 11.7 cholesky.817
  1284.4 21.3 custom-call.113
  1338.7 11.7 cholesky.839
  1380.2 39.3 %custom-call.115 = f32[4,128,128]{1,2,0:T(8,128)S(1)} custom-call(f32[4,128,128]{2,1,0:T(8,128)S(1)} %get-tuple-element.212), custom_call_target="InvertDiagBlocksLowerTriangular" | custom-call | tf_op jit(solution)/shard_map/triangular_solve/custom-call.6 | solution.py:60
  1462.8 33.2 %collective-permute-done.32 = f32[512]{0:T(512)S(1)} collective-permute-done((f32[512]{0:T(512)S(1)}, f32[512]{0:T(512)S(1)}, u32[]{:S(2)}, u32[]{:S(2)}) %collective-permute-start.32) | collective-permute-done | bytes 2080 | tf_op jit(solution)/shard_map/ppermute | solution.py:33
  1507.6 11.7 cholesky.850
  1535.3 12.5 cholesky.861
  1558.0 20.7 custom-call.117
  1612.6 11.7 cholesky.883
  1652.1 39.3 %custom-call.119 = f32[4,128,128]{1,2,0:T(8,128)S(1)} custom-call(f32[4,128,128]{2,1,0:T(8,128)S(1)} %get-tuple-element.214), custom_call_target="InvertDiagBlocksLowerTriangular" | custom-call | tf_op jit(solution)/shard_map/triangular_solve/custom-call.6 | solution.py:60
  1744.1 11.7 cholesky.894
  1768.3 12.5 cholesky.905
  1788.7 19.9 custom-call.121
  1840.4 11.7 cholesky.927
  1856.4 13.9 while.74
  1870.3 41.1 %custom-call.123 = f32[4,128,128]{1,2,0:T(8,128)} custom-call(f32[4,128,128]{2,1,0:T(8,128)} %get-tuple-element.216), custom_call_target="InvertDiagBlocksLowerTriangular" | custom-call | tf_op jit(solution)/shard_map/triangular_solve/custom-call.6 | solution.py:60
  1995.2 11.7 cholesky.938
  2041.5 21.1 custom-call.125
  2128.7 39.3 %custom-call.135 = f32[4,128,128]{1,2,0:T(8,128)S(1)} custom-call(f32[4,128,128]{2,1,0:T(8,128)S(1)} %get-tuple-element.226), custom_call_target="InvertDiagBlocksLowerTriangular" | custom-call | tf_op jit(solution)/shard_map/triangular_solve/custom-call.9 | solution.py:64
  (1294 shorter events, 1466.2 us)
Async XLA Ops:
  9.4 12.0 all-to-all-start.2
  22.2 11.8 all-to-all-start.1
  35.1 16.3 all-to-all-start
  207.4 26.5 %all-to-all-start.3 = ((f32[4,1024,128]{1,2,0:T(8,128)}), f32[4,1024,128]{1,2,0:T(8,128)S(1)}, u32[]{:S(2)}, u32[]{:S(2)}) async-start(f32[4,1024,128]{1,2,0:T(8,128)} %broadcast_in_dim.108), calls=%async_computation.3 | async-start | bytes 4194304 | tf_op jit(solution)/shard_map/all_to_all | solution.py:9
  244.8 15.3 all-to-all-start.4
  434.6 24.5 %all-to-all-start.5 = ((f32[4,1024,128]{1,2,0:T(8,128)}), f32[4,1024,128]{1,2,0:T(8,128)S(1)}, u32[]{:S(2)}, u32[]{:S(2)}) async-start(f32[4,1024,128]{1,2,0:T(8,128)} %broadcast_in_dim.110), calls=%async_computation.5 | async-start | bytes 4194304 | tf_op jit(solution)/shard_map/all_to_all | solution.py:9
  469.1 15.4 all-to-all-start.6
  693.4 23.5 %all-to-all-start.7 = ((f32[4,1024,128]{1,2,0:T(8,128)}), f32[4,1024,128]{1,2,0:T(8,128)}, u32[]{:S(2)}, u32[]{:S(2)}) async-start(f32[4,1024,128]{1,2,0:T(8,128)} %broadcast_in_dim.112), calls=%async_computation.7 | async-start | bytes 4194304 | tf_op jit(solution)/shard_map/all_to_all | solution.py:9
  698.0 63.9 %all-gather.2.cloned.1.call-start = ((), (), s32[]{:S(2)}) async-start(), calls=%async_computation.9 | async-start | bytes 2621440 | tf_op jit(solution)/shard_map/all_gather | solution.py:38
  736.6 11.4 collective-permute-start.21
  871.5 81.3 %collective-permute-start.1 = (f32[512,512]{0,1:T(8,128)}, f32[512,512]{0,1:T(8,128)}, u32[]{:S(2)}, u32[]{:S(2)}) collective-permute-start(f32[512,512]{0,1:T(8,128)} %bitcast.1357), channel_id=1, source_target_pairs={{4,0},{8,4},{12,8},{16,12},{20,16},{24,20},{28,24},{32,28},{36,32}... | collective-permute-start | bytes 3145736 | tf_op jit(solution)/shard_map/ppermute | solution.py:33
  973.3 27.0 %collective-permute-start.2 = (f32[512,512]{0,1:T(8,128)S(1)}, f32[512,512]{0,1:T(8,128)S(1)}, u32[]{:S(2)}, u32[]{:S(2)}) collective-permute-start(f32[512,512]{0,1:T(8,128)S(1)} %fusion.182), channel_id=1, source_target_pairs={{4,0},{8,4},{12,8},{16,12},{20,16},{24,20},{28,24},{32,28},{36,32}... | collective-permute-start | bytes 3145736 | tf_op jit(solution)/shard_map/ppermute | solution.py:33
  976.1 24.3 %collective-permute-start.3 = (f32[512,512]{0,1:T(8,128)S(1)}, f32[512,512]{0,1:T(8,128)S(1)}, u32[]{:S(2)}, u32[]{:S(2)}) collective-permute-start(f32[512,512]{0,1:T(8,128)S(1)} %fusion.175), channel_id=1, source_target_pairs={{0,4},{4,8},{8,12},{12,16},{16,20},{20,24},{24,28},{28,32},{32,36}... | collective-permute-start | bytes 3145736 | tf_op jit(solution)/shard_map/ppermute | solution.py:33
  978.7 15.7 collective-permute-start.25
  980.6 17.2 collective-permute-start.24
  990.1 9.6 collective-permute-start.23
  997.8 123.4 %collective-permute-start.4 = (f32[512,512]{1,0:T(8,128)}, f32[512,512]{1,0:T(8,128)}, u32[]{:S(2)}, u32[]{:S(2)}) collective-permute-start(f32[512,512]{1,0:T(8,128)} %convolution_negate_fusion.3), channel_id=1, source_target_pairs={{0,4},{4,8},{8,12},{12,16},{16,20},{20,24},{24,28},{28,32},{32,36}... | collective-permute-start | bytes 3145736 | tf_op jit(solution)/shard_map/ppermute | solution.py:33
  1123.8 68.5 %collective-permute-start.5 = (f32[512,512]{1,0:T(8,128)}, f32[512,512]{1,0:T(8,128)}, u32[]{:S(2)}, u32[]{:S(2)}) collective-permute-start(f32[512,512]{1,0:T(8,128)} %bitcast.1354), channel_id=1, source_target_pairs={{8,0},{12,4},{16,8},{20,12},{24,16},{28,20},{32,24},{36,28},{40,32... | collective-permute-start | bytes 3145736 | tf_op jit(solution)/shard_map/ppermute | solution.py:33
  1206.8 32.3 %collective-permute-start.6 = (f32[512,512]{0,1:T(8,128)S(1)}, f32[512,512]{0,1:T(8,128)S(1)}, u32[]{:S(2)}, u32[]{:S(2)}) collective-permute-start(f32[512,512]{0,1:T(8,128)S(1)} %fusion.168), channel_id=1, source_target_pairs={{8,0},{12,4},{16,8},{20,12},{24,16},{28,20},{32,24},{36,28},{40,32... | collective-permute-start | bytes 3145736 | tf_op jit(solution)/shard_map/ppermute | solution.py:33
  1208.7 30.4 %collective-permute-start.7 = (f32[512,512]{0,1:T(8,128)S(1)}, f32[512,512]{0,1:T(8,128)S(1)}, u32[]{:S(2)}, u32[]{:S(2)}) collective-permute-start(f32[512,512]{0,1:T(8,128)S(1)} %fusion.161), channel_id=1, source_target_pairs={{0,8},{4,12},{8,16},{12,20},{16,24},{20,28},{24,32},{28,36},{32,40... | collective-permute-start | bytes 3145736 | tf_op jit(solution)/shard_map/ppermute | solution.py:33
  1213.7 18.0 collective-permute-start.28
  1217.8 17.9 collective-permute-start.29
  1223.5 15.6 collective-permute-start.27
  1231.7 7.4 collective-permute-start.26
  1235.7 116.7 %collective-permute-start.8 = (f32[512,512]{1,0:T(8,128)}, f32[512,512]{1,0:T(8,128)}, u32[]{:S(2)}, u32[]{:S(2)}) collective-permute-start(f32[512,512]{1,0:T(8,128)} %convolution_negate_fusion.2), channel_id=1, source_target_pairs={{0,8},{4,12},{8,16},{12,20},{16,24},{20,28},{24,32},{28,36},{32,40... | collective-permute-start | bytes 3145736 | tf_op jit(solution)/shard_map/ppermute | solution.py:33
  1354.9 72.1 %collective-permute-start.9 = (f32[512,512]{1,0:T(8,128)}, f32[512,512]{1,0:T(8,128)}, u32[]{:S(2)}, u32[]{:S(2)}) collective-permute-start(f32[512,512]{1,0:T(8,128)} %bitcast.1356), channel_id=1, source_target_pairs={{16,0},{20,4},{24,8},{28,12},{32,16},{36,20},{40,24},{44,28},{48,3... | collective-permute-start | bytes 3145736 | tf_op jit(solution)/shard_map/ppermute | solution.py:33
  1441.4 63.5 %collective-permute-start.10 = (f32[512,512]{0,1:T(8,128)S(1)}, f32[512,512]{0,1:T(8,128)S(1)}, u32[]{:S(2)}, u32[]{:S(2)}) collective-permute-start(f32[512,512]{0,1:T(8,128)S(1)} %fusion.154), channel_id=1, source_target_pairs={{16,0},{20,4},{24,8},{28,12},{32,16},{36,20},{40,24},{44,28},{48,3... | collective-permute-start | bytes 3145736 | tf_op jit(solution)/shard_map/ppermute | solution.py:33
  1443.5 62.1 %collective-permute-start.11 = (f32[512,512]{0,1:T(8,128)S(1)}, f32[512,512]{0,1:T(8,128)S(1)}, u32[]{:S(2)}, u32[]{:S(2)}) collective-permute-start(f32[512,512]{0,1:T(8,128)S(1)} %fusion.147), channel_id=1, source_target_pairs={{0,16},{4,20},{8,24},{12,28},{16,32},{20,36},{24,40},{28,44},{32,4... | collective-permute-start | bytes 3145736 | tf_op jit(solution)/shard_map/ppermute | solution.py:33
  1449.7 46.3 %collective-permute-start.32 = (f32[512]{0:T(512)S(1)}, f32[512]{0:T(512)S(1)}, u32[]{:S(2)}, u32[]{:S(2)}) collective-permute-start(f32[512]{0:T(512)S(1)} %bitcast.1439), channel_id=1, source_target_pairs={{16,0},{20,4},{24,8},{28,12},{32,16},{36,20},{40,24},{44,28},{48,3... | collective-permute-start | bytes 6152 | tf_op jit(solution)/shard_map/ppermute | solution.py:33
  1452.6 45.3 %collective-permute-start.33 = (f32[512]{0:T(512)S(1)}, f32[512]{0:T(512)S(1)}, u32[]{:S(2)}, u32[]{:S(2)}) collective-permute-start(f32[512]{0:T(512)S(1)} %bitcast.1443), channel_id=1, source_target_pairs={{0,16},{4,20},{8,24},{12,28},{16,32},{20,36},{24,40},{28,44},{32,4... | collective-permute-start | bytes 6152 | tf_op jit(solution)/shard_map/ppermute | solution.py:33
  1460.8 42.6 %collective-permute-start.31 = (f32[64,512]{1,0:T(8,128)S(1)}, f32[64,512]{1,0:T(8,128)S(1)}, u32[]{:S(2)}, u32[]{:S(2)}) collective-permute-start(f32[64,512]{1,0:T(8,128)S(1)} %fusion.144), channel_id=1, source_target_pairs={{0,16},{4,20},{8,24},{12,28},{16,32},{20,36},{24,40},{28,44},{32,4... | collective-permute-start | bytes 393224 | tf_op jit(solution)/shard_map/ppermute | solution.py:33
  1496.0 8.9 collective-permute-start.30
  1497.9 128.3 %collective-permute-start.12 = (f32[512,512]{1,0:T(8,128)}, f32[512,512]{1,0:T(8,128)}, u32[]{:S(2)}, u32[]{:S(2)}) collective-permute-start(f32[512,512]{1,0:T(8,128)} %convolution_negate_fusion.1), channel_id=1, source_target_pairs={{0,16},{4,20},{8,24},{12,28},{16,32},{20,36},{24,40},{28,44},{32,4... | collective-permute-start | bytes 3145736 | tf_op jit(solution)/shard_map/ppermute | solution.py:33
  1628.8 70.1 %collective-permute-start.13 = (f32[512,512]{1,0:T(8,128)}, f32[512,512]{1,0:T(8,128)}, u32[]{:S(2)}, u32[]{:S(2)}) collective-permute-start(f32[512,512]{1,0:T(8,128)} %bitcast.1355), channel_id=1, source_target_pairs={{32,0},{36,4},{40,8},{44,12},{48,16},{52,20},{56,24},{60,28},{64,3... | collective-permute-start | bytes 3145736 | tf_op jit(solution)/shard_map/ppermute | solution.py:33
  1713.3 30.2 %collective-permute-start.14 = (f32[512,512]{0,1:T(8,128)S(1)}, f32[512,512]{0,1:T(8,128)S(1)}, u32[]{:S(2)}, u32[]{:S(2)}) collective-permute-start(f32[512,512]{0,1:T(8,128)S(1)} %fusion.140), channel_id=1, source_target_pairs={{32,0},{36,4},{40,8},{44,12},{48,16},{52,20},{56,24},{60,28},{64,3... | collective-permute-start | bytes 3145736 | tf_op jit(solution)/shard_map/ppermute | solution.py:33
  1714.7 28.9 %collective-permute-start.15 = (f32[512,512]{0,1:T(8,128)S(1)}, f32[512,512]{0,1:T(8,128)S(1)}, u32[]{:S(2)}, u32[]{:S(2)}) collective-permute-start(f32[512,512]{0,1:T(8,128)S(1)} %fusion.133), channel_id=1, source_target_pairs={{0,32},{4,36},{8,40},{12,44},{16,48},{20,52},{24,56},{28,60},{32,6... | collective-permute-start | bytes 3145736 | tf_op jit(solution)/shard_map/ppermute | solution.py:33
  1717.1 19.5 collective-permute-start.36
  1721.6 20.5 collective-permute-start.37
  1726.7 16.8 collective-permute-start.35
  1742.1 177.9 %collective-permute-start.16 = (f32[512,512]{1,0:T(8,128)}, f32[512,512]{1,0:T(8,128)}, u32[]{:S(2)}, u32[]{:S(2)}) collective-permute-start(f32[512,512]{1,0:T(8,128)} %convolution_negate_fusion), channel_id=1, source_target_pairs={{0,32},{4,36},{8,40},{12,44},{16,48},{20,52},{24,56},{28,60},{32,6... | collective-permute-start | bytes 3145736 | tf_op jit(solution)/shard_map/ppermute | solution.py:33
  1922.5 24.7 %collective-permute-start.17 = (f32[512,512]{1,0:T(8,128)}, f32[512,512]{1,0:T(8,128)}, u32[]{:S(2)}, u32[]{:S(2)}) collective-permute-start(f32[512,512]{1,0:T(8,128)} %bitcast.1358), channel_id=1, source_target_pairs={{64,0},{68,4},{72,8},{76,12},{80,16},{84,20},{88,24},{92,28},{96,3... | collective-permute-start | bytes 3145736 | tf_op jit(solution)/shard_map/ppermute | solution.py:33
  1960.9 33.8 %collective-permute-start.18 = (f32[512,512]{0,1:T(8,128)S(1)}, f32[512,512]{0,1:T(8,128)S(1)}, u32[]{:S(2)}, u32[]{:S(2)}) collective-permute-start(f32[512,512]{0,1:T(8,128)S(1)} %fusion.126), channel_id=1, source_target_pairs={{64,0},{68,4},{72,8},{76,12},{80,16},{84,20},{88,24},{92,28},{96,3... | collective-permute-start | bytes 3145736 | tf_op jit(solution)/shard_map/ppermute | solution.py:33
  1967.0 27.7 %collective-permute-start.19 = (f32[512,512]{0,1:T(8,128)S(1)}, f32[512,512]{0,1:T(8,128)S(1)}, u32[]{:S(2)}, u32[]{:S(2)}) collective-permute-start(f32[512,512]{0,1:T(8,128)S(1)} %fusion.120), channel_id=1, source_target_pairs={{0,64},{4,68},{8,72},{12,76},{16,80},{20,84},{24,88},{28,92},{32,9... | collective-permute-start | bytes 3145736 | tf_op jit(solution)/shard_map/ppermute | solution.py:33
  1969.0 17.2 collective-permute-start.40
  1975.1 18.2 collective-permute-start.41
  1978.1 16.6 collective-permute-start.39
  1986.2 8.5 collective-permute-start.38
  2174.7 19.2 all-to-all-start.8
  (150 other events, 3036.4 us)
Sparse Core Ops, SparseCore 0:
  728.0 33.8 all-gather.1
where the time goes:
time: 2290 us; the launch traced here: 2270 us
  other arithmetic  1300 us (57%)
  local copies, waits for them, and re-layouts  311 us (14%)
  matrix products  305 us (13%)
  starting transfers between devices  182 us (8%)
  waiting for transfers between devices  145 us (6%)
  between operations  27.8 us (1%)
    another operation x108, other arithmetic, blocked_cholesky(): return jnp.linalg.cholesky(matrix)  454 us
    another operation x46, other arithmetic, blocked_cholesky(): lax.linalg.triangular_solve(top_factor, matrix[half:, :half], left_side=F...  385 us
    another operation x22, other arithmetic, lower_solve(): lax.linalg.triangular_solve(factor, right_side, left_side=True, lower=True)  283 us
    ppermute x43, starting transfers between devices, shifted(): return lax.ppermute(block, axis, route)  139 us
    another operation x120, matrix products, lower_solve(): lax.linalg.triangular_solve(factor, right_side, left_side=True, lower=True)  119 us
    dot_general x73, matrix products, cross_product(): lax.dot_general(first_operand, second_operand, (((0,), (0,)), ((), ())),...  90.2 us
    another operation x6, other arithmetic, upper_solve(): lax.linalg.triangular_solve(factor, right_side, left_side=True, lower=Tru...  88 us
    another operation x84, local copies, waits for them, and re-layouts, lower_solve(): lax.linalg.triangular_solve(factor, right_side, left_side=True, lower=True)  87.9 us
  transfers between devices with their start and end apart: 53, of which 25 were waited for; matrix products, arithmetic and copies ran while one was open for 40% of the time, Pallas kernels for 0%

commit v1 on v0

v1 whole, which is shorter than its diff:
```python
import jax
import jax.numpy as jnp
from jax import lax
from jax.experimental import pallas as pl
from jax.experimental.pallas import tpu as pltpu
from jax.sharding import PartitionSpec as P

AXES = ("tm", "col")
F32 = jnp.float32
TILE = 128
HALF = 256
NODES = 512


def mm(a, b):
    return lax.dot_general(
        a, b, (((1,), (0,)), ((), ())), precision=lax.Precision.HIGHEST, preferred_element_type=F32
    )


def mtm(a, b):
    return lax.dot_general(
        a, b, (((0,), (0,)), ((), ())), precision=lax.Precision.HIGHEST, preferred_element_type=F32
    )


def lane_splat(x, j):
    return jnp.broadcast_to(x[:, j : j + 1], (8, TILE))


def row_splat(x, i):
    return jnp.broadcast_to(x[i : i + 1, :], (8, TILE))


def factor_tile(tile, inv_ref, size):
    groups = size // 8
    a = [tile[8 * g : 8 * g + 8, :] for g in range(groups)]
    row = lax.broadcasted_iota(jnp.int32, (8, TILE), 0)
    lane = lax.broadcasted_iota(jnp.int32, (8, TILE), 1)
    inv = [jnp.where(lane == row + 8 * g, 1.0, 0.0).astype(F32) for g in range(groups)]
    pivots = jnp.ones((8, TILE), F32)
    for g0 in range(groups):
        top, side = a[g0], inv[g0]
        cols = [lane_splat(top, 8 * g0 + i) for i in range(8)]
        rows = [row_splat(top, i) for i in range(8)]
        side_rows = [row_splat(side, i) for i in range(8)]
        p = [[row_splat(cols[c], i) for c in range(i + 1)] for i in range(8)]
        low = [[None] * 8 for _ in range(8)]
        scale = []
        for c in range(8):
            r = lax.rsqrt(p[c][c])
            scale.append(r)
            pivots = jnp.where((row == c) & (lane == g0), p[c][c], pivots)
            for i in range(c + 1, 8):
                low[i][c] = p[i][c] * r
            for i in range(c + 1, 8):
                for k in range(c + 1, i + 1):
                    p[i][k] = p[i][k] - low[i][c] * low[k][c]
        u, v = [], []
        for i in range(8):
            x, y = rows[i], side_rows[i]
            for c in range(i):
                x = x - low[i][c] * u[c]
                y = y - low[i][c] * v[c]
            u.append(x * scale[i])
            v.append(y * scale[i])
        for g in range(g0 + 1, groups):
            e = []
            for i in range(8):
                x = lane_splat(a[g], 8 * g0 + i)
                for c in range(i):
                    x = x - low[i][c] * e[c]
                e.append(x * scale[i])
            for i in range(8):
                a[g] = a[g] - e[i] * u[i]
                inv[g] = inv[g] - e[i] * v[i]
        done = side
        for i in range(8):
            done = jnp.where(row == i, v[i], done)
        inv[g0] = done
    for g in range(groups):
        inv_ref[8 * g : 8 * g + 8, :] = inv[g]
    return pivots


def factor_body(s, inv, ma, mb, u):
    def body(k, logs):
        o = pl.multiple_of(k * TILE, TILE)
        pivots = factor_tile(s[pl.ds(o, TILE), pl.ds(o, TILE)], inv, TILE)
        for half, m in ((0, ma), (1, mb)):
            b0, b1, b2 = half * HALF, half * HALF + TILE, half * HALF + HALF

            @pl.when(k == 2 * half)
            def _():
                first = inv[...]
                panel = mm(first, s[b0:b1, b1:b2])
                s[b1:b2, b1:b2] = s[b1:b2, b1:b2] - mtm(panel, panel)
                m[0:TILE, 0:TILE] = first
                m[0:TILE, TILE:HALF] = jnp.zeros((TILE, TILE), F32)
                m[TILE:HALF, 0:TILE] = mtm(panel, first)

            @pl.when(k == 2 * half + 1)
            def _():
                second = inv[...]
                m[TILE:HALF, TILE:HALF] = second
                m[TILE:HALF, 0:TILE] = -mm(second, m[TILE:HALF, 0:TILE])
                if half == 0:
                    panel = mm(ma[...], s[0:HALF, HALF:NODES])
                    u[...] = panel
                    s[HALF:NODES, HALF:NODES] = s[HALF:NODES, HALF:NODES] - mtm(panel, panel)

        return logs + jnp.log(pivots)

    return lax.fori_loop(0, 4, body, jnp.zeros((8, TILE), F32))


def factor_first_kernel(q, ma, mb, u, logs, s, inv):
    s[...] = q[...]
    logs[...] = factor_body(s, inv, ma, mb, u)


def factor_next_kernel(q, from_left, from_right, ma, mb, u, logs, q_new, s, inv):
    value = q[...] - from_left[...] - from_right[...]
    s[...] = value
    q_new[...] = value
    logs[...] = factor_body(s, inv, ma, mb, u)


def solve_into(ma, mb, u, top, bottom, out):
    first = mm(ma[...], top)
    out[0:HALF, :] = first
    out[HALF:NODES, :] = mm(mb[...], bottom - mtm(u[...], first))


def packed_products(w, ws, out, corner):
    whole, edge = w[...], ws[...]
    out[0:HALF, :] = mtm(w[:, 0:HALF], whole)
    out[HALF:NODES, HALF:NODES] = mtm(w[:, HALF:NODES], w[:, HALF:NODES])
    crossed = mtm(whole, edge)
    out[HALF:NODES, 0:TILE] = crossed[0:HALF]
    out[HALF:NODES, TILE:HALF] = crossed[HALF:NODES]
    out[TILE:HALF, 0:TILE] = corner


def corner_sums(q, ws, logs):
    row = lax.broadcasted_iota(jnp.int32, (TILE, TILE), 0)
    lane = lax.broadcasted_iota(jnp.int32, (TILE, TILE), 1)
    log_sum = jnp.sum(logs[...])
    sums = mtm(ws[...], ws[...]) - q[TILE:HALF, 0:TILE]
    return sums + jnp.where((row == 65) & (lane == 65), log_sum, 0.0)


def eliminate_kernel(ma, mb, u, logs, q, low, high, wl, wh, ws, left, right):
    solve_into(ma, mb, u, q[HALF:NODES, 0:TILE], q[HALF:NODES, TILE:HALF], ws)
    solve_into(ma, mb, u, low[0:HALF, :], low[HALF:NODES, :], wl)
    packed_products(wl, ws, left, jnp.zeros((TILE, TILE), F32))
    solve_into(ma, mb, u, high[0:HALF, :], high[HALF:NODES, :], wh)
    packed_products(wh, ws, right, corner_sums(q, ws, logs))


def couple_kernel(odd, wl, wh, out):
    @pl.when(odd[0] == 0)
    def _():
        out[...] = -mtm(wh[...], wl[...])

    @pl.when(odd[0] != 0)
    def _():
        out[...] = -mtm(wl[...], wh[...])


def back_solve(ma, mb, u, z_top, z_bottom):
    x_bottom = jnp.sum(mb[...] * z_bottom, axis=0, keepdims=True)
    z_top = z_top - jnp.sum(u[...] * x_bottom, axis=1, keepdims=True)
    x_top = jnp.sum(ma[...] * z_top, axis=0, keepdims=True)
    return x_top, x_bottom


def root_kernel(total, ma, mb, u, logs, q, tip, fixed, out, ws, inv):
    solve_into(ma, mb, u, q[HALF:NODES, 0:TILE], q[HALF:NODES, TILE:HALF], ws)
    sums = corner_sums(q, ws, logs)
    row = lax.broadcasted_iota(jnp.int32, (TILE, TILE), 0)
    lane = lax.broadcasted_iota(jnp.int32, (TILE, TILE), 1)
    inv[...] = tip[...] - jnp.where((row < 64) & (lane < 64), sums, 0.0)
    pivots = factor_tile(inv[0:64, :], inv, 64)
    m = inv[0:64, :]
    rest = fixed[...] - sums[64:65, :]
    z = jnp.sum(m * rest, axis=1, keepdims=True)
    x_fixed = jnp.sum(m * z, axis=0, keepdims=True)
    lane1 = lax.broadcasted_iota(jnp.int32, (1, TILE), 1)
    x_fixed = jnp.where(lane1 < 64, x_fixed, 0.0)
    log_total = jnp.sum(jnp.where((row == 65) & (lane == 65), sums, 0.0)) + jnp.sum(jnp.log(pivots))
    weights = jnp.where(lane1 == 64, 1.0, -x_fixed)
    z = jnp.sum(ws[...] * weights, axis=1, keepdims=True)
    x_top, x_bottom = back_solve(ma, mb, u, z[0:HALF], z[HALF:NODES])
    out[:, 0:HALF] = x_top
    out[:, HALF:NODES] = x_bottom
    out[:, NODES : NODES + TILE] = jnp.where(lane1 == 64, log_total / total, x_fixed)


def back_kernel(leaving, from_left, from_right, own, ma, mb, u, wl, wh, ws, out):
    lane1 = lax.broadcasted_iota(jnp.int32, (1, TILE), 1)
    extra = from_right[:, NODES : NODES + TILE]
    weights = jnp.where(lane1 == 64, 1.0, jnp.where(lane1 < 64, -extra, 0.0))
    z = (
        jnp.sum(ws[...] * weights, axis=1, keepdims=True)
        - jnp.sum(wl[...] * from_left[:, 0:NODES], axis=1, keepdims=True)
        - jnp.sum(wh[...] * from_right[:, 0:NODES], axis=1, keepdims=True)
    )
    x_top, x_bottom = back_solve(ma, mb, u, z[0:HALF], z[HALF:NODES])
    mine = leaving[0] != 0
    out[:, 0:HALF] = jnp.where(mine, x_top, own[:, 0:HALF])
    out[:, HALF:NODES] = jnp.where(mine, x_bottom, own[:, HALF:NODES])
    out[:, NODES : NODES + TILE] = jnp.where(mine, extra, own[:, NODES : NODES + TILE])


def shape(*dims):
    return jax.ShapeDtypeStruct(dims, F32)


def call(kernel, ins, outs, scratch=(), scalars=0, flops=0):
    smem = pl.BlockSpec(memory_space=pltpu.SMEM)
    vmem = pl.BlockSpec(memory_space=pltpu.VMEM)
    moved = 4 * sum(a.size for a in ins) + 4 * sum(o.size for o in outs)
    return pl.pallas_call(
        kernel,
        out_shape=tuple(outs),
        in_specs=[smem] * scalars + [vmem] * (len(ins) - scalars),
        out_specs=tuple([vmem] * len(outs)),
        scratch_shapes=[pltpu.VMEM(dims, F32) for dims in scratch],
        cost_estimate=pl.CostEstimate(flops=flops, bytes_accessed=moved, transcendentals=0),
    )(*ins)


FACTORS = (shape(HALF, HALF), shape(HALF, HALF), shape(HALF, HALF), shape(8, TILE))
WORK = ((NODES, NODES), (TILE, TILE))


def moved(x, pairs):
    return lax.ppermute(x, AXES, pairs)


def per_device(blocks, upper, arrow, tip, rhs, rhs_fixed):
    node_count = blocks.shape[1]
    effects = tip.shape[0]
    cols = lax.axis_size("col")
    count = lax.axis_size("tm") * cols
    col = lax.axis_index("col")
    t = lax.axis_index("tm") * cols + col
    take = lambda x: lax.all_to_all(x, "col", split_axis=0, concat_axis=2, tiled=True)[0]
    diagonal = take(blocks)
    coupling = take(upper)
    side = take(arrow)
    own_rhs = lax.dynamic_slice_in_dim(rhs, col, 1, 0)
    ma, mb, u, logs = call(factor_first_kernel, (diagonal,), FACTORS, WORK, flops=4 * 10**9)
    high = moved(coupling, [(i + 1, i) for i in range(0, count, 2)])
    low = coupling.T * (t > 0).astype(F32)
    edge = jnp.concatenate(
        [side, own_rhs, jnp.zeros((TILE - effects - 1, node_count), F32)], axis=0
    ).T
    packed = jnp.concatenate([edge[0:HALF], edge[HALF:NODES]], axis=1)
    q = diagonal.at[HALF:NODES, 0:HALF].set(packed)
    q = q.at[TILE:HALF, 0:TILE].set(0.0)
    kept = []
    level = 0
    while (1 << level) < count:
        s = 1 << level
        leaving = [(2 * k + 1) * s - 1 for k in range(count // (2 * s))]
        products = (shape(NODES, NODES), shape(NODES, NODES), shape(NODES, TILE)) + (
            shape(NODES, NODES),
        ) * 2
        wl, wh, ws, left, right = call(
            eliminate_kernel, (ma, mb, u, logs, q, low, high), products, flops=6 * 10**9
        )
        kept.append((ma, mb, u, wl, wh, ws))
        got_left = moved(right, [(i, i + s) for i in leaving])
        got_right = moved(left, [(i, i - s) for i in leaving if i >= s])
        if 2 * s < count:
            odd = (((t + 1) // (2 * s)) % 2).astype(jnp.int32).reshape(1)
            (new,) = call(couple_kernel, (odd, wl, wh), (shape(NODES, NODES),), scalars=1, flops=10**9)
            new, got_left, got_right = lax.optimization_barrier((new, got_left, got_right))
            low = moved(new, [(i, i + s) for i in leaving[0::2]])
            high = moved(new, [(i, i - s) for i in leaving[1::2]])
        ma, mb, u, logs, q = call(
            factor_next_kernel,
            (q, got_left, got_right),
            FACTORS + (shape(NODES, NODES),),
            WORK,
            flops=4 * 10**9,
        )
        level += 1
    whole_tip = jnp.eye(TILE, dtype=F32).at[0:effects, 0:effects].set(tip)
    whole_fixed = jnp.pad(rhs_fixed, (0, TILE - effects)).reshape(1, TILE)
    total = float(count * node_count + effects)
    (state,) = call(
        lambda *refs: root_kernel(total, *refs),
        (ma, mb, u, logs, q, whole_tip, whole_fixed),
        (shape(1, NODES + TILE),),
        ((NODES, TILE), (TILE, TILE)),
        flops=10**8,
    )
    for level in reversed(range(len(kept))):
        s = 1 << level
        leaving = [(2 * k + 1) * s - 1 for k in range(count // (2 * s))]
        from_left = moved(state, [(i - s, i) for i in leaving if i >= s])
        from_right = moved(state, [(i + s, i) for i in leaving])
        mine = ((t + 1) % (2 * s) == s).astype(jnp.int32).reshape(1)
        (state,) = call(
            back_kernel,
            (mine, from_left, from_right, state) + kept[level],
            (shape(1, NODES + TILE),),
            scalars=1,
            flops=10**7,
        )
    solution = lax.all_to_all(state[:, 0:NODES], "col", split_axis=1, concat_axis=0, tiled=True)
    return (solution, state[0, NODES : NODES + effects], state[0, NODES + 64])


def solution(mesh):
    placed = (
        P("tm", None, "col"),
        P("tm", None, "col"),
        P("tm", None, "col"),
        P(),
        P("tm", None),
        P(),
    )
    return jax.shard_map(
        per_device,
        mesh=mesh,
        in_specs=placed,
        out_specs=(P("tm", "col"), P(), P()),
        check_vma=False,
    )
```

time: 2290 us -> 622 us (0.27)
  other arithmetic: 1300 us -> 1 us
  Pallas kernels: 0 us -> 310 us
  matrix products: 305 us -> 0 us
  local copies, waits for them, and re-layouts: 311 us -> 23.7 us
  waiting for transfers between devices: 145 us -> 26.9 us
  starting transfers between devices: 182 us -> 222 us
  blocking collectives: 0 us -> 28.7 us
  between operations: 27.8 us -> 1.8 us
    another operation x190 -> x0, other arithmetic: 1220 us -> none  [the longest x108 454 us: blocked_cholesky(): return jnp.linalg.cholesky(matrix)]
    pallas_call x0 -> x29, Pallas kernels: none -> 310 us  [call(): pl.pallas_call(kernel, out_shape=tuple(outs), in_specs=[smem] * scalars +...]
    another operation x194 -> x0, matrix products: 184 us -> none  [the longest x120 119 us: lower_solve(): lax.linalg.triangular_solve(factor, right_side, left_side=True, lower=True)]
    another operation x191 -> x0, local copies, waits for them, and re-layouts: 166 us -> none  [the longest x84 87.9 us: lower_solve(): lax.linalg.triangular_solve(factor, right_side, left_side=True, lower=True)]
    dot_general x110 -> x0, matrix products: 121 us -> none  [the longest x73 90.2 us: cross_product(): lax.dot_general(first_operand, second_operand, (((0,), (0,)), ((), ())),...]
    ppermute x43 -> x41, starting transfers between devices: 139 us -> 215 us  [moved(): return lax.ppermute(x, AXES, pairs)]
    ppermute x43 -> x41, waiting for transfers between devices: 77.9 us -> 15 us  [moved(): return lax.ppermute(x, AXES, pairs)]
    gather x10 -> x0, local copies, waits for them, and re-layouts: 55.8 us -> none  [log_pivots(): return 2.0 * jnp.sum(jnp.log(jnp.diagonal(factor)))]
  transfers between devices with their start and end apart: 53 -> 43, of which waited for: 25 -> 4; matrix products, arithmetic and copies ran while one was open for 40% -> 2% of each run, Pallas kernels for 0% -> 29%
where the time goes in v1:
time: 622 us; the launch traced here: 614 us
  Pallas kernels  310 us (50%)
  starting transfers between devices  222 us (36%)
  blocking collectives  28.7 us (5%)
  waiting for transfers between devices  26.9 us (4%)
  local copies, waits for them, and re-layouts  23.7 us (4%)
    pallas_call x29, Pallas kernels, call(): pl.pallas_call(kernel, out_shape=tuple(outs), in_specs=[smem] * scalars +...  310 us
    ppermute x41, starting transfers between devices, moved(): return lax.ppermute(x, AXES, pairs)  215 us
    all_to_all x2, blocking collectives, per_device(): lax.all_to_all(x, 'col', split_axis=0, concat_axis=2, tiled=True)[0]  28.7 us
    ppermute x41, waiting for transfers between devices, moved(): return lax.ppermute(x, AXES, pairs)  15 us
    unnamed x82, local copies, waits for them, and re-layouts  14.9 us
  transfers between devices with their start and end apart: 43, of which 4 were waited for; matrix products, arithmetic and copies ran while one was open for 2% of the time, Pallas kernels for 29%

profile of v1, /device:TPU:6, one launch (start us, length us, event | category | flops | bytes accessed | tf_op | source)
XLA Modules:
  0.0 614.3 jit_solution(15857884862759268252)
XLA Ops:
  0.6 11.3 %all_to_all.61 = f32[4,64,128]{2,1,0:T(8,128)S(1)} all-to-all(f32[4,64,128]{2,1,0:T(8,128)} %param.14), channel_id=1, replica_groups=mesh['tm'=32,'col'=4] {'col'}, dimensions={0} | all-to-all | bytes 262144 | tf_op jit(solution)/shard_map/all_to_all | solution.py:249
  11.9 17.4 %all_to_all.62 = f32[4,512,128]{2,1,0:T(8,128)S(1)} all-to-all(f32[4,512,128]{2,1,0:T(8,128)} %param.13), channel_id=1, replica_groups=mesh['tm'=32,'col'=4] {'col'}, dimensions={0} | all-to-all | bytes 2097152 | tf_op jit(solution)/shard_map/all_to_all | solution.py:249
  29.4 3.5 all-to-all-start
  36.5 9.2 %all-to-all-done = f32[4,512,128]{2,1,0:T(8,128)S(1)} async-done(((f32[4,512,128]{2,1,0:T(8,128)}), f32[4,512,128]{2,1,0:T(8,128)S(1)}, u32[]{:S(2)}, u32[]{:S(2)}) %all-to-all-start) | async-done | bytes 1048608 | tf_op jit(solution)/shard_map/all_to_all | solution.py:249
  47.5 1.4 copy.18.low
  48.9 20.7 %shard_map.85 = (f32[256,256]{1,0:T(8,128)}, f32[256,256]{1,0:T(8,128)}, f32[256,256]{1,0:T(8,128)}, f32[8,128]{1,0:T(8,128)}) custom-call(f32[512,512]{1,0:T(8,128)} %bitcast.54), custom_call_target="tpu_custom_call" | custom-call | flops 4000000000 | bytes 1839104 | tf_op jit(solution)/shard_map/pallas_call | solution.py:224
  71.0 12.0 %shard_map.86 = (f32[512,512]{1,0:T(8,128)}, f32[512,512]{1,0:T(8,128)}, f32[512,128]{1,0:T(8,128)}, f32[512,512]{1,0:T(8,128)}, f32[512,512]{1,0:T(8,128)}) custom-call(f32[256,256]{1,0:T(8,128)} %get-tuple-element.131.ma, f32[256,256]{1,0:T(8,128)} %get-tuple-element.132.mb, f32[256,256]{1,0:T(8,128)} %get-tuple-element.133.u, ...), custom_call_target="tpu_custom_call" | custom-call | flops 6000000000 | bytes 8392704 | tf_op jit(solution)/shard_map/pallas_call | solution.py:224
  83.0 11.8 %collective-permute-start.1 = (f32[512,512]{1,0:T(8,128)}, f32[512,512]{1,0:T(8,128)S(1)}, u32[]{:S(2)}, u32[]{:S(2)}) collective-permute-start(f32[512,512]{1,0:T(8,128)} %get-tuple-element.137), channel_id=1, source_target_pairs={{0,1},{2,3},{4,5},{6,7},{8,9},{10,11},{12,13},{14,15},{16,17},{18,... | collective-permute-start | bytes 3145736 | tf_op jit(solution)/shard_map/ppermute | solution.py:239
  94.8 10.2 %collective-permute-start.2 = (f32[512,512]{1,0:T(8,128)}, f32[512,512]{1,0:T(8,128)S(1)}, u32[]{:S(2)}, u32[]{:S(2)}) collective-permute-start(f32[512,512]{1,0:T(8,128)} %get-tuple-element.138), channel_id=1, source_target_pairs={{2,1},{4,3},{6,5},{8,7},{10,9},{12,11},{14,13},{16,15},{18,17},{20... | collective-permute-start | bytes 3145736 | tf_op jit(solution)/shard_map/ppermute | solution.py:239
  105.0 4.5 shard_map.87
  109.6 8.4 %collective-permute-done.1.from_left = f32[512,512]{1,0:T(8,128)S(1)} collective-permute-done((f32[512,512]{1,0:T(8,128)}, f32[512,512]{1,0:T(8,128)S(1)}, u32[]{:S(2)}, u32[]{:S(2)}) %collective-permute-start.1) | collective-permute-done | bytes 1048608 | tf_op jit(solution)/shard_map/ppermute | solution.py:239
  118.0 15.9 %collective-permute-start.3 = (f32[512,512]{1,0:T(8,128)}, f32[512,512]{1,0:T(8,128)S(1)}, u32[]{:S(2)}, u32[]{:S(2)}) collective-permute-start(f32[512,512]{1,0:T(8,128)} %shard_map.87), channel_id=1, source_target_pairs={{0,1},{4,5},{8,9},{12,13},{16,17},{20,21},{24,25},{28,29},{32,33},... | collective-permute-start | bytes 3145736 | tf_op jit(solution)/shard_map/ppermute | solution.py:239
  133.9 1.7 collective-permute-start.4
  135.6 21.8 %shard_map.88 = (f32[256,256]{1,0:T(8,128)}, f32[256,256]{1,0:T(8,128)}, f32[256,256]{1,0:T(8,128)}, f32[8,128]{1,0:T(8,128)}, f32[512,512]{1,0:T(8,128)}) custom-call(f32[512,512]{1,0:T(8,128)} %broadcast_dynamic-update-slice_fusion.q, f32[512,512]{1,0:T(8,128)} %copy-done.18, f32[512,512]{1,0:T(8,128)} %copy-done.19), custom_call_target="tpu_custom_call" | custom-call | flops 4000000000 | bytes 4984832 | tf_op jit(solution)/shard_map/pallas_call | solution.py:224
  158.4 12.0 %shard_map.89 = (f32[512,512]{1,0:T(8,128)}, f32[512,512]{1,0:T(8,128)}, f32[512,128]{1,0:T(8,128)}, f32[512,512]{1,0:T(8,128)}, f32[512,512]{1,0:T(8,128)}) custom-call(f32[256,256]{1,0:T(8,128)} %get-tuple-element.142.ma, f32[256,256]{1,0:T(8,128)} %get-tuple-element.143.mb, f32[256,256]{1,0:T(8,128)} %get-tuple-element.144.u, ...), custom_call_target="tpu_custom_call" | custom-call | flops 6000000000 | bytes 8392704 | tf_op jit(solution)/shard_map/pallas_call | solution.py:224
  171.8 4.6 shard_map.90
  177.2 1.7 collective-permute-start.8
  178.9 21.9 %shard_map.91 = (f32[256,256]{1,0:T(8,128)}, f32[256,256]{1,0:T(8,128)}, f32[256,256]{1,0:T(8,128)}, f32[8,128]{1,0:T(8,128)}, f32[512,512]{1,0:T(8,128)}) custom-call(f32[512,512]{1,0:T(8,128)} %get-tuple-element.141.q, f32[512,512]{1,0:T(8,128)} %copy-done.25, f32[512,512]{1,0:T(8,128)} %copy-done.29), custom_call_target="tpu_custom_call" | custom-call | flops 4000000000 | bytes 4984832 | tf_op jit(solution)/shard_map/pallas_call | solution.py:224
  201.8 12.0 %shard_map.92 = (f32[512,512]{1,0:T(8,128)}, f32[512,512]{1,0:T(8,128)}, f32[512,128]{1,0:T(8,128)}, f32[512,512]{1,0:T(8,128)}, f32[512,512]{1,0:T(8,128)}) custom-call(f32[256,256]{1,0:T(8,128)} %get-tuple-element.154.ma, f32[256,256]{1,0:T(8,128)} %get-tuple-element.155.mb, f32[256,256]{1,0:T(8,128)} %get-tuple-element.156.u, ...), custom_call_target="tpu_custom_call" | custom-call | flops 6000000000 | bytes 8392704 | tf_op jit(solution)/shard_map/pallas_call | solution.py:224
  215.3 4.6 shard_map.93
  220.6 1.6 collective-permute-start.12
  222.3 21.6 %shard_map.94 = (f32[256,256]{1,0:T(8,128)}, f32[256,256]{1,0:T(8,128)}, f32[256,256]{1,0:T(8,128)}, f32[8,128]{1,0:T(8,128)}, f32[512,512]{1,0:T(8,128)}) custom-call(f32[512,512]{1,0:T(8,128)} %get-tuple-element.153.q, f32[512,512]{1,0:T(8,128)} %copy-done.21, f32[512,512]{1,0:T(8,128)} %copy-done.26), custom_call_target="tpu_custom_call" | custom-call | flops 4000000000 | bytes 4984832 | tf_op jit(solution)/shard_map/pallas_call | solution.py:224
  244.9 11.9 %shard_map.95 = (f32[512,512]{1,0:T(8,128)}, f32[512,512]{1,0:T(8,128)}, f32[512,128]{1,0:T(8,128)}, f32[512,512]{1,0:T(8,128)}, f32[512,512]{1,0:T(8,128)}) custom-call(f32[256,256]{1,0:T(8,128)} %get-tuple-element.166.ma, f32[256,256]{1,0:T(8,128)} %get-tuple-element.167.mb, f32[256,256]{1,0:T(8,128)} %get-tuple-element.168.u, ...), custom_call_target="tpu_custom_call" | custom-call | flops 6000000000 | bytes 8392704 | tf_op jit(solution)/shard_map/pallas_call | solution.py:224
  258.3 4.6 shard_map.96
  263.7 1.6 collective-permute-start.16
  265.3 21.9 %shard_map.97 = (f32[256,256]{1,0:T(8,128)}, f32[256,256]{1,0:T(8,128)}, f32[256,256]{1,0:T(8,128)}, f32[8,128]{1,0:T(8,128)}, f32[512,512]{1,0:T(8,128)}) custom-call(f32[512,512]{1,0:T(8,128)} %get-tuple-element.165.q, f32[512,512]{1,0:T(8,128)} %copy-done.23, f32[512,512]{1,0:T(8,128)} %copy-done.28), custom_call_target="tpu_custom_call" | custom-call | flops 4000000000 | bytes 4984832 | tf_op jit(solution)/shard_map/pallas_call | solution.py:224
  288.2 12.0 %shard_map.98 = (f32[512,512]{1,0:T(8,128)}, f32[512,512]{1,0:T(8,128)}, f32[512,128]{1,0:T(8,128)}, f32[512,512]{1,0:T(8,128)}, f32[512,512]{1,0:T(8,128)}) custom-call(f32[256,256]{1,0:T(8,128)} %get-tuple-element.178.ma, f32[256,256]{1,0:T(8,128)} %get-tuple-element.179.mb, f32[256,256]{1,0:T(8,128)} %get-tuple-element.180.u, ...), custom_call_target="tpu_custom_call" | custom-call | flops 6000000000 | bytes 8392704 | tf_op jit(solution)/shard_map/pallas_call | solution.py:224
  301.6 4.5 shard_map.99
  306.9 1.7 collective-permute-start.20
  308.6 21.6 %shard_map.100 = (f32[256,256]{1,0:T(8,128)}, f32[256,256]{1,0:T(8,128)}, f32[256,256]{1,0:T(8,128)}, f32[8,128]{1,0:T(8,128)}, f32[512,512]{1,0:T(8,128)}) custom-call(f32[512,512]{1,0:T(8,128)} %get-tuple-element.177.q, f32[512,512]{1,0:T(8,128)} %copy-done.22, f32[512,512]{1,0:T(8,128)} %copy-done.27), custom_call_target="tpu_custom_call" | custom-call | flops 4000000000 | bytes 4984832 | tf_op jit(solution)/shard_map/pallas_call | solution.py:224
  331.3 12.0 %shard_map.101 = (f32[512,512]{1,0:T(8,128)}, f32[512,512]{1,0:T(8,128)}, f32[512,128]{1,0:T(8,128)}, f32[512,512]{1,0:T(8,128)}, f32[512,512]{1,0:T(8,128)}) custom-call(f32[256,256]{1,0:T(8,128)} %get-tuple-element.190.ma, f32[256,256]{1,0:T(8,128)} %get-tuple-element.191.mb, f32[256,256]{1,0:T(8,128)} %get-tuple-element.192.u, ...), custom_call_target="tpu_custom_call" | custom-call | flops 6000000000 | bytes 8392704 | tf_op jit(solution)/shard_map/pallas_call | solution.py:224
  344.8 4.6 shard_map.102
  350.2 1.7 collective-permute-start.24
  352.0 21.9 %shard_map.103 = (f32[256,256]{1,0:T(8,128)}, f32[256,256]{1,0:T(8,128)}, f32[256,256]{1,0:T(8,128)}, f32[8,128]{1,0:T(8,128)}, f32[512,512]{1,0:T(8,128)}) custom-call(f32[512,512]{1,0:T(8,128)} %get-tuple-element.189.q, f32[512,512]{1,0:T(8,128)} %copy-done.20, f32[512,512]{1,0:T(8,128)} %copy-done.24), custom_call_target="tpu_custom_call" | custom-call | flops 4000000000 | bytes 4984832 | tf_op jit(solution)/shard_map/pallas_call | solution.py:224
  374.8 12.0 %shard_map.104 = (f32[512,512]{1,0:T(8,128)}, f32[512,512]{1,0:T(8,128)}, f32[512,128]{1,0:T(8,128)}, f32[512,512]{1,0:T(8,128)}, f32[512,512]{1,0:T(8,128)}) custom-call(f32[256,256]{1,0:T(8,128)} %get-tuple-element.202.ma, f32[256,256]{1,0:T(8,128)} %get-tuple-element.203.mb, f32[256,256]{1,0:T(8,128)} %get-tuple-element.204.u, ...), custom_call_target="tpu_custom_call" | custom-call | flops 6000000000 | bytes 8392704 | tf_op jit(solution)/shard_map/pallas_call | solution.py:224
  391.8 21.7 %shard_map.105 = (f32[256,256]{1,0:T(8,128)}, f32[256,256]{1,0:T(8,128)}, f32[256,256]{1,0:T(8,128)}, f32[8,128]{1,0:T(8,128)}, f32[512,512]{1,0:T(8,128)}) custom-call(f32[512,512]{1,0:T(8,128)} %get-tuple-element.201.q, f32[512,512]{1,0:T(8,128)} %copy-done.36, f32[512,512]{1,0:T(8,128)} %copy-done.37), custom_call_target="tpu_custom_call" | custom-call | flops 4000000000 | bytes 4984832 | tf_op jit(solution)/shard_map/pallas_call | solution.py:224
  413.5 6.2 %shard_map.106.own = f32[1,640]{1,0:T(1,128)} custom-call(f32[256,256]{1,0:T(8,128)} %get-tuple-element.209.refs_0_, f32[256,256]{1,0:T(8,128)} %get-tuple-element.210.refs_1_, f32[256,256]{1,0:T(8,128)} %get-tuple-element.211.refs_2_, f32[8,128]{1,0:T(8,128)} %get-tuple-element.212.refs_3_, f32[512,512]{1,0:T(8,128)} %get-tuple-element.213.refs_4_, ...), custom_call_target="tpu_custom_call" | custom-call | flops 100000000 | bytes 1907712 | tf_op jit(solution)/shard_map/pallas_call | solution.py:224
  421.7 2.8 shard_map.107.own
  426.4 2.8 shard_map.108.own
  431.2 2.8 shard_map.109.own
  436.0 2.8 shard_map.110.own
  440.7 2.8 shard_map.111.own
  445.5 2.8 shard_map.112.own
  448.3 144.4 %collective-permute-start.39 = (f32[1,640]{1,0:T(1,128)}, f32[1,640]{1,0:T(1,128)S(1)}, u32[]{:S(2)}, u32[]{:S(2)}) collective-permute-start(f32[1,640]{1,0:T(1,128)} %shard_map.112.own), channel_id=1, source_target_pairs={{1,2},{3,4},{5,6},{7,8},{9,10},{11,12},{13,14},{15,16},{17,18},{19... | collective-permute-start | bytes 7688 | tf_op jit(solution)/shard_map/ppermute | solution.py:239
  594.0 6.5 %collective-permute-done.39.from_left = f32[1,640]{1,0:T(1,128)S(1)} collective-permute-done((f32[1,640]{1,0:T(1,128)}, f32[1,640]{1,0:T(1,128)S(1)}, u32[]{:S(2)}, u32[]{:S(2)}) %collective-permute-start.39) | collective-permute-done | bytes 2592 | tf_op jit(solution)/shard_map/ppermute | solution.py:239
  601.1 2.8 shard_map.113
  605.2 3.2 all-to-all-start.3
  610.8 2.8 all-to-all-done.3
  (169 shorter events, 46.1 us)
Async XLA Ops:
  0.6 32.3 %copy-start = (f32[4,512]{1,0:T(4,128)S(1)}, f32[4,512]{1,0:T(4,128)}, u32[]{:S(2)}) copy-start(f32[4,512]{1,0:T(4,128)} %param.16) | copy-start | bytes 24580
  29.4 16.3 %all-to-all-start = ((f32[4,512,128]{2,1,0:T(8,128)}), f32[4,512,128]{2,1,0:T(8,128)S(1)}, u32[]{:S(2)}, u32[]{:S(2)}) async-start(f32[4,512,128]{2,1,0:T(8,128)} %param.12), calls=%async_computation | async-start | bytes 2097152 | tf_op jit(solution)/shard_map/all_to_all | solution.py:249
  35.2 35.9 %collective-permute-start = (f32[512,512]{1,0:T(8,128)}, f32[512,512]{1,0:T(8,128)}, u32[]{:S(2)}, u32[]{:S(2)}) collective-permute-start(f32[512,512]{1,0:T(8,128)} %bitcast.47), channel_id=1, source_target_pairs={{1,0},{3,2},{5,4},{7,6},{9,8},{11,10},{13,12},{15,14},{17,16},{19,... | collective-permute-start | bytes 3145736 | tf_op jit(solution)/shard_map/ppermute | solution.py:239
  83.0 35.0 %collective-permute-start.1 = (f32[512,512]{1,0:T(8,128)}, f32[512,512]{1,0:T(8,128)S(1)}, u32[]{:S(2)}, u32[]{:S(2)}) collective-permute-start(f32[512,512]{1,0:T(8,128)} %get-tuple-element.137), channel_id=1, source_target_pairs={{0,1},{2,3},{4,5},{6,7},{8,9},{10,11},{12,13},{14,15},{16,17},{18,... | collective-permute-start | bytes 3145736 | tf_op jit(solution)/shard_map/ppermute | solution.py:239
  94.8 23.2 %collective-permute-start.2 = (f32[512,512]{1,0:T(8,128)}, f32[512,512]{1,0:T(8,128)S(1)}, u32[]{:S(2)}, u32[]{:S(2)}) collective-permute-start(f32[512,512]{1,0:T(8,128)} %get-tuple-element.138), channel_id=1, source_target_pairs={{2,1},{4,3},{6,5},{8,7},{10,9},{12,11},{14,13},{16,15},{18,17},{20... | collective-permute-start | bytes 3145736 | tf_op jit(solution)/shard_map/ppermute | solution.py:239
  118.0 17.6 %copy-start.18 = (f32[512,512]{1,0:T(8,128)}, f32[512,512]{1,0:T(8,128)S(1)}, u32[]{:S(2)}) copy-start(f32[512,512]{1,0:T(8,128)S(1)} %collective-permute-done.1.from_left) | copy-start | bytes 3145732
  118.0 17.6 %copy-start.19 = (f32[512,512]{1,0:T(8,128)}, f32[512,512]{1,0:T(8,128)S(1)}, u32[]{:S(2)}) copy-start(f32[512,512]{1,0:T(8,128)S(1)} %collective-permute-done.2.from_right) | copy-start | bytes 3145732
  118.0 39.4 %collective-permute-start.3 = (f32[512,512]{1,0:T(8,128)}, f32[512,512]{1,0:T(8,128)S(1)}, u32[]{:S(2)}, u32[]{:S(2)}) collective-permute-start(f32[512,512]{1,0:T(8,128)} %shard_map.87), channel_id=1, source_target_pairs={{0,1},{4,5},{8,9},{12,13},{16,17},{20,21},{24,25},{28,29},{32,33},... | collective-permute-start | bytes 3145736 | tf_op jit(solution)/shard_map/ppermute | solution.py:239
  133.9 23.4 %collective-permute-start.4 = (f32[512,512]{1,0:T(8,128)}, f32[512,512]{1,0:T(8,128)}, u32[]{:S(2)}, u32[]{:S(2)}) collective-permute-start(f32[512,512]{1,0:T(8,128)} %shard_map.87), channel_id=1, source_target_pairs={{2,1},{6,5},{10,9},{14,13},{18,17},{22,21},{26,25},{30,29},{34,33}... | collective-permute-start | bytes 3145736 | tf_op jit(solution)/shard_map/ppermute | solution.py:239
  170.4 6.1 collective-permute-start.5
  171.1 5.4 collective-permute-start.6
  176.5 24.3 %collective-permute-start.7 = (f32[512,512]{1,0:T(8,128)}, f32[512,512]{1,0:T(8,128)S(1)}, u32[]{:S(2)}, u32[]{:S(2)}) collective-permute-start(f32[512,512]{1,0:T(8,128)} %shard_map.90), channel_id=1, source_target_pairs={{1,3},{9,11},{17,19},{25,27},{33,35},{41,43},{49,51},{57,59},{65,6... | collective-permute-start | bytes 3145736 | tf_op jit(solution)/shard_map/ppermute | solution.py:239
  177.2 23.6 %collective-permute-start.8 = (f32[512,512]{1,0:T(8,128)}, f32[512,512]{1,0:T(8,128)}, u32[]{:S(2)}, u32[]{:S(2)}) collective-permute-start(f32[512,512]{1,0:T(8,128)} %shard_map.90), channel_id=1, source_target_pairs={{5,3},{13,11},{21,19},{29,27},{37,35},{45,43},{53,51},{61,59},{69,... | collective-permute-start | bytes 3145736 | tf_op jit(solution)/shard_map/ppermute | solution.py:239
  213.8 6.1 collective-permute-start.9
  214.5 5.4 collective-permute-start.10
  219.9 24.0 %collective-permute-start.11 = (f32[512,512]{1,0:T(8,128)}, f32[512,512]{1,0:T(8,128)S(1)}, u32[]{:S(2)}, u32[]{:S(2)}) collective-permute-start(f32[512,512]{1,0:T(8,128)} %shard_map.93), channel_id=1, source_target_pairs={{3,7},{19,23},{35,39},{51,55},{67,71},{83,87},{99,103},{115,119}} | collective-permute-start | bytes 3145736 | tf_op jit(solution)/shard_map/ppermute | solution.py:239
  220.6 23.3 %collective-permute-start.12 = (f32[512,512]{1,0:T(8,128)}, f32[512,512]{1,0:T(8,128)}, u32[]{:S(2)}, u32[]{:S(2)}) collective-permute-start(f32[512,512]{1,0:T(8,128)} %shard_map.93), channel_id=1, source_target_pairs={{11,7},{27,23},{43,39},{59,55},{75,71},{91,87},{107,103},{123,119}} | collective-permute-start | bytes 3145736 | tf_op jit(solution)/shard_map/ppermute | solution.py:239
  256.8 6.1 collective-permute-start.13
  257.5 5.4 collective-permute-start.14
  263.0 24.3 %collective-permute-start.15 = (f32[512,512]{1,0:T(8,128)}, f32[512,512]{1,0:T(8,128)S(1)}, u32[]{:S(2)}, u32[]{:S(2)}) collective-permute-start(f32[512,512]{1,0:T(8,128)} %shard_map.96), channel_id=1, source_target_pairs={{7,15},{39,47},{71,79},{103,111}} | collective-permute-start | bytes 3145736 | tf_op jit(solution)/shard_map/ppermute | solution.py:239
  263.7 23.5 %collective-permute-start.16 = (f32[512,512]{1,0:T(8,128)}, f32[512,512]{1,0:T(8,128)}, u32[]{:S(2)}, u32[]{:S(2)}) collective-permute-start(f32[512,512]{1,0:T(8,128)} %shard_map.96), channel_id=1, source_target_pairs={{23,15},{55,47},{87,79},{119,111}} | collective-permute-start | bytes 3145736 | tf_op jit(solution)/shard_map/ppermute | solution.py:239
  300.2 6.0 collective-permute-start.17
  300.9 5.3 collective-permute-start.18
  306.2 24.0 %collective-permute-start.19 = (f32[512,512]{1,0:T(8,128)}, f32[512,512]{1,0:T(8,128)S(1)}, u32[]{:S(2)}, u32[]{:S(2)}) collective-permute-start(f32[512,512]{1,0:T(8,128)} %shard_map.99), channel_id=1, source_target_pairs={{15,31},{79,95}} | collective-permute-start | bytes 3145736 | tf_op jit(solution)/shard_map/ppermute | solution.py:239
  306.9 23.3 %collective-permute-start.20 = (f32[512,512]{1,0:T(8,128)}, f32[512,512]{1,0:T(8,128)}, u32[]{:S(2)}, u32[]{:S(2)}) collective-permute-start(f32[512,512]{1,0:T(8,128)} %shard_map.99), channel_id=1, source_target_pairs={{47,31},{111,95}} | collective-permute-start | bytes 3145736 | tf_op jit(solution)/shard_map/ppermute | solution.py:239
  343.3 6.1 collective-permute-start.21
  344.0 5.4 collective-permute-start.22
  349.5 24.3 %collective-permute-start.23 = (f32[512,512]{1,0:T(8,128)}, f32[512,512]{1,0:T(8,128)S(1)}, u32[]{:S(2)}, u32[]{:S(2)}) collective-permute-start(f32[512,512]{1,0:T(8,128)} %shard_map.102), channel_id=1, source_target_pairs={{31,63}} | collective-permute-start | bytes 3145736 | tf_op jit(solution)/shard_map/ppermute | solution.py:239
  350.2 23.6 %collective-permute-start.24 = (f32[512,512]{1,0:T(8,128)}, f32[512,512]{1,0:T(8,128)}, u32[]{:S(2)}, u32[]{:S(2)}) collective-permute-start(f32[512,512]{1,0:T(8,128)} %shard_map.102), channel_id=1, source_target_pairs={{95,63}} | collective-permute-start | bytes 3145736 | tf_op jit(solution)/shard_map/ppermute | solution.py:239
  386.8 3.0 collective-permute-start.25
  387.5 2.3 collective-permute-start.26
  389.3 24.3 %copy-start.2 = (f32[128,128]{1,0:T(8,128)}, f32[128,128]{1,0:T(8,128)S(1)}, u32[]{:S(2)}) copy-start(f32[128,128]{1,0:T(8,128)S(1)} %scatter.14.refs_5_) | copy-start | bytes 196612
  419.7 1.3 collective-permute-start.27
  420.4 0.7 collective-permute-start.28
  424.5 1.3 collective-permute-start.29
  425.1 0.7 collective-permute-start.30
  429.3 1.3 collective-permute-start.31
  429.9 0.7 collective-permute-start.32
  434.0 1.3 collective-permute-start.33
  434.7 0.7 collective-permute-start.34
  438.8 1.3 collective-permute-start.35
  439.5 0.7 collective-permute-start.36
  443.5 1.3 collective-permute-start.37
  444.2 0.7 collective-permute-start.38
  448.3 152.2 %collective-permute-start.39 = (f32[1,640]{1,0:T(1,128)}, f32[1,640]{1,0:T(1,128)S(1)}, u32[]{:S(2)}, u32[]{:S(2)}) collective-permute-start(f32[1,640]{1,0:T(1,128)} %shard_map.112.own), channel_id=1, source_target_pairs={{1,2},{3,4},{5,6},{7,8},{9,10},{11,12},{13,14},{15,16},{17,18},{19... | collective-permute-start | bytes 7688 | tf_op jit(solution)/shard_map/ppermute | solution.py:239
  592.7 7.8 %collective-permute-start.40 = (f32[1,640]{1,0:T(1,128)}, f32[1,640]{1,0:T(1,128)S(1)}, u32[]{:S(2)}, u32[]{:S(2)}) collective-permute-start(f32[1,640]{1,0:T(1,128)} %shard_map.112.own), channel_id=1, source_target_pairs={{1,0},{3,2},{5,4},{7,6},{9,8},{11,10},{13,12},{15,14},{17,16},{19,... | collective-permute-start | bytes 7688 | tf_op jit(solution)/shard_map/ppermute | solution.py:239
  603.9 10.2 %copy-start.1 = (f32[4,512]{1,0:T(4,128)S(1)}, f32[4,512]{1,0:T(4,128)}, u32[]{:S(2)}) copy-start(f32[4,512]{1,0:T(4,128)} %param.16) | copy-start | bytes 24580
  605.2 8.4 %all-to-all-start.3 = ((f32[1,4,128]{2,0,1:T(1,128)}), f32[1,4,128]{2,0,1:T(1,128)S(1)}, u32[]{:S(2)}, u32[]{:S(2)}) async-start(f32[1,4,128]{2,0,1:T(1,128)} %slice_bitcast_fusion), calls=%async_computation.3 | async-start | bytes 4096 | tf_op jit(solution)/shard_map/all_to_all | solution.py:314
  (34 other events, 42.3 us)

commit v2 on v1

--- a/solution.py
+++ b/solution.py
@@ -10,6 +10,7 @@
 TILE = 128
 HALF = 256
 NODES = 512
+EFFECTS = 64
 
 
 def mm(a, b):
@@ -114,13 +115,43 @@
     return lax.fori_loop(0, 4, body, jnp.zeros((8, TILE), F32))
 
 
-def factor_first_kernel(q, ma, mb, u, logs, s, inv):
-    s[...] = q[...]
+def factor_first_kernel(place, own, one, two, three, rhs, ma, mb, u, logs, q_new, s, inv):
+    col, pos = place[0], place[1]
+    right = rhs[pl.ds(pos, 1), :]
+    for back, ref in enumerate((own, one, two, three)):
+        source = lax.rem(col - back + 4, 4)
+        o = pl.multiple_of(source * TILE, TILE)
+        s[:, pl.ds(o, TILE)] = ref[0:NODES, :]
+    q_new[...] = s[...]
+    q_new[TILE:HALF, 0:TILE] = jnp.zeros((TILE, TILE), F32)
+    row = lax.broadcasted_iota(jnp.int32, (TILE - EFFECTS, TILE), 0)
+    for back, ref in enumerate((own, one, two, three)):
+        source = lax.rem(col - back + 4, 4)
+        part = jnp.zeros((1, TILE), F32)
+        for k in range(4):
+            part = jnp.where(source == k, right[:, k * TILE : (k + 1) * TILE], part)
+        rest = jnp.where(row == 0, jnp.broadcast_to(part, row.shape), 0.0)
+        edge = jnp.concatenate([ref[NODES : NODES + EFFECTS, :], rest], axis=0).T
+        o0 = pl.multiple_of(HALF + lax.rem(source, 2) * TILE, TILE)
+        o1 = pl.multiple_of((source // 2) * TILE, TILE)
+        q_new[pl.ds(o0, TILE), pl.ds(o1, TILE)] = edge
     logs[...] = factor_body(s, inv, ma, mb, u)
 
 
-def factor_next_kernel(q, from_left, from_right, ma, mb, u, logs, q_new, s, inv):
-    value = q[...] - from_left[...] - from_right[...]
+def couple_first_kernel(place, own, one, two, three, low, high):
+    col, keep = place[0], place[2]
+    for back, ref in enumerate((own, one, two, three)):
+        source = lax.rem(col - back + 4, 4)
+        o = pl.multiple_of(source * TILE, TILE)
+        high[:, pl.ds(o, TILE)] = ref[1]
+        low[pl.ds(o, TILE), :] = jnp.where(keep > 0, ref[0].T, 0.0)
+
+
+def factor_next_kernel(count, *refs):
+    parts, (ma, mb, u, logs, q_new, s, inv) = refs[:count], refs[count:]
+    value = parts[0][...]
+    for part in parts[1:]:
+        value = value - part[...]
     s[...] = value
     q_new[...] = value
     logs[...] = factor_body(s, inv, ma, mb, u)
@@ -150,22 +181,28 @@
     return sums + jnp.where((row == 65) & (lane == 65), log_sum, 0.0)
 
 
-def eliminate_kernel(ma, mb, u, logs, q, low, high, wl, wh, ws, left, right):
+def near_kernel(odd, ma, mb, u, logs, q, low, high, wn, ws, out):
+    flag = odd[0] != 0
+    pick = lambda rows: jnp.where(flag, low[rows, :], high[rows, :])
     solve_into(ma, mb, u, q[HALF:NODES, 0:TILE], q[HALF:NODES, TILE:HALF], ws)
-    solve_into(ma, mb, u, low[0:HALF, :], low[HALF:NODES, :], wl)
-    packed_products(wl, ws, left, jnp.zeros((TILE, TILE), F32))
-    solve_into(ma, mb, u, high[0:HALF, :], high[HALF:NODES, :], wh)
-    packed_products(wh, ws, right, corner_sums(q, ws, logs))
-
-
-def couple_kernel(odd, wl, wh, out):
-    @pl.when(odd[0] == 0)
-    def _():
-        out[...] = -mtm(wh[...], wl[...])
-
-    @pl.when(odd[0] != 0)
-    def _():
-        out[...] = -mtm(wl[...], wh[...])
+    solve_into(ma, mb, u, pick(slice(0, HALF)), pick(slice(HALF, NODES)), wn)
+    packed_products(wn, ws, out, jnp.where(flag, 0.0, corner_sums(q, ws, logs)))
+
+
+def far_kernel(count, odd, ma, mb, u, logs, low, high, wn, ws, *refs):
+    parts, outs = refs[: 1 + count], refs[1 + count :]
+    wf, new, out = outs[:3]
+    q = parts[0]
+    flag = odd[0] != 0
+    pick = lambda rows: jnp.where(flag, high[rows, :], low[rows, :])
+    solve_into(ma, mb, u, pick(slice(0, HALF)), pick(slice(HALF, NODES)), wf)
+    new[...] = -mtm(wn[...], wf[...])
+    packed_products(wf, ws, out, jnp.where(flag, corner_sums(q, ws, logs), 0.0))
+    if count:
+        value = q[...]
+        for part in parts[1:]:
+            value = value - part[...]
+        outs[3][...] = value
 
 
 def back_solve(ma, mb, u, z_top, z_bottom):
@@ -197,17 +234,18 @@
     out[:, NODES : NODES + TILE] = jnp.where(lane1 == 64, log_total / total, x_fixed)
 
 
-def back_kernel(leaving, from_left, from_right, own, ma, mb, u, wl, wh, ws, out):
+def back_kernel(flags, from_left, from_right, own, ma, mb, u, wn, wf, ws, out):
     lane1 = lax.broadcasted_iota(jnp.int32, (1, TILE), 1)
     extra = from_right[:, NODES : NODES + TILE]
     weights = jnp.where(lane1 == 64, 1.0, jnp.where(lane1 < 64, -extra, 0.0))
-    z = (
-        jnp.sum(ws[...] * weights, axis=1, keepdims=True)
-        - jnp.sum(wl[...] * from_left[:, 0:NODES], axis=1, keepdims=True)
-        - jnp.sum(wh[...] * from_right[:, 0:NODES], axis=1, keepdims=True)
+    odd = flags[1] != 0
+    x_left, x_right = from_left[:, 0:NODES], from_right[:, 0:NODES]
+    x_near, x_far = jnp.where(odd, x_left, x_right), jnp.where(odd, x_right, x_left)
+    z = jnp.sum(ws[...] * weights, axis=1, keepdims=True) - jnp.sum(
+        wn[...] * x_near + wf[...] * x_far, axis=1, keepdims=True
     )
     x_top, x_bottom = back_solve(ma, mb, u, z[0:HALF], z[HALF:NODES])
-    mine = leaving[0] != 0
+    mine = flags[0] != 0
     out[:, 0:HALF] = jnp.where(mine, x_top, own[:, 0:HALF])
     out[:, HALF:NODES] = jnp.where(mine, x_bottom, own[:, HALF:NODES])
     out[:, NODES : NODES + TILE] = jnp.where(mine, extra, own[:, NODES : NODES + TILE])
@@ -235,55 +273,93 @@
 WORK = ((NODES, NODES), (TILE, TILE))
 
 
+def device_of(t):
+    return (t // 4) * 4 + (t % 4 + 2 * ((t // 4) % 2)) % 4
+
+
 def moved(x, pairs):
-    return lax.ppermute(x, AXES, pairs)
+    return lax.ppermute(x, AXES, [(device_of(i), device_of(j)) for i, j in pairs])
 
 
 def per_device(blocks, upper, arrow, tip, rhs, rhs_fixed):
     node_count = blocks.shape[1]
     effects = tip.shape[0]
-    cols = lax.axis_size("col")
+    cols = 4
     count = lax.axis_size("tm") * cols
-    col = lax.axis_index("col")
-    t = lax.axis_index("tm") * cols + col
-    take = lambda x: lax.all_to_all(x, "col", split_axis=0, concat_axis=2, tiled=True)[0]
-    diagonal = take(blocks)
-    coupling = take(upper)
-    side = take(arrow)
-    own_rhs = lax.dynamic_slice_in_dim(rhs, col, 1, 0)
-    ma, mb, u, logs = call(factor_first_kernel, (diagonal,), FACTORS, WORK, flops=4 * 10**9)
-    high = moved(coupling, [(i + 1, i) for i in range(0, count, 2)])
-    low = coupling.T * (t > 0).astype(F32)
-    edge = jnp.concatenate(
-        [side, own_rhs, jnp.zeros((TILE - effects - 1, node_count), F32)], axis=0
-    ).T
-    packed = jnp.concatenate([edge[0:HALF], edge[HALF:NODES]], axis=1)
-    q = diagonal.at[HALF:NODES, 0:HALF].set(packed)
-    q = q.at[TILE:HALF, 0:TILE].set(0.0)
-    kept = []
+    col, shift = lax.axis_index("col"), 2 * (lax.axis_index("tm") % 2)
+    pos = (col + shift) % cols
+    t = lax.axis_index("tm") * cols + pos
+    place = jnp.stack([col, pos, (t > 0).astype(jnp.int32)]).astype(jnp.int32)
+
+    def diagonal_for(p):
+        return jnp.concatenate(
+            [
+                lax.dynamic_index_in_dim(blocks, p, 0, keepdims=False),
+                lax.dynamic_index_in_dim(arrow, p, 0, keepdims=False),
+            ],
+            axis=0,
+        )
+
+    got, wanted = [diagonal_for(pos)], [lax.dynamic_slice_in_dim(upper, pos, 2, 0)]
+    for d in (1, 2, 3):
+        pairs = [(c, (c + d) % cols) for c in range(cols)]
+        got.append(lax.ppermute(diagonal_for((pos + d) % cols), "col", pairs))
+        wanted.append(lax.dynamic_slice_in_dim(upper, (pos + d) % cols, 2, 0))
+    got, wanted = lax.optimization_barrier((got, wanted))
+    for d in (1, 2, 3):
+        pairs = [(c, (c + d) % cols) for c in range(cols) if (c + d) % 2 == 0]
+        wanted[d] = lax.ppermute(wanted[d], "col", pairs)
+    big = shape(NODES, NODES)
+    ma, mb, u, logs, q = call(
+        factor_first_kernel, (place, *got, rhs), FACTORS + (big,), WORK, scalars=1, flops=4 * 10**9
+    )
+    low, high = call(couple_first_kernel, (place, *wanted), (big, big), scalars=1, flops=10**6)
+    kept, late = [], ()
     level = 0
     while (1 << level) < count:
         s = 1 << level
         leaving = [(2 * k + 1) * s - 1 for k in range(count // (2 * s))]
-        products = (shape(NODES, NODES), shape(NODES, NODES), shape(NODES, TILE)) + (
-            shape(NODES, NODES),
-        ) * 2
-        wl, wh, ws, left, right = call(
-            eliminate_kernel, (ma, mb, u, logs, q, low, high), products, flops=6 * 10**9
+        even, uneven = leaving[0::2], leaving[1::2]
+        odd = (((t + 1) // (2 * s)) % 2).astype(jnp.int32).reshape(1)
+        last = 2 * s == count
+        wn, ws, near = call(
+            near_kernel,
+            (odd, ma, mb, u, logs, q, low, high),
+            (big, shape(NODES, TILE), big),
+            scalars=1,
+            flops=3 * 10**9,
         )
-        kept.append((ma, mb, u, wl, wh, ws))
-        got_left = moved(right, [(i, i + s) for i in leaving])
-        got_right = moved(left, [(i, i - s) for i in leaving if i >= s])
-        if 2 * s < count:
-            odd = (((t + 1) // (2 * s)) % 2).astype(jnp.int32).reshape(1)
-            (new,) = call(couple_kernel, (odd, wl, wh), (shape(NODES, NODES),), scalars=1, flops=10**9)
-            new, got_left, got_right = lax.optimization_barrier((new, got_left, got_right))
-            low = moved(new, [(i, i + s) for i in leaving[0::2]])
-            high = moved(new, [(i, i - s) for i in leaving[1::2]])
+        arrived = [moved(near, [(i, i + s) for i in even])]
+        if last:
+            wf = jnp.zeros((NODES, NODES), F32)
+            parts = (q, *arrived, *late)
+        else:
+            arrived.append(moved(near, [(i, i - s) for i in uneven]))
+            n = len(late)
+            wf, new, far, *q_adjusted = call(
+                lambda *refs: far_kernel(n, *refs),
+                (odd, ma, mb, u, logs, low, high, wn, ws, q, *late),
+                (big,) * (4 if n else 3),
+                scalars=1,
+                flops=4 * 10**9,
+            )
+            q = q_adjusted[0] if n else q
+            new, far, arrived = lax.optimization_barrier((new, far, arrived))
+            parts = (q, *arrived)
+            late = (
+                moved(far, [(i, i - s) for i in even if i >= s]),
+                moved(far, [(i, i + s) for i in uneven]),
+            )
+            low = moved(new, [(i, i + s) for i in even])
+            high = moved(new, [(i, i - s) for i in uneven])
+        mine = ((t + 1) % (2 * s) == s).astype(jnp.int32).reshape(1)
+        flags = jnp.concatenate([mine, odd])
+        kept.append((flags, s, (ma, mb, u, wn, wf, ws)))
+        n_parts = len(parts)
         ma, mb, u, logs, q = call(
-            factor_next_kernel,
-            (q, got_left, got_right),
-            FACTORS + (shape(NODES, NODES),),
+            lambda *refs: factor_next_kernel(n_parts, *refs),
+            parts,
+            FACTORS + (big,),
             WORK,
             flops=4 * 10**9,
         )
@@ -298,21 +374,20 @@
         ((NODES, TILE), (TILE, TILE)),
         flops=10**8,
     )
-    for level in reversed(range(len(kept))):
-        s = 1 << level
+    for flags, s, factors in reversed(kept):
         leaving = [(2 * k + 1) * s - 1 for k in range(count // (2 * s))]
         from_left = moved(state, [(i - s, i) for i in leaving if i >= s])
         from_right = moved(state, [(i + s, i) for i in leaving])
-        mine = ((t + 1) % (2 * s) == s).astype(jnp.int32).reshape(1)
         (state,) = call(
             back_kernel,
-            (mine, from_left, from_right, state) + kept[level],
+            (flags, from_left, from_right, state) + factors,
             (shape(1, NODES + TILE),),
             scalars=1,
             flops=10**7,
         )
-    solution = lax.all_to_all(state[:, 0:NODES], "col", split_axis=1, concat_axis=0, tiled=True)
-    return (solution, state[0, NODES : NODES + effects], state[0, NODES + 64])
+    rows = lax.all_to_all(state[:, 0:NODES], "col", split_axis=1, concat_axis=0, tiled=True)
+    rows = jnp.where(shift > 0, jnp.roll(rows, 2, axis=0), rows)
+    return (rows, state[0, NODES : NODES + effects], state[0, NODES + 64])
 
 
 def solution(mesh):

time: 622 us -> 602 us (0.968)
  blocking collectives: 28.7 us -> 0 us
  Pallas kernels: 310 us -> 323 us
  waiting for transfers between devices: 26.9 us -> 16.3 us
  starting transfers between devices: 222 us -> 214 us
    all_to_all x2 -> x0, blocking collectives: 28.7 us -> none  [per_device(): lax.all_to_all(x, 'col', split_axis=0, concat_axis=2, tiled=True)[0]]
    pallas_call x29 -> x30, Pallas kernels: 310 us -> 323 us  [call(): pl.pallas_call(kernel, out_shape=tuple(outs), in_specs=[smem] * scalars +...]
    all_to_all x1 -> x0, waiting for transfers between devices: 9.17 us -> none  [per_device(): lax.all_to_all(x, 'col', split_axis=0, concat_axis=2, tiled=True)[0]]
    unnamed x82 -> x98, local copies, waits for them, and re-layouts: 14.9 us -> 21.2 us
    ppermute x41 -> x57, starting transfers between devices: 215 us -> 210 us  [the longest x51 161 us: moved(): lax.ppermute(x, AXES, [(device_of(i), device_of(j)) for i, j in pairs])]
    ppermute x41 -> x57, waiting for transfers between devices: 15 us -> 13.6 us  [the longest x3 7.23 us: per_device(): got.append(lax.ppermute(diagonal_for((pos + d) % cols), 'col', pairs))]
  transfers between devices with their start and end apart: 43 -> 58, of which waited for: 4 -> 4; matrix products, arithmetic and copies ran while one was open for 2% -> 2% of each run, Pallas kernels for 29% -> 45%
where the time goes in v2:
time: 602 us; the launch traced here: 591 us
  Pallas kernels  323 us (54%)
  starting transfers between devices  214 us (36%)
  local copies, waits for them, and re-layouts  29.5 us (5%)
  waiting for transfers between devices  16.3 us (3%)
  other arithmetic  6.41 us (1%)
    pallas_call x30, Pallas kernels, call(): pl.pallas_call(kernel, out_shape=tuple(outs), in_specs=[smem] * scalars +...  323 us
    ppermute x51, starting transfers between devices, moved(): lax.ppermute(x, AXES, [(device_of(i), device_of(j)) for i, j in pairs])  161 us
    ppermute x3, starting transfers between devices, per_device(): got.append(lax.ppermute(diagonal_for((pos + d) % cols), 'col', pairs))  27.6 us
    ppermute x3, starting transfers between devices, per_device(): wanted[d] = lax.ppermute(wanted[d], 'col', pairs)  21.5 us
    unnamed x98, local copies, waits for them, and re-layouts  21.2 us
  transfers between devices with their start and end apart: 58, of which 4 were waited for; matrix products, arithmetic and copies ran while one was open for 2% of the time, Pallas kernels for 45%

profile of v2, /device:TPU:6, one launch (start us, length us, event | category | flops | bytes accessed | tf_op | source)
XLA Modules:
  0.0 591.5 jit_solution(14143508097471203690)
XLA Ops:
  2.9 9.7 %collective-permute-start = (f32[576,128]{1,0:T(8,128)S(1)}, f32[576,128]{1,0:T(8,128)S(1)}, u32[]{:S(2)}, u32[]{:S(2)}) collective-permute-start(f32[576,128]{1,0:T(8,128)S(1)} %pad_maximum_fusion.1), channel_id=1, source_target_pairs={{0,1},{1,2},{2,3},{3,0},{4,5},{5,6},{6,7},{7,4},{8,9},{9,10},{10,1... | collective-permute-start | bytes 884744 | tf_op jit(solution)/shard_map/ppermute | solution.py:306
  12.6 9.0 %collective-permute-start.1 = (f32[576,128]{1,0:T(8,128)S(1)}, f32[576,128]{1,0:T(8,128)S(1)}, u32[]{:S(2)}, u32[]{:S(2)}) collective-permute-start(f32[576,128]{1,0:T(8,128)S(1)} %pad_maximum_fusion.2), channel_id=1, source_target_pairs={{0,2},{1,3},{2,0},{3,1},{4,6},{5,7},{6,4},{7,5},{8,10},{9,11},{10,... | collective-permute-start | bytes 884744 | tf_op jit(solution)/shard_map/ppermute | solution.py:306
  21.6 9.0 %collective-permute-start.2 = (f32[576,128]{1,0:T(8,128)S(1)}, f32[576,128]{1,0:T(8,128)S(1)}, u32[]{:S(2)}, u32[]{:S(2)}) collective-permute-start(f32[576,128]{1,0:T(8,128)S(1)} %pad_maximum_fusion.3), channel_id=1, source_target_pairs={{0,3},{1,0},{2,1},{3,2},{4,7},{5,4},{6,5},{7,6},{8,11},{9,8},{10,9... | collective-permute-start | bytes 884744 | tf_op jit(solution)/shard_map/ppermute | solution.py:306
  32.3 7.2 %collective-permute-done.2.three = f32[576,128]{1,0:T(8,128)S(1)} collective-permute-done((f32[576,128]{1,0:T(8,128)S(1)}, f32[576,128]{1,0:T(8,128)S(1)}, u32[]{:S(2)}, u32[]{:S(2)}) %collective-permute-start.2) | collective-permute-done | bytes 294944 | tf_op jit(solution)/shard_map/ppermute | solution.py:306
  40.2 9.3 %collective-permute-start.3 = (f32[2,512,128]{2,1,0:T(8,128)S(1)}, f32[2,512,128]{2,1,0:T(8,128)S(1)}, u32[]{:S(2)}, u32[]{:S(2)}) collective-permute-start(f32[2,512,128]{2,1,0:T(8,128)S(1)} %get-tuple-element.143), channel_id=1, source_target_pairs={{1,2},{3,0},{5,6},{7,4},{9,10},{11,8},{13,14},{15,12},{17,18},{19,... | collective-permute-start | bytes 1572872 | tf_op jit(solution)/shard_map/ppermute | solution.py:311
  49.5 10.8 %collective-permute-start.4 = (f32[2,512,128]{2,1,0:T(8,128)S(1)}, f32[2,512,128]{2,1,0:T(8,128)S(1)}, u32[]{:S(2)}, u32[]{:S(2)}) collective-permute-start(f32[2,512,128]{2,1,0:T(8,128)S(1)} %get-tuple-element.144), channel_id=1, source_target_pairs={{0,2},{2,0},{4,6},{6,4},{8,10},{10,8},{12,14},{14,12},{16,18},{18,... | collective-permute-start | bytes 1572872 | tf_op jit(solution)/shard_map/ppermute | solution.py:311
  62.3 21.1 %shard_map.85 = (f32[256,256]{1,0:T(8,128)}, f32[256,256]{1,0:T(8,128)}, f32[256,256]{1,0:T(8,128)}, f32[8,128]{1,0:T(8,128)}, f32[512,512]{1,0:T(8,128)}) custom-call(s32[3]{0:T(128)} %pad_add_fusion.7.place, f32[576,128]{1,0:T(8,128)} %pad_maximum_fusion.own, f32[576,128]{1,0:T(8,128)} %copy-done.45, f32[576,128]{1,0:T(8,128)} %copy-done.46, ...), custom_call_target="tpu_custom_call" | custom-call | flops 4000000000 | bytes 3026956 | tf_op jit(solution)/shard_map/pallas_call | solution.py:262
  85.2 3.2 shard_map.86
  88.5 8.4 %shard_map.87 = (f32[512,512]{1,0:T(8,128)}, f32[512,128]{1,0:T(8,128)}, f32[512,512]{1,0:T(8,128)}) custom-call(s32[1]{0:T(128)} %bitcast.1.odd.refs_0_, f32[256,256]{1,0:T(8,128)} %get-tuple-element.138.ma.refs_1_, f32[256,256]{1,0:T(8,128)} %get-tuple-element.139.mb.refs_2_, f32[256,256]{1,0:T(8,128)} %get-tuple-element.140.u.refs_3_, ...), custom_call_target="tpu_custom_call" | custom-call | flops 3000000000 | bytes 6295556 | tf_op jit(solution)/shard_map/pallas_call | solution.py:262
  96.8 4.6 collective-permute-start.6
  102.4 9.6 %shard_map.88 = (f32[512,512]{1,0:T(8,128)}, f32[512,512]{1,0:T(8,128)}, f32[512,512]{1,0:T(8,128)}) custom-call(s32[1]{0:T(128)} %bitcast.1.odd.refs_0_, f32[256,256]{1,0:T(8,128)} %get-tuple-element.138.ma.refs_1_, f32[256,256]{1,0:T(8,128)} %get-tuple-element.139.mb.refs_2_, f32[256,256]{1,0:T(8,128)} %get-tuple-element.140.u.refs_3_, ...), custom_call_target="tpu_custom_call" | custom-call | flops 4000000000 | bytes 8392708 | tf_op jit(solution)/shard_map/pallas_call | solution.py:262
  112.0 2.0 collective-permute-done.6.refs_1_
  115.0 5.6 collective-permute-start.8
  121.4 2.2 collective-permute-start.10
  123.7 10.1 %collective-permute-start.11 = (f32[512,512]{1,0:T(8,128)}, f32[512,512]{1,0:T(8,128)}, u32[]{:S(2)}, u32[]{:S(2)}) collective-permute-start(f32[512,512]{1,0:T(8,128)} %get-tuple-element.163), channel_id=1, source_target_pairs={{2,3},{4,5},{10,11},{12,13},{18,19},{20,21},{26,27},{28,29},{34,35... | collective-permute-start | bytes 3145736 | tf_op jit(solution)/shard_map/ppermute | solution.py:281
  133.8 21.8 %shard_map.89 = (f32[256,256]{1,0:T(8,128)}, f32[256,256]{1,0:T(8,128)}, f32[256,256]{1,0:T(8,128)}, f32[8,128]{1,0:T(8,128)}, f32[512,512]{1,0:T(8,128)}) custom-call(f32[512,512]{1,0:T(8,128)} %get-tuple-element.137.q.refs_9_.refs_0_, f32[512,512]{1,0:T(8,128)} %copy-done.41, f32[512,512]{1,0:T(8,128)} %copy-done.42), custom_call_target="tpu_custom_call" | custom-call | flops 4000000000 | bytes 4984832 | tf_op jit(solution)/shard_map/pallas_call | solution.py:262
  157.0 8.4 %shard_map.90 = (f32[512,512]{1,0:T(8,128)}, f32[512,128]{1,0:T(8,128)}, f32[512,512]{1,0:T(8,128)}) custom-call(s32[1]{0:T(128)} %bitcast.3.odd.refs_0_, f32[256,256]{1,0:T(8,128)} %get-tuple-element.155.ma.refs_1_, f32[256,256]{1,0:T(8,128)} %get-tuple-element.156.mb.refs_2_, f32[256,256]{1,0:T(8,128)} %get-tuple-element.157.u.refs_3_, ...), custom_call_target="tpu_custom_call" | custom-call | flops 3000000000 | bytes 6295556 | tf_op jit(solution)/shard_map/pallas_call | solution.py:262
  167.1 10.5 %shard_map.91 = (f32[512,512]{1,0:T(8,128)}, f32[512,512]{1,0:T(8,128)}, f32[512,512]{1,0:T(8,128)}, f32[512,512]{1,0:T(8,128)}) custom-call(s32[1]{0:T(128)} %bitcast.3.odd.refs_0_, f32[256,256]{1,0:T(8,128)} %get-tuple-element.155.ma.refs_1_, f32[256,256]{1,0:T(8,128)} %get-tuple-element.156.mb.refs_2_, f32[256,256]{1,0:T(8,128)} %get-tuple-element.157.u.refs_3_, ...), custom_call_target="tpu_custom_call" | custom-call | flops 4000000000 | bytes 11538436 | tf_op jit(solution)/shard_map/pallas_call | solution.py:262
  183.6 21.7 %shard_map.92 = (f32[256,256]{1,0:T(8,128)}, f32[256,256]{1,0:T(8,128)}, f32[256,256]{1,0:T(8,128)}, f32[8,128]{1,0:T(8,128)}, f32[512,512]{1,0:T(8,128)}) custom-call(f32[512,512]{1,0:T(8,128)} %get-tuple-element.164.refs_0_, f32[512,512]{1,0:T(8,128)} %copy-done.30, f32[512,512]{1,0:T(8,128)} %copy-done.39), custom_call_target="tpu_custom_call" | custom-call | flops 4000000000 | bytes 4984832 | tf_op jit(solution)/shard_map/pallas_call | solution.py:262
  206.6 8.4 %shard_map.93 = (f32[512,512]{1,0:T(8,128)}, f32[512,128]{1,0:T(8,128)}, f32[512,512]{1,0:T(8,128)}) custom-call(s32[1]{0:T(128)} %bitcast.5.odd.refs_0_, f32[256,256]{1,0:T(8,128)} %get-tuple-element.170.ma.refs_1_, f32[256,256]{1,0:T(8,128)} %get-tuple-element.171.mb.refs_2_, f32[256,256]{1,0:T(8,128)} %get-tuple-element.172.u.refs_3_, ...), custom_call_target="tpu_custom_call" | custom-call | flops 3000000000 | bytes 6295556 | tf_op jit(solution)/shard_map/pallas_call | solution.py:262
  216.7 10.4 %shard_map.94 = (f32[512,512]{1,0:T(8,128)}, f32[512,512]{1,0:T(8,128)}, f32[512,512]{1,0:T(8,128)}, f32[512,512]{1,0:T(8,128)}) custom-call(s32[1]{0:T(128)} %bitcast.5.odd.refs_0_, f32[256,256]{1,0:T(8,128)} %get-tuple-element.170.ma.refs_1_, f32[256,256]{1,0:T(8,128)} %get-tuple-element.171.mb.refs_2_, f32[256,256]{1,0:T(8,128)} %get-tuple-element.172.u.refs_3_, ...), custom_call_target="tpu_custom_call" | custom-call | flops 4000000000 | bytes 11538436 | tf_op jit(solution)/shard_map/pallas_call | solution.py:262
  231.3 2.1 collective-permute-start.23
  233.4 21.7 %shard_map.95 = (f32[256,256]{1,0:T(8,128)}, f32[256,256]{1,0:T(8,128)}, f32[256,256]{1,0:T(8,128)}, f32[8,128]{1,0:T(8,128)}, f32[512,512]{1,0:T(8,128)}) custom-call(f32[512,512]{1,0:T(8,128)} %get-tuple-element.179.refs_0_, f32[512,512]{1,0:T(8,128)} %copy-done.31, f32[512,512]{1,0:T(8,128)} %copy-done.40), custom_call_target="tpu_custom_call" | custom-call | flops 4000000000 | bytes 4984832 | tf_op jit(solution)/shard_map/pallas_call | solution.py:262
  256.5 8.4 %shard_map.96 = (f32[512,512]{1,0:T(8,128)}, f32[512,128]{1,0:T(8,128)}, f32[512,512]{1,0:T(8,128)}) custom-call(s32[1]{0:T(128)} %bitcast.7.odd.refs_0_, f32[256,256]{1,0:T(8,128)} %get-tuple-element.185.ma.refs_1_, f32[256,256]{1,0:T(8,128)} %get-tuple-element.186.mb.refs_2_, f32[256,256]{1,0:T(8,128)} %get-tuple-element.187.u.refs_3_, ...), custom_call_target="tpu_custom_call" | custom-call | flops 3000000000 | bytes 6295556 | tf_op jit(solution)/shard_map/pallas_call | solution.py:262
  266.6 10.5 %shard_map.97 = (f32[512,512]{1,0:T(8,128)}, f32[512,512]{1,0:T(8,128)}, f32[512,512]{1,0:T(8,128)}, f32[512,512]{1,0:T(8,128)}) custom-call(s32[1]{0:T(128)} %bitcast.7.odd.refs_0_, f32[256,256]{1,0:T(8,128)} %get-tuple-element.185.ma.refs_1_, f32[256,256]{1,0:T(8,128)} %get-tuple-element.186.mb.refs_2_, f32[256,256]{1,0:T(8,128)} %get-tuple-element.187.u.refs_3_, ...), custom_call_target="tpu_custom_call" | custom-call | flops 4000000000 | bytes 11538436 | tf_op jit(solution)/shard_map/pallas_call | solution.py:262
  283.1 21.7 %shard_map.98 = (f32[256,256]{1,0:T(8,128)}, f32[256,256]{1,0:T(8,128)}, f32[256,256]{1,0:T(8,128)}, f32[8,128]{1,0:T(8,128)}, f32[512,512]{1,0:T(8,128)}) custom-call(f32[512,512]{1,0:T(8,128)} %get-tuple-element.194.refs_0_, f32[512,512]{1,0:T(8,128)} %copy-done.28, f32[512,512]{1,0:T(8,128)} %copy-done.37), custom_call_target="tpu_custom_call" | custom-call | flops 4000000000 | bytes 4984832 | tf_op jit(solution)/shard_map/pallas_call | solution.py:262
  306.1 8.4 %shard_map.99 = (f32[512,512]{1,0:T(8,128)}, f32[512,128]{1,0:T(8,128)}, f32[512,512]{1,0:T(8,128)}) custom-call(s32[1]{0:T(128)} %bitcast.9.odd.refs_0_, f32[256,256]{1,0:T(8,128)} %get-tuple-element.200.ma.refs_1_, f32[256,256]{1,0:T(8,128)} %get-tuple-element.201.mb.refs_2_, f32[256,256]{1,0:T(8,128)} %get-tuple-element.202.u.refs_3_, ...), custom_call_target="tpu_custom_call" | custom-call | flops 3000000000 | bytes 6295556 | tf_op jit(solution)/shard_map/pallas_call | solution.py:262
  316.2 10.6 %shard_map.100 = (f32[512,512]{1,0:T(8,128)}, f32[512,512]{1,0:T(8,128)}, f32[512,512]{1,0:T(8,128)}, f32[512,512]{1,0:T(8,128)}) custom-call(s32[1]{0:T(128)} %bitcast.9.odd.refs_0_, f32[256,256]{1,0:T(8,128)} %get-tuple-element.200.ma.refs_1_, f32[256,256]{1,0:T(8,128)} %get-tuple-element.201.mb.refs_2_, f32[256,256]{1,0:T(8,128)} %get-tuple-element.202.u.refs_3_, ...), custom_call_target="tpu_custom_call" | custom-call | flops 4000000000 | bytes 11538436 | tf_op jit(solution)/shard_map/pallas_call | solution.py:262
  331.0 2.1 collective-permute-start.35
  333.1 21.7 %shard_map.101 = (f32[256,256]{1,0:T(8,128)}, f32[256,256]{1,0:T(8,128)}, f32[256,256]{1,0:T(8,128)}, f32[8,128]{1,0:T(8,128)}, f32[512,512]{1,0:T(8,128)}) custom-call(f32[512,512]{1,0:T(8,128)} %get-tuple-element.209.refs_0_, f32[512,512]{1,0:T(8,128)} %copy-done.29, f32[512,512]{1,0:T(8,128)} %copy-done.38), custom_call_target="tpu_custom_call" | custom-call | flops 4000000000 | bytes 4984832 | tf_op jit(solution)/shard_map/pallas_call | solution.py:262
  356.2 8.4 %shard_map.102 = (f32[512,512]{1,0:T(8,128)}, f32[512,128]{1,0:T(8,128)}, f32[512,512]{1,0:T(8,128)}) custom-call(s32[1]{0:T(128)} %bitcast.11.odd.refs_0_, f32[256,256]{1,0:T(8,128)} %get-tuple-element.215.ma.refs_1_, f32[256,256]{1,0:T(8,128)} %get-tuple-element.216.mb.refs_2_, f32[256,256]{1,0:T(8,128)} %get-tuple-element.217.u.refs_3_, ...), custom_call_target="tpu_custom_call" | custom-call | flops 3000000000 | bytes 6295556 | tf_op jit(solution)/shard_map/pallas_call | solution.py:262
  366.2 10.5 %shard_map.103 = (f32[512,512]{1,0:T(8,128)}, f32[512,512]{1,0:T(8,128)}, f32[512,512]{1,0:T(8,128)}, f32[512,512]{1,0:T(8,128)}) custom-call(s32[1]{0:T(128)} %bitcast.11.odd.refs_0_, f32[256,256]{1,0:T(8,128)} %get-tuple-element.215.ma.refs_1_, f32[256,256]{1,0:T(8,128)} %get-tuple-element.216.mb.refs_2_, f32[256,256]{1,0:T(8,128)} %get-tuple-element.217.u.refs_3_, ...), custom_call_target="tpu_custom_call" | custom-call | flops 4000000000 | bytes 11538436 | tf_op jit(solution)/shard_map/pallas_call | solution.py:262
  382.7 21.7 %shard_map.104 = (f32[256,256]{1,0:T(8,128)}, f32[256,256]{1,0:T(8,128)}, f32[256,256]{1,0:T(8,128)}, f32[8,128]{1,0:T(8,128)}, f32[512,512]{1,0:T(8,128)}) custom-call(f32[512,512]{1,0:T(8,128)} %get-tuple-element.224.refs_0_, f32[512,512]{1,0:T(8,128)} %copy-done.21, f32[512,512]{1,0:T(8,128)} %copy-done.26), custom_call_target="tpu_custom_call" | custom-call | flops 4000000000 | bytes 4984832 | tf_op jit(solution)/shard_map/pallas_call | solution.py:262
  405.3 8.4 %shard_map.105 = (f32[512,512]{1,0:T(8,128)}, f32[512,128]{1,0:T(8,128)}, f32[512,512]{1,0:T(8,128)}) custom-call(s32[1]{0:T(128)} %bitcast.13.odd, f32[256,256]{1,0:T(8,128)} %get-tuple-element.231.ma, f32[256,256]{1,0:T(8,128)} %get-tuple-element.232.mb, f32[256,256]{1,0:T(8,128)} %get-tuple-element.233.u, f32[8,128]{1,0:T(8,128)} %get-tuple-element.234.logs, ...), custom_call_target="tpu_custom_call" | custom-call | flops 3000000000 | bytes 6295556 | tf_op jit(solution)/shard_map/pallas_call | solution.py:262
  417.8 22.0 %shard_map.106 = (f32[256,256]{1,0:T(8,128)}, f32[256,256]{1,0:T(8,128)}, f32[256,256]{1,0:T(8,128)}, f32[8,128]{1,0:T(8,128)}, f32[512,512]{1,0:T(8,128)}) custom-call(f32[512,512]{1,0:T(8,128)} %get-tuple-element.230.q.refs_0_, f32[512,512]{1,0:T(8,128)} %copy-done.44, f32[512,512]{1,0:T(8,128)} %collective-permute-done.41.refs_2_, ...), custom_call_target="tpu_custom_call" | custom-call | flops 4000000000 | bytes 6033408 | tf_op jit(solution)/shard_map/pallas_call | solution.py:262
  439.8 6.2 %shard_map.107.own = f32[1,640]{1,0:T(1,128)} custom-call(f32[256,256]{1,0:T(8,128)} %get-tuple-element.238.refs_0_, f32[256,256]{1,0:T(8,128)} %get-tuple-element.239.refs_1_, f32[256,256]{1,0:T(8,128)} %get-tuple-element.240.refs_2_, f32[8,128]{1,0:T(8,128)} %get-tuple-element.241.refs_3_, f32[512,512]{1,0:T(8,128)} %get-tuple-element.242.refs_4_, ...), custom_call_target="tpu_custom_call" | custom-call | flops 100000000 | bytes 1907712 | tf_op jit(solution)/shard_map/pallas_call | solution.py:262
  449.0 2.7 shard_map.108.own
  454.3 2.8 shard_map.109.own
  459.7 2.8 shard_map.110.own
  465.1 2.7 shard_map.111.own
  470.4 2.8 shard_map.112.own
  473.8 80.4 %collective-permute-start.54 = (f32[1,640]{1,0:T(1,128)}, f32[1,640]{1,0:T(1,128)S(1)}, u32[]{:S(2)}, u32[]{:S(2)}) collective-permute-start(f32[1,640]{1,0:T(1,128)} %shard_map.112.own), channel_id=1, source_target_pairs={{3,1},{5,7},{11,9},{13,15},{19,17},{21,23},{27,25},{29,31},{35,33}... | collective-permute-start | bytes 7688 | tf_op jit(solution)/shard_map/ppermute | solution.py:281
  555.4 2.8 shard_map.113.own
  558.1 12.2 %collective-permute-start.55 = (f32[1,640]{1,0:T(1,128)}, f32[1,640]{1,0:T(1,128)S(1)}, u32[]{:S(2)}, u32[]{:S(2)}) collective-permute-start(f32[1,640]{1,0:T(1,128)} %shard_map.113.own), channel_id=1, source_target_pairs={{1,2},{3,6},{7,4},{5,8},{9,10},{11,14},{15,12},{13,16},{17,18},{19... | collective-permute-start | bytes 7688 | tf_op jit(solution)/shard_map/ppermute | solution.py:281
  572.2 4.2 collective-permute-done.55.from_left
  577.0 2.8 shard_map.114
  580.9 4.3 all-to-all-start
  587.7 2.8 all-to-all-done
  (221 shorter events, 78.6 us)
Async XLA Ops:
  2.9 29.4 %collective-permute-start = (f32[576,128]{1,0:T(8,128)S(1)}, f32[576,128]{1,0:T(8,128)S(1)}, u32[]{:S(2)}, u32[]{:S(2)}) collective-permute-start(f32[576,128]{1,0:T(8,128)S(1)} %pad_maximum_fusion.1), channel_id=1, source_target_pairs={{0,1},{1,2},{2,3},{3,0},{4,5},{5,6},{6,7},{7,4},{8,9},{9,10},{10,1... | collective-permute-start | bytes 884744 | tf_op jit(solution)/shard_map/ppermute | solution.py:306
  12.6 19.7 %collective-permute-start.1 = (f32[576,128]{1,0:T(8,128)S(1)}, f32[576,128]{1,0:T(8,128)S(1)}, u32[]{:S(2)}, u32[]{:S(2)}) collective-permute-start(f32[576,128]{1,0:T(8,128)S(1)} %pad_maximum_fusion.2), channel_id=1, source_target_pairs={{0,2},{1,3},{2,0},{3,1},{4,6},{5,7},{6,4},{7,5},{8,10},{9,11},{10,... | collective-permute-start | bytes 884744 | tf_op jit(solution)/shard_map/ppermute | solution.py:306
  21.6 17.9 %collective-permute-start.2 = (f32[576,128]{1,0:T(8,128)S(1)}, f32[576,128]{1,0:T(8,128)S(1)}, u32[]{:S(2)}, u32[]{:S(2)}) collective-permute-start(f32[576,128]{1,0:T(8,128)S(1)} %pad_maximum_fusion.3), channel_id=1, source_target_pairs={{0,3},{1,0},{2,1},{3,2},{4,7},{5,4},{6,5},{7,6},{8,11},{9,8},{10,9... | collective-permute-start | bytes 884744 | tf_op jit(solution)/shard_map/ppermute | solution.py:306
  40.2 43.3 %collective-permute-start.3 = (f32[2,512,128]{2,1,0:T(8,128)S(1)}, f32[2,512,128]{2,1,0:T(8,128)S(1)}, u32[]{:S(2)}, u32[]{:S(2)}) collective-permute-start(f32[2,512,128]{2,1,0:T(8,128)S(1)} %get-tuple-element.143), channel_id=1, source_target_pairs={{1,2},{3,0},{5,6},{7,4},{9,10},{11,8},{13,14},{15,12},{17,18},{19,... | collective-permute-start | bytes 1572872 | tf_op jit(solution)/shard_map/ppermute | solution.py:311
  49.5 33.9 %collective-permute-start.4 = (f32[2,512,128]{2,1,0:T(8,128)S(1)}, f32[2,512,128]{2,1,0:T(8,128)S(1)}, u32[]{:S(2)}, u32[]{:S(2)}) collective-permute-start(f32[2,512,128]{2,1,0:T(8,128)S(1)} %get-tuple-element.144), channel_id=1, source_target_pairs={{0,2},{2,0},{4,6},{6,4},{8,10},{10,8},{12,14},{14,12},{16,18},{18,... | collective-permute-start | bytes 1572872 | tf_op jit(solution)/shard_map/ppermute | solution.py:311
  60.4 23.1 %collective-permute-start.5 = (f32[2,512,128]{2,1,0:T(8,128)S(1)}, f32[2,512,128]{2,1,0:T(8,128)S(1)}, u32[]{:S(2)}, u32[]{:S(2)}) collective-permute-start(f32[2,512,128]{2,1,0:T(8,128)S(1)} %get-tuple-element.145), channel_id=1, source_target_pairs={{1,0},{3,2},{5,4},{7,6},{9,8},{11,10},{13,12},{15,14},{17,16},{19,... | collective-permute-start | bytes 1572872 | tf_op jit(solution)/shard_map/ppermute | solution.py:311
  96.8 17.2 %collective-permute-start.6 = (f32[512,512]{1,0:T(8,128)}, f32[512,512]{1,0:T(8,128)S(1)}, u32[]{:S(2)}, u32[]{:S(2)}) collective-permute-start(f32[512,512]{1,0:T(8,128)} %get-tuple-element.152), channel_id=1, source_target_pairs={{0,1},{6,7},{8,9},{14,15},{16,17},{22,23},{24,25},{30,31},{32,33},... | collective-permute-start | bytes 3145736 | tf_op jit(solution)/shard_map/ppermute | solution.py:281
  101.5 12.6 %collective-permute-start.7 = (f32[512,512]{1,0:T(8,128)}, f32[512,512]{1,0:T(8,128)S(1)}, u32[]{:S(2)}, u32[]{:S(2)}) collective-permute-start(f32[512,512]{1,0:T(8,128)} %get-tuple-element.152), channel_id=1, source_target_pairs={{2,1},{4,7},{10,9},{12,15},{18,17},{20,23},{26,25},{28,31},{34,33}... | collective-permute-start | bytes 3145736 | tf_op jit(solution)/shard_map/ppermute | solution.py:281
  115.0 40.6 %collective-permute-start.8 = (f32[512,512]{1,0:T(8,128)}, f32[512,512]{1,0:T(8,128)S(1)}, u32[]{:S(2)}, u32[]{:S(2)}) collective-permute-start(f32[512,512]{1,0:T(8,128)} %get-tuple-element.159), channel_id=1, source_target_pairs={{0,1},{6,7},{8,9},{14,15},{16,17},{22,23},{24,25},{30,31},{32,33},... | collective-permute-start | bytes 3145736 | tf_op jit(solution)/shard_map/ppermute | solution.py:281
  120.6 35.0 %collective-permute-start.9 = (f32[512,512]{1,0:T(8,128)}, f32[512,512]{1,0:T(8,128)S(1)}, u32[]{:S(2)}, u32[]{:S(2)}) collective-permute-start(f32[512,512]{1,0:T(8,128)} %get-tuple-element.159), channel_id=1, source_target_pairs={{2,1},{4,7},{10,9},{12,15},{18,17},{20,23},{26,25},{28,31},{34,33}... | collective-permute-start | bytes 3145736 | tf_op jit(solution)/shard_map/ppermute | solution.py:281
  121.4 45.6 %collective-permute-start.10 = (f32[512,512]{1,0:T(8,128)}, f32[512,512]{1,0:T(8,128)}, u32[]{:S(2)}, u32[]{:S(2)}) collective-permute-start(f32[512,512]{1,0:T(8,128)} %get-tuple-element.163), channel_id=1, source_target_pairs={{6,3},{8,5},{14,11},{16,13},{22,19},{24,21},{30,27},{32,29},{38,35... | collective-permute-start | bytes 3145736 | tf_op jit(solution)/shard_map/ppermute | solution.py:281
  123.7 43.4 %collective-permute-start.11 = (f32[512,512]{1,0:T(8,128)}, f32[512,512]{1,0:T(8,128)}, u32[]{:S(2)}, u32[]{:S(2)}) collective-permute-start(f32[512,512]{1,0:T(8,128)} %get-tuple-element.163), channel_id=1, source_target_pairs={{2,3},{4,5},{10,11},{12,13},{18,19},{20,21},{26,27},{28,29},{34,35... | collective-permute-start | bytes 3145736 | tf_op jit(solution)/shard_map/ppermute | solution.py:281
  165.4 12.1 %collective-permute-start.12 = (f32[512,512]{1,0:T(8,128)}, f32[512,512]{1,0:T(8,128)S(1)}, u32[]{:S(2)}, u32[]{:S(2)}) collective-permute-start(f32[512,512]{1,0:T(8,128)} %get-tuple-element.167), channel_id=1, source_target_pairs={{1,3},{9,11},{17,19},{25,27},{33,35},{41,43},{49,51},{57,59},{65,6... | collective-permute-start | bytes 3145736 | tf_op jit(solution)/shard_map/ppermute | solution.py:281
  166.1 11.4 %collective-permute-start.13 = (f32[512,512]{1,0:T(8,128)}, f32[512,512]{1,0:T(8,128)S(1)}, u32[]{:S(2)}, u32[]{:S(2)}) collective-permute-start(f32[512,512]{1,0:T(8,128)} %get-tuple-element.167), channel_id=1, source_target_pairs={{7,3},{15,11},{23,19},{31,27},{39,35},{47,43},{55,51},{63,59},{71,... | collective-permute-start | bytes 3145736 | tf_op jit(solution)/shard_map/ppermute | solution.py:281
  178.5 26.7 %collective-permute-start.14 = (f32[512,512]{1,0:T(8,128)}, f32[512,512]{1,0:T(8,128)S(1)}, u32[]{:S(2)}, u32[]{:S(2)}) collective-permute-start(f32[512,512]{1,0:T(8,128)} %get-tuple-element.174), channel_id=1, source_target_pairs={{1,3},{9,11},{17,19},{25,27},{33,35},{41,43},{49,51},{57,59},{65,6... | collective-permute-start | bytes 3145736 | tf_op jit(solution)/shard_map/ppermute | solution.py:281
  179.2 26.0 %collective-permute-start.15 = (f32[512,512]{1,0:T(8,128)}, f32[512,512]{1,0:T(8,128)S(1)}, u32[]{:S(2)}, u32[]{:S(2)}) collective-permute-start(f32[512,512]{1,0:T(8,128)} %get-tuple-element.174), channel_id=1, source_target_pairs={{7,3},{15,11},{23,19},{31,27},{39,35},{47,43},{55,51},{63,59},{71,... | collective-permute-start | bytes 3145736 | tf_op jit(solution)/shard_map/ppermute | solution.py:281
  180.0 36.7 %collective-permute-start.16 = (f32[512,512]{1,0:T(8,128)}, f32[512,512]{1,0:T(8,128)}, u32[]{:S(2)}, u32[]{:S(2)}) collective-permute-start(f32[512,512]{1,0:T(8,128)} %get-tuple-element.178), channel_id=1, source_target_pairs={{9,5},{17,13},{25,21},{33,29},{41,37},{49,45},{57,53},{65,61},{73,... | collective-permute-start | bytes 3145736 | tf_op jit(solution)/shard_map/ppermute | solution.py:281
  181.7 35.0 %collective-permute-start.17 = (f32[512,512]{1,0:T(8,128)}, f32[512,512]{1,0:T(8,128)}, u32[]{:S(2)}, u32[]{:S(2)}) collective-permute-start(f32[512,512]{1,0:T(8,128)} %get-tuple-element.178), channel_id=1, source_target_pairs={{7,5},{15,13},{23,21},{31,29},{39,37},{47,45},{55,53},{63,61},{71,... | collective-permute-start | bytes 3145736 | tf_op jit(solution)/shard_map/ppermute | solution.py:281
  215.0 12.2 %collective-permute-start.18 = (f32[512,512]{1,0:T(8,128)}, f32[512,512]{1,0:T(8,128)S(1)}, u32[]{:S(2)}, u32[]{:S(2)}) collective-permute-start(f32[512,512]{1,0:T(8,128)} %get-tuple-element.182), channel_id=1, source_target_pairs={{3,5},{19,21},{35,37},{51,53},{67,69},{83,85},{99,101},{115,117}} | collective-permute-start | bytes 3145736 | tf_op jit(solution)/shard_map/ppermute | solution.py:281
  215.7 11.5 %collective-permute-start.19 = (f32[512,512]{1,0:T(8,128)}, f32[512,512]{1,0:T(8,128)S(1)}, u32[]{:S(2)}, u32[]{:S(2)}) collective-permute-start(f32[512,512]{1,0:T(8,128)} %get-tuple-element.182), channel_id=1, source_target_pairs={{11,5},{27,21},{43,37},{59,53},{75,69},{91,85},{107,101},{123,117}} | collective-permute-start | bytes 3145736 | tf_op jit(solution)/shard_map/ppermute | solution.py:281
  228.2 27.0 %collective-permute-start.20 = (f32[512,512]{1,0:T(8,128)}, f32[512,512]{1,0:T(8,128)S(1)}, u32[]{:S(2)}, u32[]{:S(2)}) collective-permute-start(f32[512,512]{1,0:T(8,128)} %get-tuple-element.189), channel_id=1, source_target_pairs={{3,5},{19,21},{35,37},{51,53},{67,69},{83,85},{99,101},{115,117}} | collective-permute-start | bytes 3145736 | tf_op jit(solution)/shard_map/ppermute | solution.py:281
  228.9 26.3 %collective-permute-start.21 = (f32[512,512]{1,0:T(8,128)}, f32[512,512]{1,0:T(8,128)S(1)}, u32[]{:S(2)}, u32[]{:S(2)}) collective-permute-start(f32[512,512]{1,0:T(8,128)} %get-tuple-element.189), channel_id=1, source_target_pairs={{11,5},{27,21},{43,37},{59,53},{75,69},{91,85},{107,101},{123,117}} | collective-permute-start | bytes 3145736 | tf_op jit(solution)/shard_map/ppermute | solution.py:281
  229.7 36.9 %collective-permute-start.22 = (f32[512,512]{1,0:T(8,128)}, f32[512,512]{1,0:T(8,128)}, u32[]{:S(2)}, u32[]{:S(2)}) collective-permute-start(f32[512,512]{1,0:T(8,128)} %get-tuple-element.193), channel_id=1, source_target_pairs={{19,13},{35,29},{51,45},{67,61},{83,77},{99,93},{115,109}} | collective-permute-start | bytes 3145736 | tf_op jit(solution)/shard_map/ppermute | solution.py:281
  231.3 35.2 %collective-permute-start.23 = (f32[512,512]{1,0:T(8,128)}, f32[512,512]{1,0:T(8,128)}, u32[]{:S(2)}, u32[]{:S(2)}) collective-permute-start(f32[512,512]{1,0:T(8,128)} %get-tuple-element.193), channel_id=1, source_target_pairs={{11,13},{27,29},{43,45},{59,61},{75,77},{91,93},{107,109},{123,125}} | collective-permute-start | bytes 3145736 | tf_op jit(solution)/shard_map/ppermute | solution.py:281
  264.9 12.1 %collective-permute-start.24 = (f32[512,512]{1,0:T(8,128)}, f32[512,512]{1,0:T(8,128)S(1)}, u32[]{:S(2)}, u32[]{:S(2)}) collective-permute-start(f32[512,512]{1,0:T(8,128)} %get-tuple-element.197), channel_id=1, source_target_pairs={{5,13},{37,45},{69,77},{101,109}} | collective-permute-start | bytes 3145736 | tf_op jit(solution)/shard_map/ppermute | solution.py:281
  265.7 11.4 %collective-permute-start.25 = (f32[512,512]{1,0:T(8,128)}, f32[512,512]{1,0:T(8,128)S(1)}, u32[]{:S(2)}, u32[]{:S(2)}) collective-permute-start(f32[512,512]{1,0:T(8,128)} %get-tuple-element.197), channel_id=1, source_target_pairs={{21,13},{53,45},{85,77},{117,109}} | collective-permute-start | bytes 3145736 | tf_op jit(solution)/shard_map/ppermute | solution.py:281
  278.1 26.6 %collective-permute-start.26 = (f32[512,512]{1,0:T(8,128)}, f32[512,512]{1,0:T(8,128)S(1)}, u32[]{:S(2)}, u32[]{:S(2)}) collective-permute-start(f32[512,512]{1,0:T(8,128)} %get-tuple-element.204), channel_id=1, source_target_pairs={{5,13},{37,45},{69,77},{101,109}} | collective-permute-start | bytes 3145736 | tf_op jit(solution)/shard_map/ppermute | solution.py:281
  278.9 25.9 %collective-permute-start.27 = (f32[512,512]{1,0:T(8,128)}, f32[512,512]{1,0:T(8,128)S(1)}, u32[]{:S(2)}, u32[]{:S(2)}) collective-permute-start(f32[512,512]{1,0:T(8,128)} %get-tuple-element.204), channel_id=1, source_target_pairs={{21,13},{53,45},{85,77},{117,109}} | collective-permute-start | bytes 3145736 | tf_op jit(solution)/shard_map/ppermute | solution.py:281
  279.6 36.6 %collective-permute-start.28 = (f32[512,512]{1,0:T(8,128)}, f32[512,512]{1,0:T(8,128)}, u32[]{:S(2)}, u32[]{:S(2)}) collective-permute-start(f32[512,512]{1,0:T(8,128)} %get-tuple-element.208), channel_id=1, source_target_pairs={{37,29},{69,61},{101,93}} | collective-permute-start | bytes 3145736 | tf_op jit(solution)/shard_map/ppermute | solution.py:281
  281.3 34.9 %collective-permute-start.29 = (f32[512,512]{1,0:T(8,128)}, f32[512,512]{1,0:T(8,128)}, u32[]{:S(2)}, u32[]{:S(2)}) collective-permute-start(f32[512,512]{1,0:T(8,128)} %get-tuple-element.208), channel_id=1, source_target_pairs={{21,29},{53,61},{85,93},{117,125}} | collective-permute-start | bytes 3145736 | tf_op jit(solution)/shard_map/ppermute | solution.py:281
  314.5 12.3 %collective-permute-start.30 = (f32[512,512]{1,0:T(8,128)}, f32[512,512]{1,0:T(8,128)S(1)}, u32[]{:S(2)}, u32[]{:S(2)}) collective-permute-start(f32[512,512]{1,0:T(8,128)} %get-tuple-element.212), channel_id=1, source_target_pairs={{13,29},{77,93}} | collective-permute-start | bytes 3145736 | tf_op jit(solution)/shard_map/ppermute | solution.py:281
  315.2 11.6 %collective-permute-start.31 = (f32[512,512]{1,0:T(8,128)}, f32[512,512]{1,0:T(8,128)S(1)}, u32[]{:S(2)}, u32[]{:S(2)}) collective-permute-start(f32[512,512]{1,0:T(8,128)} %get-tuple-element.212), channel_id=1, source_target_pairs={{45,29},{109,93}} | collective-permute-start | bytes 3145736 | tf_op jit(solution)/shard_map/ppermute | solution.py:281
  327.8 27.0 %collective-permute-start.32 = (f32[512,512]{1,0:T(8,128)}, f32[512,512]{1,0:T(8,128)S(1)}, u32[]{:S(2)}, u32[]{:S(2)}) collective-permute-start(f32[512,512]{1,0:T(8,128)} %get-tuple-element.219), channel_id=1, source_target_pairs={{13,29},{77,93}} | collective-permute-start | bytes 3145736 | tf_op jit(solution)/shard_map/ppermute | solution.py:281
  328.5 26.3 %collective-permute-start.33 = (f32[512,512]{1,0:T(8,128)}, f32[512,512]{1,0:T(8,128)S(1)}, u32[]{:S(2)}, u32[]{:S(2)}) collective-permute-start(f32[512,512]{1,0:T(8,128)} %get-tuple-element.219), channel_id=1, source_target_pairs={{45,29},{109,93}} | collective-permute-start | bytes 3145736 | tf_op jit(solution)/shard_map/ppermute | solution.py:281
  329.3 36.9 %collective-permute-start.34 = (f32[512,512]{1,0:T(8,128)}, f32[512,512]{1,0:T(8,128)}, u32[]{:S(2)}, u32[]{:S(2)}) collective-permute-start(f32[512,512]{1,0:T(8,128)} %get-tuple-element.223), channel_id=1, source_target_pairs={{77,61}} | collective-permute-start | bytes 3145736 | tf_op jit(solution)/shard_map/ppermute | solution.py:281
  331.0 35.2 %collective-permute-start.35 = (f32[512,512]{1,0:T(8,128)}, f32[512,512]{1,0:T(8,128)}, u32[]{:S(2)}, u32[]{:S(2)}) collective-permute-start(f32[512,512]{1,0:T(8,128)} %get-tuple-element.223), channel_id=1, source_target_pairs={{45,61},{109,125}} | collective-permute-start | bytes 3145736 | tf_op jit(solution)/shard_map/ppermute | solution.py:281
  364.6 12.2 %collective-permute-start.36 = (f32[512,512]{1,0:T(8,128)}, f32[512,512]{1,0:T(8,128)S(1)}, u32[]{:S(2)}, u32[]{:S(2)}) collective-permute-start(f32[512,512]{1,0:T(8,128)} %get-tuple-element.227), channel_id=1, source_target_pairs={{29,61}} | collective-permute-start | bytes 3145736 | tf_op jit(solution)/shard_map/ppermute | solution.py:281
  365.3 11.4 %collective-permute-start.37 = (f32[512,512]{1,0:T(8,128)}, f32[512,512]{1,0:T(8,128)S(1)}, u32[]{:S(2)}, u32[]{:S(2)}) collective-permute-start(f32[512,512]{1,0:T(8,128)} %get-tuple-element.227), channel_id=1, source_target_pairs={{93,61}} | collective-permute-start | bytes 3145736 | tf_op jit(solution)/shard_map/ppermute | solution.py:281
  376.8 27.6 %collective-permute-start.38 = (f32[512,512]{1,0:T(8,128)}, f32[512,512]{1,0:T(8,128)S(1)}, u32[]{:S(2)}, u32[]{:S(2)}) collective-permute-start(f32[512,512]{1,0:T(8,128)} %get-tuple-element.235), channel_id=1, source_target_pairs={{29,61}} | collective-permute-start | bytes 3145736 | tf_op jit(solution)/shard_map/ppermute | solution.py:281
  377.5 26.8 %collective-permute-start.39 = (f32[512,512]{1,0:T(8,128)}, f32[512,512]{1,0:T(8,128)}, u32[]{:S(2)}, u32[]{:S(2)}) collective-permute-start(f32[512,512]{1,0:T(8,128)} %get-tuple-element.235), channel_id=1, source_target_pairs={{93,61}} | collective-permute-start | bytes 3145736 | tf_op jit(solution)/shard_map/ppermute | solution.py:281
  379.2 37.6 %collective-permute-start.41 = (f32[512,512]{1,0:T(8,128)}, f32[512,512]{1,0:T(8,128)}, u32[]{:S(2)}, u32[]{:S(2)}) collective-permute-start(f32[512,512]{1,0:T(8,128)} %get-tuple-element.237), channel_id=1, source_target_pairs={} | collective-permute-start | bytes 3145736 | tf_op jit(solution)/shard_map/ppermute | solution.py:281
  380.8 36.0 %collective-permute-start.42 = (f32[512,512]{1,0:T(8,128)}, f32[512,512]{1,0:T(8,128)}, u32[]{:S(2)}, u32[]{:S(2)}) collective-permute-start(f32[512,512]{1,0:T(8,128)} %get-tuple-element.237), channel_id=1, source_target_pairs={{93,125}} | collective-permute-start | bytes 3145736 | tf_op jit(solution)/shard_map/ppermute | solution.py:281
  413.7 3.0 collective-permute-start.40
  473.1 81.6 %collective-permute-start.53 = (f32[1,640]{1,0:T(1,128)}, f32[1,640]{1,0:T(1,128)S(1)}, u32[]{:S(2)}, u32[]{:S(2)}) collective-permute-start(f32[1,640]{1,0:T(1,128)} %shard_map.112.own), channel_id=1, source_target_pairs={{3,7},{5,9},{11,15},{13,17},{19,23},{21,25},{27,31},{29,33},{35,39... | collective-permute-start | bytes 7688 | tf_op jit(solution)/shard_map/ppermute | solution.py:281
  473.8 81.0 %collective-permute-start.54 = (f32[1,640]{1,0:T(1,128)}, f32[1,640]{1,0:T(1,128)S(1)}, u32[]{:S(2)}, u32[]{:S(2)}) collective-permute-start(f32[1,640]{1,0:T(1,128)} %shard_map.112.own), channel_id=1, source_target_pairs={{3,1},{5,7},{11,9},{13,15},{19,17},{21,23},{27,25},{29,31},{35,33}... | collective-permute-start | bytes 7688 | tf_op jit(solution)/shard_map/ppermute | solution.py:281
  558.1 18.2 %collective-permute-start.55 = (f32[1,640]{1,0:T(1,128)}, f32[1,640]{1,0:T(1,128)S(1)}, u32[]{:S(2)}, u32[]{:S(2)}) collective-permute-start(f32[1,640]{1,0:T(1,128)} %shard_map.113.own), channel_id=1, source_target_pairs={{1,2},{3,6},{7,4},{5,8},{9,10},{11,14},{15,12},{13,16},{17,18},{19... | collective-permute-start | bytes 7688 | tf_op jit(solution)/shard_map/ppermute | solution.py:281
  570.3 6.1 %collective-permute-start.56 = (f32[1,640]{1,0:T(1,128)}, f32[1,640]{1,0:T(1,128)S(1)}, u32[]{:S(2)}, u32[]{:S(2)}) collective-permute-start(f32[1,640]{1,0:T(1,128)} %shard_map.113.own), channel_id=1, source_target_pairs={{1,0},{3,2},{7,6},{5,4},{9,8},{11,10},{15,14},{13,12},{17,16},{19,... | collective-permute-start | bytes 7688 | tf_op jit(solution)/shard_map/ppermute | solution.py:281
  580.9 9.5 %all-to-all-start = ((f32[1,4,128]{2,0,1:T(1,128)}), f32[1,4,128]{2,0,1:T(1,128)S(1)}, u32[]{:S(2)}, u32[]{:S(2)}) async-start(f32[1,4,128]{2,0,1:T(1,128)} %slice_bitcast_fusion), calls=%async_computation | async-start | bytes 4096 | tf_op jit(solution)/shard_map/all_to_all | solution.py:388
  (59 other events, 195.7 us)

commit v3 on v2

--- a/solution.py
+++ b/solution.py
@@ -115,46 +115,42 @@
     return lax.fori_loop(0, 4, body, jnp.zeros((8, TILE), F32))
 
 
-def factor_first_kernel(place, own, one, two, three, rhs, ma, mb, u, logs, q_new, s, inv):
-    col, pos = place[0], place[1]
-    right = rhs[pl.ds(pos, 1), :]
-    for back, ref in enumerate((own, one, two, three)):
-        source = lax.rem(col - back + 4, 4)
-        o = pl.multiple_of(source * TILE, TILE)
-        s[:, pl.ds(o, TILE)] = ref[0:NODES, :]
+def factor_first_kernel(flags, got, rhs, ma, mb, u, logs, q_new, s, inv):
+    right = rhs[pl.ds(flags[2], 1), :]
+    for k in range(4):
+        s[:, k * TILE : (k + 1) * TILE] = got[k, 0:NODES, :]
     q_new[...] = s[...]
     q_new[TILE:HALF, 0:TILE] = jnp.zeros((TILE, TILE), F32)
     row = lax.broadcasted_iota(jnp.int32, (TILE - EFFECTS, TILE), 0)
-    for back, ref in enumerate((own, one, two, three)):
-        source = lax.rem(col - back + 4, 4)
-        part = jnp.zeros((1, TILE), F32)
-        for k in range(4):
-            part = jnp.where(source == k, right[:, k * TILE : (k + 1) * TILE], part)
-        rest = jnp.where(row == 0, jnp.broadcast_to(part, row.shape), 0.0)
-        edge = jnp.concatenate([ref[NODES : NODES + EFFECTS, :], rest], axis=0).T
-        o0 = pl.multiple_of(HALF + lax.rem(source, 2) * TILE, TILE)
-        o1 = pl.multiple_of((source // 2) * TILE, TILE)
-        q_new[pl.ds(o0, TILE), pl.ds(o1, TILE)] = edge
-    logs[...] = factor_body(s, inv, ma, mb, u)
-
-
-def couple_first_kernel(place, own, one, two, three, low, high):
-    col, keep = place[0], place[2]
-    for back, ref in enumerate((own, one, two, three)):
-        source = lax.rem(col - back + 4, 4)
-        o = pl.multiple_of(source * TILE, TILE)
-        high[:, pl.ds(o, TILE)] = ref[1]
-        low[pl.ds(o, TILE), :] = jnp.where(keep > 0, ref[0].T, 0.0)
-
-
-def factor_next_kernel(count, *refs):
+    for k in range(4):
+        part = jnp.broadcast_to(right[:, k * TILE : (k + 1) * TILE], row.shape)
+        rest = jnp.where(row == 0, part, 0.0)
+        edge = jnp.concatenate([got[k, NODES : NODES + EFFECTS, :], rest], axis=0).T
+        o0, o1 = HALF + (k % 2) * TILE, (k // 2) * TILE
+        q_new[o0 : o0 + TILE, o1 : o1 + TILE] = edge
+
+    @pl.when(flags[0] != 0)
+    def _():
+        logs[...] = factor_body(s, inv, ma, mb, u)
+
+
+def couple_first_kernel(flags, got, low, high):
+    for k in range(4):
+        high[:, k * TILE : (k + 1) * TILE] = got[k, 1]
+        low[k * TILE : (k + 1) * TILE, :] = jnp.where(flags[3] > 0, got[k, 0].T, 0.0)
+
+
+def factor_next_kernel(count, flags, *refs):
     parts, (ma, mb, u, logs, q_new, s, inv) = refs[:count], refs[count:]
     value = parts[0][...]
     for part in parts[1:]:
         value = value - part[...]
-    s[...] = value
     q_new[...] = value
-    logs[...] = factor_body(s, inv, ma, mb, u)
+
+    @pl.when(flags[0] != 0)
+    def _():
+        s[...] = q_new[...]
+        logs[...] = factor_body(s, inv, ma, mb, u)
 
 
 def solve_into(ma, mb, u, top, bottom, out):
@@ -181,23 +177,29 @@
     return sums + jnp.where((row == 65) & (lane == 65), log_sum, 0.0)
 
 
-def near_kernel(odd, ma, mb, u, logs, q, low, high, wn, ws, out):
-    flag = odd[0] != 0
-    pick = lambda rows: jnp.where(flag, low[rows, :], high[rows, :])
-    solve_into(ma, mb, u, q[HALF:NODES, 0:TILE], q[HALF:NODES, TILE:HALF], ws)
-    solve_into(ma, mb, u, pick(slice(0, HALF)), pick(slice(HALF, NODES)), wn)
-    packed_products(wn, ws, out, jnp.where(flag, 0.0, corner_sums(q, ws, logs)))
-
-
-def far_kernel(count, odd, ma, mb, u, logs, low, high, wn, ws, *refs):
+def near_kernel(flags, ma, mb, u, logs, q, low, high, wn, ws, out):
+    @pl.when(flags[0] != 0)
+    def _():
+        odd = flags[1] != 0
+        pick = lambda rows: jnp.where(odd, low[rows, :], high[rows, :])
+        solve_into(ma, mb, u, q[HALF:NODES, 0:TILE], q[HALF:NODES, TILE:HALF], ws)
+        solve_into(ma, mb, u, pick(slice(0, HALF)), pick(slice(HALF, NODES)), wn)
+        packed_products(wn, ws, out, jnp.where(odd, 0.0, corner_sums(q, ws, logs)))
+
+
+def far_kernel(count, flags, ma, mb, u, logs, low, high, wn, ws, *refs):
     parts, outs = refs[: 1 + count], refs[1 + count :]
     wf, new, out = outs[:3]
     q = parts[0]
-    flag = odd[0] != 0
-    pick = lambda rows: jnp.where(flag, high[rows, :], low[rows, :])
-    solve_into(ma, mb, u, pick(slice(0, HALF)), pick(slice(HALF, NODES)), wf)
-    new[...] = -mtm(wn[...], wf[...])
-    packed_products(wf, ws, out, jnp.where(flag, corner_sums(q, ws, logs), 0.0))
+
+    @pl.when(flags[0] != 0)
+    def _():
+        odd = flags[1] != 0
+        pick = lambda rows: jnp.where(odd, high[rows, :], low[rows, :])
+        solve_into(ma, mb, u, pick(slice(0, HALF)), pick(slice(HALF, NODES)), wf)
+        new[...] = -mtm(wn[...], wf[...])
+        packed_products(wf, ws, out, jnp.where(odd, corner_sums(q, ws, logs), 0.0))
+
     if count:
         value = q[...]
         for part in parts[1:]:
@@ -212,7 +214,13 @@
     return x_top, x_bottom
 
 
-def root_kernel(total, ma, mb, u, logs, q, tip, fixed, out, ws, inv):
+def root_kernel(total, flags, ma, mb, u, logs, q, tip, fixed, out, ws, inv):
+    @pl.when(flags[0] != 0)
+    def _():
+        root_body(total, ma, mb, u, logs, q, tip, fixed, out, ws, inv)
+
+
+def root_body(total, ma, mb, u, logs, q, tip, fixed, out, ws, inv):
     solve_into(ma, mb, u, q[HALF:NODES, 0:TILE], q[HALF:NODES, TILE:HALF], ws)
     sums = corner_sums(q, ws, logs)
     row = lax.broadcasted_iota(jnp.int32, (TILE, TILE), 0)
@@ -289,42 +297,36 @@
     col, shift = lax.axis_index("col"), 2 * (lax.axis_index("tm") % 2)
     pos = (col + shift) % cols
     t = lax.axis_index("tm") * cols + pos
-    place = jnp.stack([col, pos, (t > 0).astype(jnp.int32)]).astype(jnp.int32)
-
-    def diagonal_for(p):
-        return jnp.concatenate(
-            [
-                lax.dynamic_index_in_dim(blocks, p, 0, keepdims=False),
-                lax.dynamic_index_in_dim(arrow, p, 0, keepdims=False),
-            ],
-            axis=0,
-        )
-
-    got, wanted = [diagonal_for(pos)], [lax.dynamic_slice_in_dim(upper, pos, 2, 0)]
-    for d in (1, 2, 3):
-        pairs = [(c, (c + d) % cols) for c in range(cols)]
-        got.append(lax.ppermute(diagonal_for((pos + d) % cols), "col", pairs))
-        wanted.append(lax.dynamic_slice_in_dim(upper, (pos + d) % cols, 2, 0))
+    number = lambda *values: jnp.stack([jnp.asarray(v).astype(jnp.int32) for v in values])
+    leaves = lambda s: (t + 1) % (2 * s) == s
+    first = number(leaves(1), (t + 1) // 2 % 2, pos, t > 0)
+    sent = jnp.concatenate([blocks, arrow], axis=1)
+    sent = jnp.where(shift > 0, jnp.concatenate([sent[2:4], sent[0:2]], axis=0), sent)
+    got = lax.all_to_all(sent, "col", split_axis=0, concat_axis=0, tiled=True)
+    pairs = upper.reshape(2, 2, node_count, TILE)
+    pairs = jnp.where(shift > 0, pairs[::-1], pairs)
+    wanted = jnp.concatenate([pairs[:, None], jnp.zeros_like(pairs)[:, None]], axis=1)
+    wanted = wanted.reshape(4, 2, node_count, TILE)
     got, wanted = lax.optimization_barrier((got, wanted))
-    for d in (1, 2, 3):
-        pairs = [(c, (c + d) % cols) for c in range(cols) if (c + d) % 2 == 0]
-        wanted[d] = lax.ppermute(wanted[d], "col", pairs)
+    wanted = lax.all_to_all(wanted, "col", split_axis=0, concat_axis=0, tiled=True)
     big = shape(NODES, NODES)
     ma, mb, u, logs, q = call(
-        factor_first_kernel, (place, *got, rhs), FACTORS + (big,), WORK, scalars=1, flops=4 * 10**9
-    )
-    low, high = call(couple_first_kernel, (place, *wanted), (big, big), scalars=1, flops=10**6)
+        factor_first_kernel, (first, got, rhs), FACTORS + (big,), WORK, scalars=1, flops=4 * 10**9
+    )
+    low, high = call(couple_first_kernel, (first, wanted), (big, big), scalars=1, flops=10**6)
+    middle, upper_middle = count // 2 - 1, 3 * count // 4 - 1
+    top_pairs = [(middle, upper_middle), (count - 1, middle), (upper_middle, count - 1)]
     kept, late = [], ()
     level = 0
     while (1 << level) < count:
         s = 1 << level
         leaving = [(2 * k + 1) * s - 1 for k in range(count // (2 * s))]
         even, uneven = leaving[0::2], leaving[1::2]
-        odd = (((t + 1) // (2 * s)) % 2).astype(jnp.int32).reshape(1)
+        flags = number(leaves(s), (t + 1) // (2 * s) % 2)
         last = 2 * s == count
         wn, ws, near = call(
             near_kernel,
-            (odd, ma, mb, u, logs, q, low, high),
+            (flags, ma, mb, u, logs, q, low, high),
             (big, shape(NODES, TILE), big),
             scalars=1,
             flops=3 * 10**9,
@@ -338,7 +340,7 @@
             n = len(late)
             wf, new, far, *q_adjusted = call(
                 lambda *refs: far_kernel(n, *refs),
-                (odd, ma, mb, u, logs, low, high, wn, ws, q, *late),
+                (flags, ma, mb, u, logs, low, high, wn, ws, q, *late),
                 (big,) * (4 if n else 3),
                 scalars=1,
                 flops=4 * 10**9,
@@ -346,21 +348,20 @@
             q = q_adjusted[0] if n else q
             new, far, arrived = lax.optimization_barrier((new, far, arrived))
             parts = (q, *arrived)
-            late = (
-                moved(far, [(i, i - s) for i in even if i >= s]),
-                moved(far, [(i, i + s) for i in uneven]),
-            )
+            late = (moved(far, top_pairs if 4 * s == count else [(i, i + s) for i in uneven]),)
+            if any(i >= s for i in even):
+                late += (moved(far, [(i, i - s) for i in even if i >= s]),)
             low = moved(new, [(i, i + s) for i in even])
             high = moved(new, [(i, i - s) for i in uneven])
-        mine = ((t + 1) % (2 * s) == s).astype(jnp.int32).reshape(1)
-        flags = jnp.concatenate([mine, odd])
         kept.append((flags, s, (ma, mb, u, wn, wf, ws)))
         n_parts = len(parts)
+        active = number(t == count - 1 if last else leaves(2 * s))
         ma, mb, u, logs, q = call(
             lambda *refs: factor_next_kernel(n_parts, *refs),
-            parts,
+            (active, *parts),
             FACTORS + (big,),
             WORK,
+            scalars=1,
             flops=4 * 10**9,
         )
         level += 1
@@ -369,15 +370,21 @@
     total = float(count * node_count + effects)
     (state,) = call(
         lambda *refs: root_kernel(total, *refs),
-        (ma, mb, u, logs, q, whole_tip, whole_fixed),
+        (active, ma, mb, u, logs, q, whole_tip, whole_fixed),
         (shape(1, NODES + TILE),),
         ((NODES, TILE), (TILE, TILE)),
+        scalars=1,
         flops=10**8,
     )
     for flags, s, factors in reversed(kept):
         leaving = [(2 * k + 1) * s - 1 for k in range(count // (2 * s))]
-        from_left = moved(state, [(i - s, i) for i in leaving if i >= s])
-        from_right = moved(state, [(i + s, i) for i in leaving])
+        if 2 * s < count:
+            pairs = [(i - s, i) for i in leaving if i >= s]
+            from_left = moved(state, top_pairs if 4 * s == count else pairs)
+            from_right = moved(state, [(i + s, i) for i in leaving])
+        else:
+            from_left = jnp.zeros_like(state)
+            from_right = moved(state, top_pairs)
         (state,) = call(
             back_kernel,
             (flags, from_left, from_right, state) + factors,

time: 602 us -> 562 us (0.934)
  waiting for transfers between devices: 16.3 us -> 311 us
  Pallas kernels: 323 us -> 136 us
  starting transfers between devices: 214 us -> 65 us
    ppermute x51 -> x49, waiting for transfers between devices: 6.35 us -> 290 us  [moved(): lax.ppermute(x, AXES, [(device_of(i), device_of(j)) for i, j in pairs])]
    pallas_call x30, Pallas kernels: 323 us -> 136 us  [call(): pl.pallas_call(kernel, out_shape=tuple(outs), in_specs=[smem] * scalars +...]
    ppermute x51 -> x49, starting transfers between devices: 161 us -> 52.8 us  [moved(): lax.ppermute(x, AXES, [(device_of(i), device_of(j)) for i, j in pairs])]
    ppermute x6 -> x0, starting transfers between devices: 49.1 us -> none  [the longest x3 27.6 us: per_device(): got.append(lax.ppermute(diagonal_for((pos + d) % cols), 'col', pairs))]
    all_to_all x0 -> x2, waiting for transfers between devices: none -> 18 us  [the longest x1 15 us: per_device(): got = lax.all_to_all(sent, 'col', split_axis=0, concat_axis=0, tiled=True)]
    all_to_all x0 -> x2, starting transfers between devices: none -> 9.04 us  [the longest x1 5.44 us: per_device(): got = lax.all_to_all(sent, 'col', split_axis=0, concat_axis=0, tiled=True)]
    ppermute x6 -> x0, waiting for transfers between devices: 7.24 us -> none  [the longest x3 7.23 us: per_device(): got.append(lax.ppermute(diagonal_for((pos + d) % cols), 'col', pairs))]
    unnamed x98 -> x89, local copies, waits for them, and re-layouts: 21.2 us -> 20.7 us
  transfers between devices with their start and end apart: 58 -> 52, of which waited for: 4 -> 7; matrix products, arithmetic and copies ran while one was open for 2% -> 2% of each run, Pallas kernels for 45% -> 18%
where the time goes in v3:
time: 562 us; the launch traced here: 550 us
  waiting for transfers between devices  311 us (55%)
  Pallas kernels  136 us (24%)
  starting transfers between devices  65 us (12%)
  local copies, waits for them, and re-layouts  29 us (5%)
  other arithmetic  6.68 us (1%)
    ppermute x49, waiting for transfers between devices, moved(): lax.ppermute(x, AXES, [(device_of(i), device_of(j)) for i, j in pairs])  290 us
    pallas_call x30, Pallas kernels, call(): pl.pallas_call(kernel, out_shape=tuple(outs), in_specs=[smem] * scalars +...  136 us
    ppermute x49, starting transfers between devices, moved(): lax.ppermute(x, AXES, [(device_of(i), device_of(j)) for i, j in pairs])  52.8 us
    unnamed x89, local copies, waits for them, and re-layouts  20.7 us
    all_to_all x1, waiting for transfers between devices, per_device(): got = lax.all_to_all(sent, 'col', split_axis=0, concat_axis=0, tiled=True)  15 us
  transfers between devices with their start and end apart: 52, of which 7 were waited for; matrix products, arithmetic and copies ran while one was open for 2% of the time, Pallas kernels for 18%

profile of v3, /device:TPU:6, one launch (start us, length us, event | category | flops | bytes accessed | tf_op | source)
XLA Modules:
  0.0 550.5 jit_solution(16455425752626594995)
XLA Ops:
  3.2 5.4 all-to-all-start
  10.2 15.0 %all-to-all-done.got = f32[4,576,128]{2,1,0:T(8,128)S(1)} async-done(((f32[4,576,128]{2,1,0:T(8,128)}), f32[4,576,128]{2,1,0:T(8,128)S(1)}, u32[]{:S(2)}, u32[]{:S(2)}) %all-to-all-start) | async-done | bytes 1179680 | tf_op jit(solution)/shard_map/all_to_all | solution.py:305
  26.2 3.6 all-to-all-start.1
  31.1 21.1 %shard_map.85 = (f32[256,256]{1,0:T(8,128)}, f32[256,256]{1,0:T(8,128)}, f32[256,256]{1,0:T(8,128)}, f32[8,128]{1,0:T(8,128)}, f32[512,512]{1,0:T(8,128)}) custom-call(s32[4]{0:T(128)} %pad_add_fusion.7.flags, f32[4,576,128]{2,1,0:T(8,128)} %copy-done.1, f32[4,512]{1,0:T(4,128)} %rhs.2), custom_call_target="tpu_custom_call" | custom-call | flops 4000000000 | bytes 3026960 | tf_op jit(solution)/shard_map/pallas_call | solution.py:270
  52.2 3.1 all-to-all-done.1.got
  56.6 3.3 shard_map.86
  59.9 8.8 %shard_map.87 = (f32[512,512]{1,0:T(8,128)}, f32[512,128]{1,0:T(8,128)}, f32[512,512]{1,0:T(8,128)}) custom-call(s32[2]{0:T(128)} %pad_add_fusion.flags.refs_0_, f32[256,256]{1,0:T(8,128)} %get-tuple-element.129.ma.refs_1_, f32[256,256]{1,0:T(8,128)} %get-tuple-element.130.mb.refs_2_, f32[256,256]{1,0:T(8,128)} %get-tuple-element.131.u.refs_3_, ...), custom_call_target="tpu_custom_call" | custom-call | flops 3000000000 | bytes 6295560 | tf_op jit(solution)/shard_map/pallas_call | solution.py:270
  71.2 10.2 %shard_map.88 = (f32[512,512]{1,0:T(8,128)}, f32[512,512]{1,0:T(8,128)}, f32[512,512]{1,0:T(8,128)}) custom-call(s32[2]{0:T(128)} %pad_add_fusion.flags.refs_0_, f32[256,256]{1,0:T(8,128)} %get-tuple-element.129.ma.refs_1_, f32[256,256]{1,0:T(8,128)} %get-tuple-element.130.mb.refs_2_, f32[256,256]{1,0:T(8,128)} %get-tuple-element.131.u.refs_3_, ...), custom_call_target="tpu_custom_call" | custom-call | flops 4000000000 | bytes 8392712 | tf_op jit(solution)/shard_map/pallas_call | solution.py:270
  83.7 4.3 collective-permute-start.2
  91.0 2.2 collective-permute-start.5
  93.2 3.4 shard_map.89
  96.7 25.2 %collective-permute-done.2.low.refs_5_ = f32[512,512]{1,0:T(8,128)S(1)} collective-permute-done((f32[512,512]{1,0:T(8,128)}, f32[512,512]{1,0:T(8,128)S(1)}, u32[]{:S(2)}, u32[]{:S(2)}) %collective-permute-start.2) | collective-permute-done | bytes 1048608 | tf_op jit(solution)/shard_map/ppermute | solution.py:289
  123.2 3.7 shard_map.90
  128.4 5.2 shard_map.91
  136.7 1.9 collective-permute-start.10
  140.3 3.2 shard_map.92
  144.8 3.6 shard_map.93
  149.9 5.5 %shard_map.94 = (f32[512,512]{1,0:T(8,128)}, f32[512,512]{1,0:T(8,128)}, f32[512,512]{1,0:T(8,128)}, f32[512,512]{1,0:T(8,128)}) custom-call(s32[2]{0:T(128)} %pad_add_fusion.2.flags.refs_0_, f32[256,256]{1,0:T(8,128)} %get-tuple-element.158.ma.refs_1_, f32[256,256]{1,0:T(8,128)} %get-tuple-element.159.mb.refs_2_, f32[256,256]{1,0:T(8,128)} %get-tuple-element.160.u.refs_3_, ...), custom_call_target="tpu_custom_call" | custom-call | flops 4000000000 | bytes 11538440 | tf_op jit(solution)/shard_map/pallas_call | solution.py:270
  161.8 3.3 shard_map.95
  166.4 3.7 shard_map.96
  171.6 5.1 shard_map.97
  179.8 1.8 collective-permute-start.22
  181.6 1.7 collective-permute-start.23
  183.3 3.3 shard_map.98
  187.9 3.6 shard_map.99
  193.0 5.5 %shard_map.100 = (f32[512,512]{1,0:T(8,128)}, f32[512,512]{1,0:T(8,128)}, f32[512,512]{1,0:T(8,128)}, f32[512,512]{1,0:T(8,128)}) custom-call(s32[2]{0:T(128)} %pad_add_fusion.4.flags.refs_0_, f32[256,256]{1,0:T(8,128)} %get-tuple-element.188.ma.refs_1_, f32[256,256]{1,0:T(8,128)} %get-tuple-element.189.mb.refs_2_, f32[256,256]{1,0:T(8,128)} %get-tuple-element.190.u.refs_3_, ...), custom_call_target="tpu_custom_call" | custom-call | flops 4000000000 | bytes 11538440 | tf_op jit(solution)/shard_map/pallas_call | solution.py:270
  201.6 1.7 collective-permute-start.28
  203.3 1.6 collective-permute-start.29
  204.9 3.3 shard_map.101
  209.6 3.8 shard_map.102
  214.9 5.2 shard_map.103
  220.8 1.6 collective-permute-start.33
  223.1 1.8 collective-permute-start.35
  224.9 3.3 shard_map.104
  229.1 3.5 shard_map.105
  235.8 3.6 shard_map.106
  239.3 2.1 shard_map.107.own
  243.8 2.8 shard_map.108.own
  248.5 2.8 shard_map.109.own
  253.2 2.7 shard_map.110.own
  257.9 2.7 shard_map.111.own
  262.6 2.7 shard_map.112.own
  267.3 2.8 shard_map.113.own
  272.6 257.3 %collective-permute-done.47.from_left = f32[1,640]{1,0:T(1,128)S(1)} collective-permute-done((f32[1,640]{1,0:T(1,128)}, f32[1,640]{1,0:T(1,128)S(1)}, u32[]{:S(2)}, u32[]{:S(2)}) %collective-permute-start.47) | collective-permute-done | bytes 2592 | tf_op jit(solution)/shard_map/ppermute | solution.py:289
  529.9 6.5 %collective-permute-done.48.from_right = f32[1,640]{1,0:T(1,128)S(1)} collective-permute-done((f32[1,640]{1,0:T(1,128)}, f32[1,640]{1,0:T(1,128)S(1)}, u32[]{:S(2)}, u32[]{:S(2)}) %collective-permute-start.48) | collective-permute-done | bytes 2592 | tf_op jit(solution)/shard_map/ppermute | solution.py:289
  537.1 2.8 shard_map.114
  541.1 3.2 all-to-all-start.2
  546.7 2.8 all-to-all-done.2
  (199 shorter events, 70.9 us)
Async XLA Ops:
  3.2 21.9 %all-to-all-start = ((f32[4,576,128]{2,1,0:T(8,128)}), f32[4,576,128]{2,1,0:T(8,128)S(1)}, u32[]{:S(2)}, u32[]{:S(2)}) async-start(f32[4,576,128]{2,1,0:T(8,128)} %maximum_select_fusion), calls=%async_computation | async-start | bytes 2359296 | tf_op jit(solution)/shard_map/all_to_all | solution.py:305
  26.2 29.1 %all-to-all-start.1 = ((f32[4,2,512,128]{3,2,1,0:T(8,128)}), f32[4,2,512,128]{3,2,1,0:T(8,128)S(1)}, u32[]{:S(2)}, u32[]{:S(2)}) async-start(f32[4,2,512,128]{3,2,1,0:T(8,128)} %bitcast.36), calls=%async_computation.1 | async-start | bytes 4194304 | tf_op jit(solution)/shard_map/all_to_all | solution.py:311
  68.7 13.9 %collective-permute-start = (f32[512,512]{1,0:T(8,128)}, f32[512,512]{1,0:T(8,128)S(1)}, u32[]{:S(2)}, u32[]{:S(2)}) collective-permute-start(f32[512,512]{1,0:T(8,128)} %get-tuple-element.140), channel_id=1, source_target_pairs={{0,1},{6,7},{8,9},{14,15},{16,17},{22,23},{24,25},{30,31},{32,33},... | collective-permute-start | bytes 3145736 | tf_op jit(solution)/shard_map/ppermute | solution.py:289
  70.0 12.6 %collective-permute-start.1 = (f32[512,512]{1,0:T(8,128)}, f32[512,512]{1,0:T(8,128)S(1)}, u32[]{:S(2)}, u32[]{:S(2)}) collective-permute-start(f32[512,512]{1,0:T(8,128)} %get-tuple-element.140), channel_id=1, source_target_pairs={{2,1},{4,7},{10,9},{12,15},{18,17},{20,23},{26,25},{28,31},{34,33}... | collective-permute-start | bytes 3145736 | tf_op jit(solution)/shard_map/ppermute | solution.py:289
  83.7 38.2 %collective-permute-start.2 = (f32[512,512]{1,0:T(8,128)}, f32[512,512]{1,0:T(8,128)S(1)}, u32[]{:S(2)}, u32[]{:S(2)}) collective-permute-start(f32[512,512]{1,0:T(8,128)} %get-tuple-element.147), channel_id=1, source_target_pairs={{0,1},{6,7},{8,9},{14,15},{16,17},{22,23},{24,25},{30,31},{32,33},... | collective-permute-start | bytes 3145736 | tf_op jit(solution)/shard_map/ppermute | solution.py:289
  88.0 33.8 %collective-permute-start.3 = (f32[512,512]{1,0:T(8,128)}, f32[512,512]{1,0:T(8,128)S(1)}, u32[]{:S(2)}, u32[]{:S(2)}) collective-permute-start(f32[512,512]{1,0:T(8,128)} %get-tuple-element.147), channel_id=1, source_target_pairs={{2,1},{4,7},{10,9},{12,15},{18,17},{20,23},{26,25},{28,31},{34,33}... | collective-permute-start | bytes 3145736 | tf_op jit(solution)/shard_map/ppermute | solution.py:289
  89.4 39.0 %collective-permute-start.4 = (f32[512,512]{1,0:T(8,128)}, f32[512,512]{1,0:T(8,128)}, u32[]{:S(2)}, u32[]{:S(2)}) collective-permute-start(f32[512,512]{1,0:T(8,128)} %get-tuple-element.151), channel_id=1, source_target_pairs={{2,3},{4,5},{10,11},{12,13},{18,19},{20,21},{26,27},{28,29},{34,35... | collective-permute-start | bytes 3145736 | tf_op jit(solution)/shard_map/ppermute | solution.py:289
  91.0 37.4 %collective-permute-start.5 = (f32[512,512]{1,0:T(8,128)}, f32[512,512]{1,0:T(8,128)}, u32[]{:S(2)}, u32[]{:S(2)}) collective-permute-start(f32[512,512]{1,0:T(8,128)} %get-tuple-element.151), channel_id=1, source_target_pairs={{6,3},{8,5},{14,11},{16,13},{22,19},{24,21},{30,27},{32,29},{38,35... | collective-permute-start | bytes 3145736 | tf_op jit(solution)/shard_map/ppermute | solution.py:289
  126.9 6.6 %collective-permute-start.6 = (f32[512,512]{1,0:T(8,128)}, f32[512,512]{1,0:T(8,128)S(1)}, u32[]{:S(2)}, u32[]{:S(2)}) collective-permute-start(f32[512,512]{1,0:T(8,128)} %get-tuple-element.155), channel_id=1, source_target_pairs={{1,3},{9,11},{17,19},{25,27},{33,35},{41,43},{49,51},{57,59},{65,6... | collective-permute-start | bytes 3145736 | tf_op jit(solution)/shard_map/ppermute | solution.py:289
  127.6 5.9 %collective-permute-start.7 = (f32[512,512]{1,0:T(8,128)}, f32[512,512]{1,0:T(8,128)S(1)}, u32[]{:S(2)}, u32[]{:S(2)}) collective-permute-start(f32[512,512]{1,0:T(8,128)} %get-tuple-element.155), channel_id=1, source_target_pairs={{7,3},{15,11},{23,19},{31,27},{39,35},{47,43},{55,51},{63,59},{71,... | collective-permute-start | bytes 3145736 | tf_op jit(solution)/shard_map/ppermute | solution.py:289
  134.5 9.0 %collective-permute-start.8 = (f32[512,512]{1,0:T(8,128)}, f32[512,512]{1,0:T(8,128)S(1)}, u32[]{:S(2)}, u32[]{:S(2)}) collective-permute-start(f32[512,512]{1,0:T(8,128)} %get-tuple-element.162), channel_id=1, source_target_pairs={{1,3},{9,11},{17,19},{25,27},{33,35},{41,43},{49,51},{57,59},{65,6... | collective-permute-start | bytes 3145736 | tf_op jit(solution)/shard_map/ppermute | solution.py:289
  135.3 8.2 %collective-permute-start.9 = (f32[512,512]{1,0:T(8,128)}, f32[512,512]{1,0:T(8,128)S(1)}, u32[]{:S(2)}, u32[]{:S(2)}) collective-permute-start(f32[512,512]{1,0:T(8,128)} %get-tuple-element.162), channel_id=1, source_target_pairs={{7,3},{15,11},{23,19},{31,27},{39,35},{47,43},{55,51},{63,59},{71,... | collective-permute-start | bytes 3145736 | tf_op jit(solution)/shard_map/ppermute | solution.py:289
  136.7 13.1 %collective-permute-start.10 = (f32[512,512]{1,0:T(8,128)}, f32[512,512]{1,0:T(8,128)}, u32[]{:S(2)}, u32[]{:S(2)}) collective-permute-start(f32[512,512]{1,0:T(8,128)} %get-tuple-element.166), channel_id=1, source_target_pairs={{7,5},{15,13},{23,21},{31,29},{39,37},{47,45},{55,53},{63,61},{71,... | collective-permute-start | bytes 3145736 | tf_op jit(solution)/shard_map/ppermute | solution.py:289
  138.6 11.2 %collective-permute-start.11 = (f32[512,512]{1,0:T(8,128)}, f32[512,512]{1,0:T(8,128)}, u32[]{:S(2)}, u32[]{:S(2)}) collective-permute-start(f32[512,512]{1,0:T(8,128)} %get-tuple-element.166), channel_id=1, source_target_pairs={{9,5},{17,13},{25,21},{33,29},{41,37},{49,45},{57,53},{65,61},{73,... | collective-permute-start | bytes 3145736 | tf_op jit(solution)/shard_map/ppermute | solution.py:289
  148.4 7.0 %collective-permute-start.12 = (f32[512,512]{1,0:T(8,128)}, f32[512,512]{1,0:T(8,128)S(1)}, u32[]{:S(2)}, u32[]{:S(2)}) collective-permute-start(f32[512,512]{1,0:T(8,128)} %get-tuple-element.170), channel_id=1, source_target_pairs={{3,5},{19,21},{35,37},{51,53},{67,69},{83,85},{99,101},{115,117}} | collective-permute-start | bytes 3145736 | tf_op jit(solution)/shard_map/ppermute | solution.py:289
  149.1 6.3 %collective-permute-start.13 = (f32[512,512]{1,0:T(8,128)}, f32[512,512]{1,0:T(8,128)S(1)}, u32[]{:S(2)}, u32[]{:S(2)}) collective-permute-start(f32[512,512]{1,0:T(8,128)} %get-tuple-element.170), channel_id=1, source_target_pairs={{11,5},{27,21},{43,37},{59,53},{75,69},{91,85},{107,101},{123,117}} | collective-permute-start | bytes 3145736 | tf_op jit(solution)/shard_map/ppermute | solution.py:289
  156.4 8.7 %collective-permute-start.14 = (f32[512,512]{1,0:T(8,128)}, f32[512,512]{1,0:T(8,128)S(1)}, u32[]{:S(2)}, u32[]{:S(2)}) collective-permute-start(f32[512,512]{1,0:T(8,128)} %get-tuple-element.177), channel_id=1, source_target_pairs={{3,5},{19,21},{35,37},{51,53},{67,69},{83,85},{99,101},{115,117}} | collective-permute-start | bytes 3145736 | tf_op jit(solution)/shard_map/ppermute | solution.py:289
  157.2 7.9 %collective-permute-start.15 = (f32[512,512]{1,0:T(8,128)}, f32[512,512]{1,0:T(8,128)S(1)}, u32[]{:S(2)}, u32[]{:S(2)}) collective-permute-start(f32[512,512]{1,0:T(8,128)} %get-tuple-element.177), channel_id=1, source_target_pairs={{11,5},{27,21},{43,37},{59,53},{75,69},{91,85},{107,101},{123,117}} | collective-permute-start | bytes 3145736 | tf_op jit(solution)/shard_map/ppermute | solution.py:289
  158.5 13.1 %collective-permute-start.16 = (f32[512,512]{1,0:T(8,128)}, f32[512,512]{1,0:T(8,128)}, u32[]{:S(2)}, u32[]{:S(2)}) collective-permute-start(f32[512,512]{1,0:T(8,128)} %get-tuple-element.181), channel_id=1, source_target_pairs={{11,13},{27,29},{43,45},{59,61},{75,77},{91,93},{107,109},{123,125}} | collective-permute-start | bytes 3145736 | tf_op jit(solution)/shard_map/ppermute | solution.py:289
  160.2 11.5 %collective-permute-start.17 = (f32[512,512]{1,0:T(8,128)}, f32[512,512]{1,0:T(8,128)}, u32[]{:S(2)}, u32[]{:S(2)}) collective-permute-start(f32[512,512]{1,0:T(8,128)} %get-tuple-element.181), channel_id=1, source_target_pairs={{19,13},{35,29},{51,45},{67,61},{83,77},{99,93},{115,109}} | collective-permute-start | bytes 3145736 | tf_op jit(solution)/shard_map/ppermute | solution.py:289
  170.1 6.6 %collective-permute-start.18 = (f32[512,512]{1,0:T(8,128)}, f32[512,512]{1,0:T(8,128)S(1)}, u32[]{:S(2)}, u32[]{:S(2)}) collective-permute-start(f32[512,512]{1,0:T(8,128)} %get-tuple-element.185), channel_id=1, source_target_pairs={{5,13},{37,45},{69,77},{101,109}} | collective-permute-start | bytes 3145736 | tf_op jit(solution)/shard_map/ppermute | solution.py:289
  170.9 5.9 %collective-permute-start.19 = (f32[512,512]{1,0:T(8,128)}, f32[512,512]{1,0:T(8,128)S(1)}, u32[]{:S(2)}, u32[]{:S(2)}) collective-permute-start(f32[512,512]{1,0:T(8,128)} %get-tuple-element.185), channel_id=1, source_target_pairs={{21,13},{53,45},{85,77},{117,109}} | collective-permute-start | bytes 3145736 | tf_op jit(solution)/shard_map/ppermute | solution.py:289
  177.7 8.9 %collective-permute-start.20 = (f32[512,512]{1,0:T(8,128)}, f32[512,512]{1,0:T(8,128)S(1)}, u32[]{:S(2)}, u32[]{:S(2)}) collective-permute-start(f32[512,512]{1,0:T(8,128)} %get-tuple-element.192), channel_id=1, source_target_pairs={{5,13},{37,45},{69,77},{101,109}} | collective-permute-start | bytes 3145736 | tf_op jit(solution)/shard_map/ppermute | solution.py:289
  178.5 8.1 %collective-permute-start.21 = (f32[512,512]{1,0:T(8,128)}, f32[512,512]{1,0:T(8,128)S(1)}, u32[]{:S(2)}, u32[]{:S(2)}) collective-permute-start(f32[512,512]{1,0:T(8,128)} %get-tuple-element.192), channel_id=1, source_target_pairs={{21,13},{53,45},{85,77},{117,109}} | collective-permute-start | bytes 3145736 | tf_op jit(solution)/shard_map/ppermute | solution.py:289
  179.8 13.1 %collective-permute-start.22 = (f32[512,512]{1,0:T(8,128)}, f32[512,512]{1,0:T(8,128)}, u32[]{:S(2)}, u32[]{:S(2)}) collective-permute-start(f32[512,512]{1,0:T(8,128)} %get-tuple-element.196), channel_id=1, source_target_pairs={{21,29},{53,61},{85,93},{117,125}} | collective-permute-start | bytes 3145736 | tf_op jit(solution)/shard_map/ppermute | solution.py:289
  181.6 11.3 %collective-permute-start.23 = (f32[512,512]{1,0:T(8,128)}, f32[512,512]{1,0:T(8,128)}, u32[]{:S(2)}, u32[]{:S(2)}) collective-permute-start(f32[512,512]{1,0:T(8,128)} %get-tuple-element.196), channel_id=1, source_target_pairs={{37,29},{69,61},{101,93}} | collective-permute-start | bytes 3145736 | tf_op jit(solution)/shard_map/ppermute | solution.py:289
  191.5 7.0 %collective-permute-start.24 = (f32[512,512]{1,0:T(8,128)}, f32[512,512]{1,0:T(8,128)S(1)}, u32[]{:S(2)}, u32[]{:S(2)}) collective-permute-start(f32[512,512]{1,0:T(8,128)} %get-tuple-element.200), channel_id=1, source_target_pairs={{13,29},{77,93}} | collective-permute-start | bytes 3145736 | tf_op jit(solution)/shard_map/ppermute | solution.py:289
  192.2 6.3 %collective-permute-start.25 = (f32[512,512]{1,0:T(8,128)}, f32[512,512]{1,0:T(8,128)S(1)}, u32[]{:S(2)}, u32[]{:S(2)}) collective-permute-start(f32[512,512]{1,0:T(8,128)} %get-tuple-element.200), channel_id=1, source_target_pairs={{45,29},{109,93}} | collective-permute-start | bytes 3145736 | tf_op jit(solution)/shard_map/ppermute | solution.py:289
  199.5 8.7 %collective-permute-start.26 = (f32[512,512]{1,0:T(8,128)}, f32[512,512]{1,0:T(8,128)S(1)}, u32[]{:S(2)}, u32[]{:S(2)}) collective-permute-start(f32[512,512]{1,0:T(8,128)} %get-tuple-element.207), channel_id=1, source_target_pairs={{13,29},{77,93}} | collective-permute-start | bytes 3145736 | tf_op jit(solution)/shard_map/ppermute | solution.py:289
  200.3 8.0 %collective-permute-start.27 = (f32[512,512]{1,0:T(8,128)}, f32[512,512]{1,0:T(8,128)S(1)}, u32[]{:S(2)}, u32[]{:S(2)}) collective-permute-start(f32[512,512]{1,0:T(8,128)} %get-tuple-element.207), channel_id=1, source_target_pairs={{45,29},{109,93}} | collective-permute-start | bytes 3145736 | tf_op jit(solution)/shard_map/ppermute | solution.py:289
  201.6 13.2 %collective-permute-start.28 = (f32[512,512]{1,0:T(8,128)}, f32[512,512]{1,0:T(8,128)}, u32[]{:S(2)}, u32[]{:S(2)}) collective-permute-start(f32[512,512]{1,0:T(8,128)} %get-tuple-element.211), channel_id=1, source_target_pairs={{45,61},{109,125}} | collective-permute-start | bytes 3145736 | tf_op jit(solution)/shard_map/ppermute | solution.py:289
  203.3 11.5 %collective-permute-start.29 = (f32[512,512]{1,0:T(8,128)}, f32[512,512]{1,0:T(8,128)}, u32[]{:S(2)}, u32[]{:S(2)}) collective-permute-start(f32[512,512]{1,0:T(8,128)} %get-tuple-element.211), channel_id=1, source_target_pairs={{77,61}} | collective-permute-start | bytes 3145736 | tf_op jit(solution)/shard_map/ppermute | solution.py:289
  213.4 6.7 %collective-permute-start.30 = (f32[512,512]{1,0:T(8,128)}, f32[512,512]{1,0:T(8,128)S(1)}, u32[]{:S(2)}, u32[]{:S(2)}) collective-permute-start(f32[512,512]{1,0:T(8,128)} %get-tuple-element.215), channel_id=1, source_target_pairs={{29,61}} | collective-permute-start | bytes 3145736 | tf_op jit(solution)/shard_map/ppermute | solution.py:289
  214.1 5.9 %collective-permute-start.31 = (f32[512,512]{1,0:T(8,128)}, f32[512,512]{1,0:T(8,128)S(1)}, u32[]{:S(2)}, u32[]{:S(2)}) collective-permute-start(f32[512,512]{1,0:T(8,128)} %get-tuple-element.215), channel_id=1, source_target_pairs={{93,61}} | collective-permute-start | bytes 3145736 | tf_op jit(solution)/shard_map/ppermute | solution.py:289
  220.1 8.1 %collective-permute-start.32 = (f32[512,512]{1,0:T(8,128)}, f32[512,512]{1,0:T(8,128)S(1)}, u32[]{:S(2)}, u32[]{:S(2)}) collective-permute-start(f32[512,512]{1,0:T(8,128)} %get-tuple-element.223), channel_id=1, source_target_pairs={{29,61}} | collective-permute-start | bytes 3145736 | tf_op jit(solution)/shard_map/ppermute | solution.py:289
  220.8 7.4 %collective-permute-start.33 = (f32[512,512]{1,0:T(8,128)}, f32[512,512]{1,0:T(8,128)}, u32[]{:S(2)}, u32[]{:S(2)}) collective-permute-start(f32[512,512]{1,0:T(8,128)} %get-tuple-element.223), channel_id=1, source_target_pairs={{93,61}} | collective-permute-start | bytes 3145736 | tf_op jit(solution)/shard_map/ppermute | solution.py:289
  223.1 11.7 %collective-permute-start.35 = (f32[512,512]{1,0:T(8,128)}, f32[512,512]{1,0:T(8,128)}, u32[]{:S(2)}, u32[]{:S(2)}) collective-permute-start(f32[512,512]{1,0:T(8,128)} %get-tuple-element.225), channel_id=1, source_target_pairs={{61,93},{125,61},{93,125}} | collective-permute-start | bytes 3145736 | tf_op jit(solution)/shard_map/ppermute | solution.py:289
  232.7 2.1 collective-permute-start.34
  246.6 1.3 collective-permute-start.37
  247.2 0.7 collective-permute-start.38
  251.3 1.3 collective-permute-start.39
  255.9 1.3 collective-permute-start.41
  260.6 1.3 collective-permute-start.43
  265.3 1.3 collective-permute-start.45
  266.0 0.7 collective-permute-start.46
  270.0 259.9 %collective-permute-start.47 = (f32[1,640]{1,0:T(1,128)}, f32[1,640]{1,0:T(1,128)S(1)}, u32[]{:S(2)}, u32[]{:S(2)}) collective-permute-start(f32[1,640]{1,0:T(1,128)} %shard_map.113.own), channel_id=1, source_target_pairs={{1,2},{3,6},{7,4},{5,8},{9,10},{11,14},{15,12},{13,16},{17,18},{19... | collective-permute-start | bytes 7688 | tf_op jit(solution)/shard_map/ppermute | solution.py:289
  271.3 265.2 %collective-permute-start.48 = (f32[1,640]{1,0:T(1,128)}, f32[1,640]{1,0:T(1,128)S(1)}, u32[]{:S(2)}, u32[]{:S(2)}) collective-permute-start(f32[1,640]{1,0:T(1,128)} %shard_map.113.own), channel_id=1, source_target_pairs={{1,0},{3,2},{7,6},{5,4},{9,8},{11,10},{15,14},{13,12},{17,16},{19,... | collective-permute-start | bytes 7688 | tf_op jit(solution)/shard_map/ppermute | solution.py:289
  541.1 8.4 %all-to-all-start.2 = ((f32[1,4,128]{2,0,1:T(1,128)}), f32[1,4,128]{2,0,1:T(1,128)S(1)}, u32[]{:S(2)}, u32[]{:S(2)}) async-start(f32[1,4,128]{2,0,1:T(1,128)} %slice_bitcast_fusion), calls=%async_computation.2 | async-start | bytes 4096 | tf_op jit(solution)/shard_map/all_to_all | solution.py:395
  (48 other events, 106.1 us)

commit v4 on v3

--- a/solution.py
+++ b/solution.py
@@ -11,6 +11,8 @@
 HALF = 256
 NODES = 512
 EFFECTS = 64
+UPPER = [(i, j) for i in range(4) for j in range(i, 4)]
+SQUARE, EDGE, WHOLE = 10 * TILE, 5 * TILE, 16 * TILE
 
 
 def mm(a, b):
@@ -115,19 +117,23 @@
     return lax.fori_loop(0, 4, body, jnp.zeros((8, TILE), F32))
 
 
-def factor_first_kernel(flags, got, rhs, ma, mb, u, logs, q_new, s, inv):
+def block_rows(index, base=0):
+    return slice(base + index * TILE, base + (index + 1) * TILE)
+
+
+def factor_first_kernel(flags, got, rhs, ma, mb, u, logs, q, s, inv):
     right = rhs[pl.ds(flags[2], 1), :]
     for k in range(4):
         s[:, k * TILE : (k + 1) * TILE] = got[k, 0:NODES, :]
-    q_new[...] = s[...]
-    q_new[TILE:HALF, 0:TILE] = jnp.zeros((TILE, TILE), F32)
+    for b, (i, j) in enumerate(UPPER):
+        q[block_rows(b), :] = got[j, block_rows(i), :]
     row = lax.broadcasted_iota(jnp.int32, (TILE - EFFECTS, TILE), 0)
     for k in range(4):
         part = jnp.broadcast_to(right[:, k * TILE : (k + 1) * TILE], row.shape)
         rest = jnp.where(row == 0, part, 0.0)
         edge = jnp.concatenate([got[k, NODES : NODES + EFFECTS, :], rest], axis=0).T
-        o0, o1 = HALF + (k % 2) * TILE, (k // 2) * TILE
-        q_new[o0 : o0 + TILE, o1 : o1 + TILE] = edge
+        q[block_rows(k, SQUARE), :] = edge
+    q[block_rows(4, SQUARE), :] = jnp.zeros((TILE, TILE), F32)
 
     @pl.when(flags[0] != 0)
     def _():
@@ -136,20 +142,25 @@
 
 def couple_first_kernel(flags, got, low, high):
     for k in range(4):
-        high[:, k * TILE : (k + 1) * TILE] = got[k, 1]
-        low[k * TILE : (k + 1) * TILE, :] = jnp.where(flags[3] > 0, got[k, 0].T, 0.0)
+        high[k * NODES : (k + 1) * NODES, :] = got[k, 1]
+        turned = jnp.where(flags[3] > 0, got[k, 0].T, 0.0)
+        for j in range(4):
+            o = j * NODES + k * TILE
+            low[o : o + TILE, :] = turned[:, j * TILE : (j + 1) * TILE]
+    for ref in (low, high):
+        ref[WHOLE : WHOLE + EDGE, :] = jnp.zeros((EDGE, TILE), F32)
 
 
 def factor_next_kernel(count, flags, *refs):
-    parts, (ma, mb, u, logs, q_new, s, inv) = refs[:count], refs[count:]
-    value = parts[0][...]
-    for part in parts[1:]:
-        value = value - part[...]
-    q_new[...] = value
-
-    @pl.when(flags[0] != 0)
-    def _():
-        s[...] = q_new[...]
+    parts, (ma, mb, u, logs, s, inv) = refs[:count], refs[count:]
+
+    @pl.when(flags[0] != 0)
+    def _():
+        for b, (i, j) in enumerate(UPPER):
+            value = parts[0][block_rows(b), :]
+            for part in parts[1:]:
+                value = value - part[block_rows(b), :]
+            s[block_rows(i), j * TILE : (j + 1) * TILE] = value
         logs[...] = factor_body(s, inv, ma, mb, u)
 
 
@@ -159,52 +170,82 @@
     out[HALF:NODES, :] = mm(mb[...], bottom - mtm(u[...], first))
 
 
-def packed_products(w, ws, out, corner):
-    whole, edge = w[...], ws[...]
-    out[0:HALF, :] = mtm(w[:, 0:HALF], whole)
-    out[HALF:NODES, HALF:NODES] = mtm(w[:, HALF:NODES], w[:, HALF:NODES])
-    crossed = mtm(whole, edge)
-    out[HALF:NODES, 0:TILE] = crossed[0:HALF]
-    out[HALF:NODES, TILE:HALF] = crossed[HALF:NODES]
-    out[TILE:HALF, 0:TILE] = corner
-
-
-def corner_sums(q, ws, logs):
+def square_products(w, out):
+    top = mtm(w[:, 0:HALF], w[...])
+    bottom = mtm(w[:, HALF:NODES], w[:, HALF:NODES])
+    for b, (i, j) in enumerate(UPPER):
+        rows, cols = block_rows(i % 2), slice(j * TILE, (j + 1) * TILE)
+        if i < 2:
+            out[block_rows(b), :] = top[rows, cols]
+        else:
+            out[block_rows(b), :] = bottom[rows, block_rows(j - 2)]
+
+
+def corner_sums(corner, ws, logs):
     row = lax.broadcasted_iota(jnp.int32, (TILE, TILE), 0)
     lane = lax.broadcasted_iota(jnp.int32, (TILE, TILE), 1)
     log_sum = jnp.sum(logs[...])
-    sums = mtm(ws[...], ws[...]) - q[TILE:HALF, 0:TILE]
+    sums = mtm(ws[...], ws[...]) - corner
     return sums + jnp.where((row == 65) & (lane == 65), log_sum, 0.0)
 
 
-def near_kernel(flags, ma, mb, u, logs, q, low, high, wn, ws, out):
+def solve_columns(ma, mb, u, flag, first, second, out):
+    def rows(o):
+        at = [slice(k * NODES + o, k * NODES + o + HALF) for k in range(4)]
+        return jnp.concatenate([jnp.where(flag, first[r, :], second[r, :]) for r in at], axis=1)
+
+    solve_into(ma, mb, u, rows(0), rows(HALF), out)
+
+
+def near_kernel(flags, ma, mb, u, low, high, wn, out):
+    @pl.when(flags[0] != 0)
+    def _():
+        solve_columns(ma, mb, u, flags[1] != 0, low, high, wn)
+        square_products(wn, out)
+
+
+def edge_part(parts, o, n):
+    value = parts[0][SQUARE + o : SQUARE + o + n, :]
+    for part, base in parts[1:]:
+        value = value - part[base + o : base + o + n, :]
+    return value
+
+
+def far_kernel(count, flags, ma, mb, u, logs, low, high, wn, *refs):
+    parts, outs = refs[: 1 + count], refs[1 + count :]
+    wf, ws, new, out = outs[:4]
+    q = parts[0]
+
     @pl.when(flags[0] != 0)
     def _():
         odd = flags[1] != 0
-        pick = lambda rows: jnp.where(odd, low[rows, :], high[rows, :])
-        solve_into(ma, mb, u, q[HALF:NODES, 0:TILE], q[HALF:NODES, TILE:HALF], ws)
-        solve_into(ma, mb, u, pick(slice(0, HALF)), pick(slice(HALF, NODES)), wn)
-        packed_products(wn, ws, out, jnp.where(odd, 0.0, corner_sums(q, ws, logs)))
-
-
-def far_kernel(count, flags, ma, mb, u, logs, low, high, wn, ws, *refs):
-    parts, outs = refs[: 1 + count], refs[1 + count :]
-    wf, new, out = outs[:3]
-    q = parts[0]
-
-    @pl.when(flags[0] != 0)
-    def _():
-        odd = flags[1] != 0
-        pick = lambda rows: jnp.where(odd, high[rows, :], low[rows, :])
-        solve_into(ma, mb, u, pick(slice(0, HALF)), pick(slice(HALF, NODES)), wf)
-        new[...] = -mtm(wn[...], wf[...])
-        packed_products(wf, ws, out, jnp.where(odd, corner_sums(q, ws, logs), 0.0))
+        edge = lambda o, n: edge_part((q, (low, WHOLE), (high, WHOLE)), o, n)
+        solve_columns(ma, mb, u, odd, high, low, wf)
+        product = -mtm(wn[...], wf[...])
+        for k in range(4):
+            new[k * NODES : (k + 1) * NODES, :] = product[:, k * TILE : (k + 1) * TILE]
+        solve_into(ma, mb, u, edge(0, HALF), edge(HALF, HALF), ws)
+        corner = corner_sums(edge(NODES, TILE), ws, logs)
+        new[WHOLE : WHOLE + NODES, :] = mtm(wn[...], ws[...])
+        new[WHOLE + NODES : WHOLE + EDGE, :] = jnp.where(odd, 0.0, corner)
+        square_products(wf, out)
+        out[SQUARE : SQUARE + NODES, :] = mtm(wf[...], ws[...])
+        out[SQUARE + NODES : SQUARE + EDGE, :] = jnp.where(odd, corner, 0.0)
 
     if count:
         value = q[...]
         for part in parts[1:]:
             value = value - part[...]
-        outs[3][...] = value
+        outs[4][...] = value
+
+
+def last_kernel(flags, ma, mb, u, logs, low, high, wn, q, ws, out):
+    @pl.when(flags[0] != 0)
+    def _():
+        edge = lambda o, n: edge_part((q, (low, WHOLE), (high, WHOLE)), o, n)
+        solve_into(ma, mb, u, edge(0, HALF), edge(HALF, HALF), ws)
+        out[0:NODES, :] = mtm(wn[...], ws[...])
+        out[NODES:EDGE, :] = corner_sums(edge(NODES, TILE), ws, logs)
 
 
 def back_solve(ma, mb, u, z_top, z_bottom):
@@ -214,15 +255,16 @@
     return x_top, x_bottom
 
 
-def root_kernel(total, flags, ma, mb, u, logs, q, tip, fixed, out, ws, inv):
-    @pl.when(flags[0] != 0)
-    def _():
-        root_body(total, ma, mb, u, logs, q, tip, fixed, out, ws, inv)
-
-
-def root_body(total, ma, mb, u, logs, q, tip, fixed, out, ws, inv):
-    solve_into(ma, mb, u, q[HALF:NODES, 0:TILE], q[HALF:NODES, TILE:HALF], ws)
-    sums = corner_sums(q, ws, logs)
+def root_kernel(total, count, flags, ma, mb, u, logs, tip, fixed, last, q, *refs):
+    @pl.when(flags[0] != 0)
+    def _():
+        parts = (q, (last, 0), *((part, SQUARE) for part in refs[:count]))
+        root_body(total, ma, mb, u, logs, parts, tip, fixed, *refs[count:])
+
+
+def root_body(total, ma, mb, u, logs, parts, tip, fixed, out, ws, inv):
+    solve_into(ma, mb, u, edge_part(parts, 0, HALF), edge_part(parts, HALF, HALF), ws)
+    sums = corner_sums(edge_part(parts, NODES, TILE), ws, logs)
     row = lax.broadcasted_iota(jnp.int32, (TILE, TILE), 0)
     lane = lax.broadcasted_iota(jnp.int32, (TILE, TILE), 1)
     inv[...] = tip[...] - jnp.where((row < 64) & (lane < 64), sums, 0.0)
@@ -309,11 +351,19 @@
     wanted = wanted.reshape(4, 2, node_count, TILE)
     got, wanted = lax.optimization_barrier((got, wanted))
     wanted = lax.all_to_all(wanted, "col", split_axis=0, concat_axis=0, tiled=True)
-    big = shape(NODES, NODES)
+    big, thin = shape(NODES, NODES), shape(NODES, TILE)
+    state_shape, coupled = shape(SQUARE + EDGE, TILE), shape(WHOLE + EDGE, TILE)
     ma, mb, u, logs, q = call(
-        factor_first_kernel, (first, got, rhs), FACTORS + (big,), WORK, scalars=1, flops=4 * 10**9
-    )
-    low, high = call(couple_first_kernel, (first, wanted), (big, big), scalars=1, flops=10**6)
+        factor_first_kernel,
+        (first, got, rhs),
+        FACTORS + (state_shape,),
+        WORK,
+        scalars=1,
+        flops=4 * 10**9,
+    )
+    low, high = call(
+        couple_first_kernel, (first, wanted), (coupled, coupled), scalars=1, flops=10**6
+    )
     middle, upper_middle = count // 2 - 1, 3 * count // 4 - 1
     top_pairs = [(middle, upper_middle), (count - 1, middle), (upper_middle, count - 1)]
     kept, late = [], ()
@@ -324,29 +374,38 @@
         even, uneven = leaving[0::2], leaving[1::2]
         flags = number(leaves(s), (t + 1) // (2 * s) % 2)
         last = 2 * s == count
-        wn, ws, near = call(
+        wn, near = call(
             near_kernel,
-            (flags, ma, mb, u, logs, q, low, high),
-            (big, shape(NODES, TILE), big),
+            (flags, ma, mb, u, low, high),
+            (big, shape(SQUARE, TILE)),
             scalars=1,
             flops=3 * 10**9,
         )
         arrived = [moved(near, [(i, i + s) for i in even])]
         if last:
             wf = jnp.zeros((NODES, NODES), F32)
+            ws, edge = call(
+                last_kernel,
+                (flags, ma, mb, u, logs, low, high, wn, q),
+                (thin, shape(EDGE, TILE)),
+                scalars=1,
+                flops=10**9,
+            )
+            edge, arrived = lax.optimization_barrier((edge, arrived))
+            edge = moved(edge, [(i, i + s) for i in even])
             parts = (q, *arrived, *late)
         else:
             arrived.append(moved(near, [(i, i - s) for i in uneven]))
             n = len(late)
-            wf, new, far, *q_adjusted = call(
+            wf, ws, new, far, *q_adjusted = call(
                 lambda *refs: far_kernel(n, *refs),
-                (flags, ma, mb, u, logs, low, high, wn, ws, q, *late),
-                (big,) * (4 if n else 3),
+                (flags, ma, mb, u, logs, low, high, wn, q, *late),
+                (big, thin, coupled, state_shape) + (state_shape,) * (1 if n else 0),
                 scalars=1,
                 flops=4 * 10**9,
             )
             q = q_adjusted[0] if n else q
-            new, far, arrived = lax.optimization_barrier((new, far, arrived))
+            new, arrived = lax.optimization_barrier((new, arrived))
             parts = (q, *arrived)
             late = (moved(far, top_pairs if 4 * s == count else [(i, i + s) for i in uneven]),)
             if any(i >= s for i in even):
@@ -356,10 +415,10 @@
         kept.append((flags, s, (ma, mb, u, wn, wf, ws)))
         n_parts = len(parts)
         active = number(t == count - 1 if last else leaves(2 * s))
-        ma, mb, u, logs, q = call(
+        ma, mb, u, logs = call(
             lambda *refs: factor_next_kernel(n_parts, *refs),
             (active, *parts),
-            FACTORS + (big,),
+            FACTORS,
             WORK,
             scalars=1,
             flops=4 * 10**9,
@@ -368,9 +427,10 @@
     whole_tip = jnp.eye(TILE, dtype=F32).at[0:effects, 0:effects].set(tip)
     whole_fixed = jnp.pad(rhs_fixed, (0, TILE - effects)).reshape(1, TILE)
     total = float(count * node_count + effects)
+    n_late = len(late)
     (state,) = call(
-        lambda *refs: root_kernel(total, *refs),
-        (active, ma, mb, u, logs, q, whole_tip, whole_fixed),
+        lambda *refs: root_kernel(total, n_late, *refs),
+        (active, ma, mb, u, logs, whole_tip, whole_fixed, edge, q, *late),
         (shape(1, NODES + TILE),),
         ((NODES, TILE), (TILE, TILE)),
         scalars=1,

time: 562 us -> 531 us (0.945)
  waiting for transfers between devices: 311 us -> 285 us
    ppermute x49 -> x50, waiting for transfers between devices: 290 us -> 264 us  [moved(): lax.ppermute(x, AXES, [(device_of(i), device_of(j)) for i, j in pairs])]
    ppermute x49 -> x50, starting transfers between devices: 52.8 us -> 48.2 us  [moved(): lax.ppermute(x, AXES, [(device_of(i), device_of(j)) for i, j in pairs])]
    unnamed x89 -> x93, local copies, waits for them, and re-layouts: 20.7 us -> 22.4 us
    pallas_call x30 -> x31, Pallas kernels: 136 us -> 137 us  [call(): pl.pallas_call(kernel, out_shape=tuple(outs), in_specs=[smem] * scalars +...]
  transfers between devices with their start and end apart: 52 -> 53, of which waited for: 7 -> 6; matrix products, arithmetic and copies ran while one was open for 2% -> 2% of each run, Pallas kernels for 18% -> 20%
where the time goes in v4:
time: 531 us; the launch traced here: 522 us
  waiting for transfers between devices  285 us (54%)
  Pallas kernels  137 us (26%)
  starting transfers between devices  60.5 us (11%)
  local copies, waits for them, and re-layouts  30.5 us (6%)
  other arithmetic  6.77 us (1%)
    ppermute x50, waiting for transfers between devices, moved(): lax.ppermute(x, AXES, [(device_of(i), device_of(j)) for i, j in pairs])  264 us
    pallas_call x31, Pallas kernels, call(): pl.pallas_call(kernel, out_shape=tuple(outs), in_specs=[smem] * scalars +...  137 us
    ppermute x50, starting transfers between devices, moved(): lax.ppermute(x, AXES, [(device_of(i), device_of(j)) for i, j in pairs])  48.2 us
    unnamed x93, local copies, waits for them, and re-layouts  22.4 us
    all_to_all x1, waiting for transfers between devices, per_device(): got = lax.all_to_all(sent, 'col', split_axis=0, concat_axis=0, tiled=True)  15 us
  transfers between devices with their start and end apart: 53, of which 6 were waited for; matrix products, arithmetic and copies ran while one was open for 2% of the time, Pallas kernels for 20%

profile of v4, /device:TPU:6, one launch (start us, length us, event | category | flops | bytes accessed | tf_op | source)
XLA Modules:
  0.0 521.8 jit_solution(10602395308157804678)
XLA Ops:
  3.2 5.4 %all-to-all-start = ((f32[4,576,128]{2,1,0:T(8,128)}), f32[4,576,128]{2,1,0:T(8,128)S(1)}, u32[]{:S(2)}, u32[]{:S(2)}) async-start(f32[4,576,128]{2,1,0:T(8,128)} %maximum_select_fusion), calls=%async_computation | async-start | bytes 2359296 | tf_op jit(solution)/shard_map/all_to_all | solution.py:347
  10.2 15.0 %all-to-all-done.got = f32[4,576,128]{2,1,0:T(8,128)S(1)} async-done(((f32[4,576,128]{2,1,0:T(8,128)}), f32[4,576,128]{2,1,0:T(8,128)S(1)}, u32[]{:S(2)}, u32[]{:S(2)}) %all-to-all-start) | async-done | bytes 1179680 | tf_op jit(solution)/shard_map/all_to_all | solution.py:347
  26.2 3.6 all-to-all-start.1
  31.2 21.1 %shard_map.85 = (f32[256,256]{1,0:T(8,128)}, f32[256,256]{1,0:T(8,128)}, f32[256,256]{1,0:T(8,128)}, f32[8,128]{1,0:T(8,128)}, f32[1920,128]{1,0:T(8,128)}) custom-call(s32[4]{0:T(128)} %pad_add_fusion.7.flags, f32[4,576,128]{2,1,0:T(8,128)} %copy-done.3, f32[4,512]{1,0:T(4,128)} %rhs.2), custom_call_target="tpu_custom_call" | custom-call | flops 4000000000 | bytes 2961424 | tf_op jit(solution)/shard_map/pallas_call | solution.py:312
  52.2 3.0 all-to-all-done.1.got
  56.6 3.5 shard_map.86
  60.0 6.6 %shard_map.87 = (f32[512,512]{1,0:T(8,128)}, f32[1280,128]{1,0:T(8,128)}) custom-call(s32[2]{0:T(128)} %pad_add_fusion.flags.refs_0_, f32[256,256]{1,0:T(8,128)} %get-tuple-element.119.ma.refs_1_, f32[256,256]{1,0:T(8,128)} %get-tuple-element.120.mb.refs_2_, f32[256,256]{1,0:T(8,128)} %get-tuple-element.121.u.refs_3_, ...), custom_call_target="tpu_custom_call" | custom-call | flops 3000000000 | bytes 5242888 | tf_op jit(solution)/shard_map/pallas_call | solution.py:312
  68.6 13.9 %shard_map.88 = (f32[512,512]{1,0:T(8,128)}, f32[512,128]{1,0:T(8,128)}, f32[2688,128]{1,0:T(8,128)}, f32[1920,128]{1,0:T(8,128)}) custom-call(s32[2]{0:T(128)} %pad_add_fusion.flags.refs_0_, f32[256,256]{1,0:T(8,128)} %get-tuple-element.119.ma.refs_1_, f32[256,256]{1,0:T(8,128)} %get-tuple-element.120.mb.refs_2_, f32[256,256]{1,0:T(8,128)} %get-tuple-element.121.u.refs_3_, ...), custom_call_target="tpu_custom_call" | custom-call | flops 4000000000 | bytes 9244680 | tf_op jit(solution)/shard_map/pallas_call | solution.py:312
  85.6 1.6 collective-permute-start.4
  87.2 2.3 collective-permute-start.5
  90.1 2.7 shard_map.89
  92.8 28.4 %collective-permute-done.2.low.refs_5_ = f32[2688,128]{1,0:T(8,128)S(1)} collective-permute-done((f32[2688,128]{1,0:T(8,128)}, f32[2688,128]{1,0:T(8,128)S(1)}, u32[]{:S(2)}, u32[]{:S(2)}) %collective-permute-start.2) | collective-permute-done | bytes 1376288 | tf_op jit(solution)/shard_map/ppermute | solution.py:331
  122.8 3.2 shard_map.90
  127.4 5.7 %shard_map.91 = (f32[512,512]{1,0:T(8,128)}, f32[512,128]{1,0:T(8,128)}, f32[2688,128]{1,0:T(8,128)}, f32[1920,128]{1,0:T(8,128)}, f32[1920,128]{1,0:T(8,128)}) custom-call(s32[2]{0:T(128)} %pad_add_fusion.1.flags.refs_0_, f32[256,256]{1,0:T(8,128)} %get-tuple-element.131.ma.refs_1_, f32[256,256]{1,0:T(8,128)} %get-tuple-element.132.mb.refs_2_, ...), custom_call_target="tpu_custom_call" | custom-call | flops 4000000000 | bytes 12193800 | tf_op jit(solution)/shard_map/pallas_call | solution.py:312
  135.6 1.6 collective-permute-start.10
  137.2 1.6 collective-permute-start.11
  139.5 2.9 shard_map.92
  143.9 3.2 shard_map.93
  148.6 5.5 %shard_map.94 = (f32[512,512]{1,0:T(8,128)}, f32[512,128]{1,0:T(8,128)}, f32[2688,128]{1,0:T(8,128)}, f32[1920,128]{1,0:T(8,128)}, f32[1920,128]{1,0:T(8,128)}) custom-call(s32[2]{0:T(128)} %pad_add_fusion.2.flags.refs_0_, f32[256,256]{1,0:T(8,128)} %get-tuple-element.143.ma.refs_1_, f32[256,256]{1,0:T(8,128)} %get-tuple-element.144.mb.refs_2_, ...), custom_call_target="tpu_custom_call" | custom-call | flops 4000000000 | bytes 12193800 | tf_op jit(solution)/shard_map/pallas_call | solution.py:312
  158.2 1.6 collective-permute-start.17
  160.5 2.7 shard_map.95
  164.7 3.2 shard_map.96
  169.3 5.6 %shard_map.97 = (f32[512,512]{1,0:T(8,128)}, f32[512,128]{1,0:T(8,128)}, f32[2688,128]{1,0:T(8,128)}, f32[1920,128]{1,0:T(8,128)}, f32[1920,128]{1,0:T(8,128)}) custom-call(s32[2]{0:T(128)} %pad_add_fusion.3.flags.refs_0_, f32[256,256]{1,0:T(8,128)} %get-tuple-element.155.ma.refs_1_, f32[256,256]{1,0:T(8,128)} %get-tuple-element.156.mb.refs_2_, ...), custom_call_target="tpu_custom_call" | custom-call | flops 4000000000 | bytes 12193800 | tf_op jit(solution)/shard_map/pallas_call | solution.py:312
  177.4 1.6 collective-permute-start.22
  181.2 2.9 shard_map.98
  185.7 3.2 shard_map.99
  190.3 5.5 %shard_map.100 = (f32[512,512]{1,0:T(8,128)}, f32[512,128]{1,0:T(8,128)}, f32[2688,128]{1,0:T(8,128)}, f32[1920,128]{1,0:T(8,128)}, f32[1920,128]{1,0:T(8,128)}) custom-call(s32[2]{0:T(128)} %pad_add_fusion.4.flags.refs_0_, f32[256,256]{1,0:T(8,128)} %get-tuple-element.167.ma.refs_1_, f32[256,256]{1,0:T(8,128)} %get-tuple-element.168.mb.refs_2_, ...), custom_call_target="tpu_custom_call" | custom-call | flops 4000000000 | bytes 12193800 | tf_op jit(solution)/shard_map/pallas_call | solution.py:312
  198.3 1.6 collective-permute-start.28
  202.2 2.7 shard_map.101
  206.4 3.2 shard_map.102
  211.1 5.7 %shard_map.103 = (f32[512,512]{1,0:T(8,128)}, f32[512,128]{1,0:T(8,128)}, f32[2688,128]{1,0:T(8,128)}, f32[1920,128]{1,0:T(8,128)}, f32[1920,128]{1,0:T(8,128)}) custom-call(s32[2]{0:T(128)} %pad_add_fusion.5.flags.refs_0_, f32[256,256]{1,0:T(8,128)} %get-tuple-element.179.ma.refs_1_, f32[256,256]{1,0:T(8,128)} %get-tuple-element.180.mb.refs_2_, ...), custom_call_target="tpu_custom_call" | custom-call | flops 4000000000 | bytes 12193800 | tf_op jit(solution)/shard_map/pallas_call | solution.py:312
  219.8 1.6 collective-permute-start.35
  221.5 2.6 shard_map.104
  225.6 3.3 shard_map.105
  231.0 3.4 shard_map.106
  235.3 2.8 shard_map.107
  238.9 2.5 shard_map.108.own
  243.8 2.8 shard_map.109.own
  248.5 2.8 shard_map.110.own
  253.2 2.8 shard_map.111.own
  257.8 2.8 shard_map.112.own
  262.5 2.7 shard_map.113.own
  267.2 2.8 shard_map.114.own
  272.6 228.8 %collective-permute-done.48.from_left = f32[1,640]{1,0:T(1,128)S(1)} collective-permute-done((f32[1,640]{1,0:T(1,128)}, f32[1,640]{1,0:T(1,128)S(1)}, u32[]{:S(2)}, u32[]{:S(2)}) %collective-permute-start.48) | collective-permute-done | bytes 2592 | tf_op jit(solution)/shard_map/ppermute | solution.py:331
  501.4 6.5 %collective-permute-done.49.from_right = f32[1,640]{1,0:T(1,128)S(1)} collective-permute-done((f32[1,640]{1,0:T(1,128)}, f32[1,640]{1,0:T(1,128)S(1)}, u32[]{:S(2)}, u32[]{:S(2)}) %collective-permute-start.49) | collective-permute-done | bytes 2592 | tf_op jit(solution)/shard_map/ppermute | solution.py:331
  508.5 2.8 shard_map.115
  512.5 3.2 all-to-all-start.2
  518.1 2.9 all-to-all-done.2
  (206 shorter events, 71.9 us)
Async XLA Ops:
  3.2 21.9 %all-to-all-start = ((f32[4,576,128]{2,1,0:T(8,128)}), f32[4,576,128]{2,1,0:T(8,128)S(1)}, u32[]{:S(2)}, u32[]{:S(2)}) async-start(f32[4,576,128]{2,1,0:T(8,128)} %maximum_select_fusion), calls=%async_computation | async-start | bytes 2359296 | tf_op jit(solution)/shard_map/all_to_all | solution.py:347
  26.2 29.1 %all-to-all-start.1 = ((f32[4,2,512,128]{3,2,1,0:T(8,128)}), f32[4,2,512,128]{3,2,1,0:T(8,128)S(1)}, u32[]{:S(2)}, u32[]{:S(2)}) async-start(f32[4,2,512,128]{3,2,1,0:T(8,128)} %bitcast.36), calls=%async_computation.1 | async-start | bytes 4194304 | tf_op jit(solution)/shard_map/all_to_all | solution.py:353
  66.6 15.9 %collective-permute-start = (f32[1280,128]{1,0:T(8,128)}, f32[1280,128]{1,0:T(8,128)S(1)}, u32[]{:S(2)}, u32[]{:S(2)}) collective-permute-start(f32[1280,128]{1,0:T(8,128)} %get-tuple-element.128), channel_id=1, source_target_pairs={{0,1},{6,7},{8,9},{14,15},{16,17},{22,23},{24,25},{30,31},{32,33},... | collective-permute-start | bytes 1966088 | tf_op jit(solution)/shard_map/ppermute | solution.py:331
  67.9 14.6 %collective-permute-start.1 = (f32[1280,128]{1,0:T(8,128)}, f32[1280,128]{1,0:T(8,128)S(1)}, u32[]{:S(2)}, u32[]{:S(2)}) collective-permute-start(f32[1280,128]{1,0:T(8,128)} %get-tuple-element.128), channel_id=1, source_target_pairs={{2,1},{4,7},{10,9},{12,15},{18,17},{20,23},{26,25},{28,31},{34,33}... | collective-permute-start | bytes 1966088 | tf_op jit(solution)/shard_map/ppermute | solution.py:331
  83.4 37.8 %collective-permute-start.2 = (f32[2688,128]{1,0:T(8,128)}, f32[2688,128]{1,0:T(8,128)S(1)}, u32[]{:S(2)}, u32[]{:S(2)}) collective-permute-start(f32[2688,128]{1,0:T(8,128)} %get-tuple-element.135), channel_id=1, source_target_pairs={{0,1},{6,7},{8,9},{14,15},{16,17},{22,23},{24,25},{30,31},{32,33},... | collective-permute-start | bytes 4128776 | tf_op jit(solution)/shard_map/ppermute | solution.py:331
  84.8 36.5 %collective-permute-start.3 = (f32[2688,128]{1,0:T(8,128)}, f32[2688,128]{1,0:T(8,128)S(1)}, u32[]{:S(2)}, u32[]{:S(2)}) collective-permute-start(f32[2688,128]{1,0:T(8,128)} %get-tuple-element.135), channel_id=1, source_target_pairs={{2,1},{4,7},{10,9},{12,15},{18,17},{20,23},{26,25},{28,31},{34,33}... | collective-permute-start | bytes 4128776 | tf_op jit(solution)/shard_map/ppermute | solution.py:331
  85.6 41.8 %collective-permute-start.4 = (f32[1920,128]{1,0:T(8,128)}, f32[1920,128]{1,0:T(8,128)}, u32[]{:S(2)}, u32[]{:S(2)}) collective-permute-start(f32[1920,128]{1,0:T(8,128)} %get-tuple-element.137), channel_id=1, source_target_pairs={{2,3},{4,5},{10,11},{12,13},{18,19},{20,21},{26,27},{28,29},{34,35... | collective-permute-start | bytes 2949128 | tf_op jit(solution)/shard_map/ppermute | solution.py:331
  87.2 40.2 %collective-permute-start.5 = (f32[1920,128]{1,0:T(8,128)}, f32[1920,128]{1,0:T(8,128)}, u32[]{:S(2)}, u32[]{:S(2)}) collective-permute-start(f32[1920,128]{1,0:T(8,128)} %get-tuple-element.137), channel_id=1, source_target_pairs={{6,3},{8,5},{14,11},{16,13},{22,19},{24,21},{30,27},{32,29},{38,35... | collective-permute-start | bytes 2949128 | tf_op jit(solution)/shard_map/ppermute | solution.py:331
  126.0 7.1 %collective-permute-start.6 = (f32[1280,128]{1,0:T(8,128)}, f32[1280,128]{1,0:T(8,128)S(1)}, u32[]{:S(2)}, u32[]{:S(2)}) collective-permute-start(f32[1280,128]{1,0:T(8,128)} %get-tuple-element.140), channel_id=1, source_target_pairs={{1,3},{9,11},{17,19},{25,27},{33,35},{41,43},{49,51},{57,59},{65,6... | collective-permute-start | bytes 1966088 | tf_op jit(solution)/shard_map/ppermute | solution.py:331
  126.7 6.4 %collective-permute-start.7 = (f32[1280,128]{1,0:T(8,128)}, f32[1280,128]{1,0:T(8,128)S(1)}, u32[]{:S(2)}, u32[]{:S(2)}) collective-permute-start(f32[1280,128]{1,0:T(8,128)} %get-tuple-element.140), channel_id=1, source_target_pairs={{7,3},{15,11},{23,19},{31,27},{39,35},{47,43},{55,51},{63,59},{71,... | collective-permute-start | bytes 1966088 | tf_op jit(solution)/shard_map/ppermute | solution.py:331
  134.0 8.4 %collective-permute-start.8 = (f32[2688,128]{1,0:T(8,128)}, f32[2688,128]{1,0:T(8,128)S(1)}, u32[]{:S(2)}, u32[]{:S(2)}) collective-permute-start(f32[2688,128]{1,0:T(8,128)} %get-tuple-element.147), channel_id=1, source_target_pairs={{1,3},{9,11},{17,19},{25,27},{33,35},{41,43},{49,51},{57,59},{65,6... | collective-permute-start | bytes 4128776 | tf_op jit(solution)/shard_map/ppermute | solution.py:331
  134.8 7.6 %collective-permute-start.9 = (f32[2688,128]{1,0:T(8,128)}, f32[2688,128]{1,0:T(8,128)S(1)}, u32[]{:S(2)}, u32[]{:S(2)}) collective-permute-start(f32[2688,128]{1,0:T(8,128)} %get-tuple-element.147), channel_id=1, source_target_pairs={{7,3},{15,11},{23,19},{31,27},{39,35},{47,43},{55,51},{63,59},{71,... | collective-permute-start | bytes 4128776 | tf_op jit(solution)/shard_map/ppermute | solution.py:331
  135.6 13.0 %collective-permute-start.10 = (f32[1920,128]{1,0:T(8,128)}, f32[1920,128]{1,0:T(8,128)}, u32[]{:S(2)}, u32[]{:S(2)}) collective-permute-start(f32[1920,128]{1,0:T(8,128)} %get-tuple-element.149), channel_id=1, source_target_pairs={{7,5},{15,13},{23,21},{31,29},{39,37},{47,45},{55,53},{63,61},{71,... | collective-permute-start | bytes 2949128 | tf_op jit(solution)/shard_map/ppermute | solution.py:331
  137.2 11.4 %collective-permute-start.11 = (f32[1920,128]{1,0:T(8,128)}, f32[1920,128]{1,0:T(8,128)}, u32[]{:S(2)}, u32[]{:S(2)}) collective-permute-start(f32[1920,128]{1,0:T(8,128)} %get-tuple-element.149), channel_id=1, source_target_pairs={{9,5},{17,13},{25,21},{33,29},{41,37},{49,45},{57,53},{65,61},{73,... | collective-permute-start | bytes 2949128 | tf_op jit(solution)/shard_map/ppermute | solution.py:331
  147.2 7.0 %collective-permute-start.12 = (f32[1280,128]{1,0:T(8,128)}, f32[1280,128]{1,0:T(8,128)S(1)}, u32[]{:S(2)}, u32[]{:S(2)}) collective-permute-start(f32[1280,128]{1,0:T(8,128)} %get-tuple-element.152), channel_id=1, source_target_pairs={{3,5},{19,21},{35,37},{51,53},{67,69},{83,85},{99,101},{115,117}} | collective-permute-start | bytes 1966088 | tf_op jit(solution)/shard_map/ppermute | solution.py:331
  147.9 6.3 %collective-permute-start.13 = (f32[1280,128]{1,0:T(8,128)}, f32[1280,128]{1,0:T(8,128)S(1)}, u32[]{:S(2)}, u32[]{:S(2)}) collective-permute-start(f32[1280,128]{1,0:T(8,128)} %get-tuple-element.152), channel_id=1, source_target_pairs={{11,5},{27,21},{43,37},{59,53},{75,69},{91,85},{107,101},{123,117}} | collective-permute-start | bytes 1966088 | tf_op jit(solution)/shard_map/ppermute | solution.py:331
  155.0 8.1 %collective-permute-start.14 = (f32[2688,128]{1,0:T(8,128)}, f32[2688,128]{1,0:T(8,128)S(1)}, u32[]{:S(2)}, u32[]{:S(2)}) collective-permute-start(f32[2688,128]{1,0:T(8,128)} %get-tuple-element.159), channel_id=1, source_target_pairs={{3,5},{19,21},{35,37},{51,53},{67,69},{83,85},{99,101},{115,117}} | collective-permute-start | bytes 4128776 | tf_op jit(solution)/shard_map/ppermute | solution.py:331
  155.8 7.4 %collective-permute-start.15 = (f32[2688,128]{1,0:T(8,128)}, f32[2688,128]{1,0:T(8,128)S(1)}, u32[]{:S(2)}, u32[]{:S(2)}) collective-permute-start(f32[2688,128]{1,0:T(8,128)} %get-tuple-element.159), channel_id=1, source_target_pairs={{11,5},{27,21},{43,37},{59,53},{75,69},{91,85},{107,101},{123,117}} | collective-permute-start | bytes 4128776 | tf_op jit(solution)/shard_map/ppermute | solution.py:331
  156.6 12.7 %collective-permute-start.16 = (f32[1920,128]{1,0:T(8,128)}, f32[1920,128]{1,0:T(8,128)}, u32[]{:S(2)}, u32[]{:S(2)}) collective-permute-start(f32[1920,128]{1,0:T(8,128)} %get-tuple-element.161), channel_id=1, source_target_pairs={{11,13},{27,29},{43,45},{59,61},{75,77},{91,93},{107,109},{123,125}} | collective-permute-start | bytes 2949128 | tf_op jit(solution)/shard_map/ppermute | solution.py:331
  158.2 11.1 %collective-permute-start.17 = (f32[1920,128]{1,0:T(8,128)}, f32[1920,128]{1,0:T(8,128)}, u32[]{:S(2)}, u32[]{:S(2)}) collective-permute-start(f32[1920,128]{1,0:T(8,128)} %get-tuple-element.161), channel_id=1, source_target_pairs={{19,13},{35,29},{51,45},{67,61},{83,77},{99,93},{115,109}} | collective-permute-start | bytes 2949128 | tf_op jit(solution)/shard_map/ppermute | solution.py:331
  167.9 7.0 %collective-permute-start.18 = (f32[1280,128]{1,0:T(8,128)}, f32[1280,128]{1,0:T(8,128)S(1)}, u32[]{:S(2)}, u32[]{:S(2)}) collective-permute-start(f32[1280,128]{1,0:T(8,128)} %get-tuple-element.164), channel_id=1, source_target_pairs={{5,13},{37,45},{69,77},{101,109}} | collective-permute-start | bytes 1966088 | tf_op jit(solution)/shard_map/ppermute | solution.py:331
  168.6 6.3 %collective-permute-start.19 = (f32[1280,128]{1,0:T(8,128)}, f32[1280,128]{1,0:T(8,128)S(1)}, u32[]{:S(2)}, u32[]{:S(2)}) collective-permute-start(f32[1280,128]{1,0:T(8,128)} %get-tuple-element.164), channel_id=1, source_target_pairs={{21,13},{53,45},{85,77},{117,109}} | collective-permute-start | bytes 1966088 | tf_op jit(solution)/shard_map/ppermute | solution.py:331
  175.8 8.3 %collective-permute-start.20 = (f32[2688,128]{1,0:T(8,128)}, f32[2688,128]{1,0:T(8,128)S(1)}, u32[]{:S(2)}, u32[]{:S(2)}) collective-permute-start(f32[2688,128]{1,0:T(8,128)} %get-tuple-element.171), channel_id=1, source_target_pairs={{5,13},{37,45},{69,77},{101,109}} | collective-permute-start | bytes 4128776 | tf_op jit(solution)/shard_map/ppermute | solution.py:331
  176.6 7.6 %collective-permute-start.21 = (f32[2688,128]{1,0:T(8,128)}, f32[2688,128]{1,0:T(8,128)S(1)}, u32[]{:S(2)}, u32[]{:S(2)}) collective-permute-start(f32[2688,128]{1,0:T(8,128)} %get-tuple-element.171), channel_id=1, source_target_pairs={{21,13},{53,45},{85,77},{117,109}} | collective-permute-start | bytes 4128776 | tf_op jit(solution)/shard_map/ppermute | solution.py:331
  177.4 13.0 %collective-permute-start.22 = (f32[1920,128]{1,0:T(8,128)}, f32[1920,128]{1,0:T(8,128)}, u32[]{:S(2)}, u32[]{:S(2)}) collective-permute-start(f32[1920,128]{1,0:T(8,128)} %get-tuple-element.173), channel_id=1, source_target_pairs={{21,29},{53,61},{85,93},{117,125}} | collective-permute-start | bytes 2949128 | tf_op jit(solution)/shard_map/ppermute | solution.py:331
  179.0 11.3 %collective-permute-start.23 = (f32[1920,128]{1,0:T(8,128)}, f32[1920,128]{1,0:T(8,128)}, u32[]{:S(2)}, u32[]{:S(2)}) collective-permute-start(f32[1920,128]{1,0:T(8,128)} %get-tuple-element.173), channel_id=1, source_target_pairs={{37,29},{69,61},{101,93}} | collective-permute-start | bytes 2949128 | tf_op jit(solution)/shard_map/ppermute | solution.py:331
  188.9 6.9 %collective-permute-start.24 = (f32[1280,128]{1,0:T(8,128)}, f32[1280,128]{1,0:T(8,128)S(1)}, u32[]{:S(2)}, u32[]{:S(2)}) collective-permute-start(f32[1280,128]{1,0:T(8,128)} %get-tuple-element.176), channel_id=1, source_target_pairs={{13,29},{77,93}} | collective-permute-start | bytes 1966088 | tf_op jit(solution)/shard_map/ppermute | solution.py:331
  189.6 6.3 %collective-permute-start.25 = (f32[1280,128]{1,0:T(8,128)}, f32[1280,128]{1,0:T(8,128)S(1)}, u32[]{:S(2)}, u32[]{:S(2)}) collective-permute-start(f32[1280,128]{1,0:T(8,128)} %get-tuple-element.176), channel_id=1, source_target_pairs={{45,29},{109,93}} | collective-permute-start | bytes 1966088 | tf_op jit(solution)/shard_map/ppermute | solution.py:331
  196.8 8.1 %collective-permute-start.26 = (f32[2688,128]{1,0:T(8,128)}, f32[2688,128]{1,0:T(8,128)S(1)}, u32[]{:S(2)}, u32[]{:S(2)}) collective-permute-start(f32[2688,128]{1,0:T(8,128)} %get-tuple-element.183), channel_id=1, source_target_pairs={{13,29},{77,93}} | collective-permute-start | bytes 4128776 | tf_op jit(solution)/shard_map/ppermute | solution.py:331
  197.5 7.4 %collective-permute-start.27 = (f32[2688,128]{1,0:T(8,128)}, f32[2688,128]{1,0:T(8,128)S(1)}, u32[]{:S(2)}, u32[]{:S(2)}) collective-permute-start(f32[2688,128]{1,0:T(8,128)} %get-tuple-element.183), channel_id=1, source_target_pairs={{45,29},{109,93}} | collective-permute-start | bytes 4128776 | tf_op jit(solution)/shard_map/ppermute | solution.py:331
  198.3 12.8 %collective-permute-start.28 = (f32[1920,128]{1,0:T(8,128)}, f32[1920,128]{1,0:T(8,128)}, u32[]{:S(2)}, u32[]{:S(2)}) collective-permute-start(f32[1920,128]{1,0:T(8,128)} %get-tuple-element.185), channel_id=1, source_target_pairs={{45,61},{109,125}} | collective-permute-start | bytes 2949128 | tf_op jit(solution)/shard_map/ppermute | solution.py:331
  199.9 11.2 %collective-permute-start.29 = (f32[1920,128]{1,0:T(8,128)}, f32[1920,128]{1,0:T(8,128)}, u32[]{:S(2)}, u32[]{:S(2)}) collective-permute-start(f32[1920,128]{1,0:T(8,128)} %get-tuple-element.185), channel_id=1, source_target_pairs={{77,61}} | collective-permute-start | bytes 2949128 | tf_op jit(solution)/shard_map/ppermute | solution.py:331
  209.7 7.2 %collective-permute-start.30 = (f32[1280,128]{1,0:T(8,128)}, f32[1280,128]{1,0:T(8,128)S(1)}, u32[]{:S(2)}, u32[]{:S(2)}) collective-permute-start(f32[1280,128]{1,0:T(8,128)} %get-tuple-element.188), channel_id=1, source_target_pairs={{29,61}} | collective-permute-start | bytes 1966088 | tf_op jit(solution)/shard_map/ppermute | solution.py:331
  210.4 6.5 %collective-permute-start.31 = (f32[1280,128]{1,0:T(8,128)}, f32[1280,128]{1,0:T(8,128)S(1)}, u32[]{:S(2)}, u32[]{:S(2)}) collective-permute-start(f32[1280,128]{1,0:T(8,128)} %get-tuple-element.188), channel_id=1, source_target_pairs={{93,61}} | collective-permute-start | bytes 1966088 | tf_op jit(solution)/shard_map/ppermute | solution.py:331
  217.7 6.4 %collective-permute-start.32 = (f32[2688,128]{1,0:T(8,128)}, f32[2688,128]{1,0:T(8,128)S(1)}, u32[]{:S(2)}, u32[]{:S(2)}) collective-permute-start(f32[2688,128]{1,0:T(8,128)} %get-tuple-element.195), channel_id=1, source_target_pairs={{29,61}} | collective-permute-start | bytes 4128776 | tf_op jit(solution)/shard_map/ppermute | solution.py:331
  218.5 5.6 %collective-permute-start.33 = (f32[2688,128]{1,0:T(8,128)}, f32[2688,128]{1,0:T(8,128)S(1)}, u32[]{:S(2)}, u32[]{:S(2)}) collective-permute-start(f32[2688,128]{1,0:T(8,128)} %get-tuple-element.195), channel_id=1, source_target_pairs={{93,61}} | collective-permute-start | bytes 4128776 | tf_op jit(solution)/shard_map/ppermute | solution.py:331
  219.8 15.3 %collective-permute-start.35 = (f32[1920,128]{1,0:T(8,128)}, f32[1920,128]{1,0:T(8,128)}, u32[]{:S(2)}, u32[]{:S(2)}) collective-permute-start(f32[1920,128]{1,0:T(8,128)} %get-tuple-element.200), channel_id=1, source_target_pairs={{61,93},{125,61},{93,125}} | collective-permute-start | bytes 2949128 | tf_op jit(solution)/shard_map/ppermute | solution.py:331
  228.9 5.5 %collective-permute-start.34 = (f32[1280,128]{1,0:T(8,128)}, f32[1280,128]{1,0:T(8,128)S(1)}, u32[]{:S(2)}, u32[]{:S(2)}) collective-permute-start(f32[1280,128]{1,0:T(8,128)} %get-tuple-element.198), channel_id=1, source_target_pairs={{61,125}} | collective-permute-start | bytes 1966088 | tf_op jit(solution)/shard_map/ppermute | solution.py:331
  234.5 3.6 collective-permute-start.36
  246.5 1.3 collective-permute-start.38
  247.2 0.7 collective-permute-start.39
  251.2 1.3 collective-permute-start.40
  255.9 1.3 collective-permute-start.42
  260.6 1.3 collective-permute-start.44
  265.3 1.3 collective-permute-start.46
  270.0 231.4 %collective-permute-start.48 = (f32[1,640]{1,0:T(1,128)}, f32[1,640]{1,0:T(1,128)S(1)}, u32[]{:S(2)}, u32[]{:S(2)}) collective-permute-start(f32[1,640]{1,0:T(1,128)} %shard_map.114.own), channel_id=1, source_target_pairs={{1,2},{3,6},{7,4},{5,8},{9,10},{11,14},{15,12},{13,16},{17,18},{19... | collective-permute-start | bytes 7688 | tf_op jit(solution)/shard_map/ppermute | solution.py:331
  271.3 236.6 %collective-permute-start.49 = (f32[1,640]{1,0:T(1,128)}, f32[1,640]{1,0:T(1,128)S(1)}, u32[]{:S(2)}, u32[]{:S(2)}) collective-permute-start(f32[1,640]{1,0:T(1,128)} %shard_map.114.own), channel_id=1, source_target_pairs={{1,0},{3,2},{7,6},{5,4},{9,8},{11,10},{15,14},{13,12},{17,16},{19,... | collective-permute-start | bytes 7688 | tf_op jit(solution)/shard_map/ppermute | solution.py:331
  512.5 8.4 %all-to-all-start.2 = ((f32[1,4,128]{2,0,1:T(1,128)}), f32[1,4,128]{2,0,1:T(1,128)S(1)}, u32[]{:S(2)}, u32[]{:S(2)}) async-start(f32[1,4,128]{2,0,1:T(1,128)} %slice_bitcast_fusion), calls=%async_computation.2 | async-start | bytes 4096 | tf_op jit(solution)/shard_map/all_to_all | solution.py:455
  (51 other events, 100.3 us)

commit v5 on v4

--- a/solution.py
+++ b/solution.py
@@ -121,8 +121,8 @@
     return slice(base + index * TILE, base + (index + 1) * TILE)
 
 
-def factor_first_kernel(flags, got, rhs, ma, mb, u, logs, q, s, inv):
-    right = rhs[pl.ds(flags[2], 1), :]
+def factor_first_kernel(place, flags, got, rhs, ma, mb, u, logs, q, s, inv):
+    right = rhs[pl.ds(flags[place], 1), :]
     for k in range(4):
         s[:, k * TILE : (k + 1) * TILE] = got[k, 0:NODES, :]
     for b, (i, j) in enumerate(UPPER):
@@ -140,10 +140,10 @@
         logs[...] = factor_body(s, inv, ma, mb, u)
 
 
-def couple_first_kernel(flags, got, low, high):
+def couple_first_kernel(place, flags, got, low, high):
     for k in range(4):
         high[k * NODES : (k + 1) * NODES, :] = got[k, 1]
-        turned = jnp.where(flags[3] > 0, got[k, 0].T, 0.0)
+        turned = jnp.where(flags[place + 1] > 0, got[k, 0].T, 0.0)
         for j in range(4):
             o = j * NODES + k * TILE
             low[o : o + TILE, :] = turned[:, j * TILE : (j + 1) * TILE]
@@ -305,14 +305,22 @@
     return jax.ShapeDtypeStruct(dims, F32)
 
 
-def call(kernel, ins, outs, scratch=(), scalars=0, flops=0):
+class Entries:
+    def __init__(self, table, base):
+        self.table, self.base = table, base
+
+    def __getitem__(self, k):
+        return self.table[self.base + k]
+
+
+def call(kernel, base, ins, outs, scratch=(), flops=0):
     smem = pl.BlockSpec(memory_space=pltpu.SMEM)
     vmem = pl.BlockSpec(memory_space=pltpu.VMEM)
     moved = 4 * sum(a.size for a in ins) + 4 * sum(o.size for o in outs)
     return pl.pallas_call(
-        kernel,
+        lambda table, *refs: kernel(Entries(table, base), *refs),
         out_shape=tuple(outs),
-        in_specs=[smem] * scalars + [vmem] * (len(ins) - scalars),
+        in_specs=[smem] + [vmem] * (len(ins) - 1),
         out_specs=tuple([vmem] * len(outs)),
         scratch_shapes=[pltpu.VMEM(dims, F32) for dims in scratch],
         cost_estimate=pl.CostEstimate(flops=flops, bytes_accessed=moved, transcendentals=0),
@@ -339,9 +347,12 @@
     col, shift = lax.axis_index("col"), 2 * (lax.axis_index("tm") % 2)
     pos = (col + shift) % cols
     t = lax.axis_index("tm") * cols + pos
-    number = lambda *values: jnp.stack([jnp.asarray(v).astype(jnp.int32) for v in values])
-    leaves = lambda s: (t + 1) % (2 * s) == s
-    first = number(leaves(1), (t + 1) // 2 % 2, pos, t > 0)
+    level_count = count.bit_length() - 1
+    entries = []
+    for s in [1 << k for k in range(level_count)]:
+        entries += [(t + 1) % (2 * s) == s, (t + 1) // (2 * s) % 2]
+    entries += [t == count - 1, 0, pos, t > 0]
+    table = jnp.stack([jnp.asarray(v).astype(jnp.int32) for v in entries])
     sent = jnp.concatenate([blocks, arrow], axis=1)
     sent = jnp.where(shift > 0, jnp.concatenate([sent[2:4], sent[0:2]], axis=0), sent)
     got = lax.all_to_all(sent, "col", split_axis=0, concat_axis=0, tiled=True)
@@ -354,41 +365,48 @@
     big, thin = shape(NODES, NODES), shape(NODES, TILE)
     state_shape, coupled = shape(SQUARE + EDGE, TILE), shape(WHOLE + EDGE, TILE)
     ma, mb, u, logs, q = call(
-        factor_first_kernel,
-        (first, got, rhs),
+        lambda *refs: factor_first_kernel(2 * level_count + 2, *refs),
+        0,
+        (table, got, rhs),
         FACTORS + (state_shape,),
         WORK,
-        scalars=1,
         flops=4 * 10**9,
     )
     low, high = call(
-        couple_first_kernel, (first, wanted), (coupled, coupled), scalars=1, flops=10**6
+        lambda *refs: couple_first_kernel(2 * level_count + 2, *refs),
+        0,
+        (table, wanted),
+        (coupled, coupled),
+        flops=10**6,
     )
     middle, upper_middle = count // 2 - 1, 3 * count // 4 - 1
     top_pairs = [(middle, upper_middle), (count - 1, middle), (upper_middle, count - 1)]
-    kept, late = [], ()
+    kept, late, sent_late = [], (), []
     level = 0
     while (1 << level) < count:
         s = 1 << level
         leaving = [(2 * k + 1) * s - 1 for k in range(count // (2 * s))]
         even, uneven = leaving[0::2], leaving[1::2]
-        flags = number(leaves(s), (t + 1) // (2 * s) % 2)
+        base = 2 * level
         last = 2 * s == count
         wn, near = call(
             near_kernel,
-            (flags, ma, mb, u, low, high),
+            base,
+            (table, ma, mb, u, low, high),
             (big, shape(SQUARE, TILE)),
-            scalars=1,
             flops=3 * 10**9,
         )
+        if sent_late:
+            near, far = lax.optimization_barrier((near, far))
+            late = tuple(moved(far, pairs) for pairs in sent_late)
         arrived = [moved(near, [(i, i + s) for i in even])]
         if last:
             wf = jnp.zeros((NODES, NODES), F32)
             ws, edge = call(
                 last_kernel,
-                (flags, ma, mb, u, logs, low, high, wn, q),
+                base,
+                (table, ma, mb, u, logs, low, high, wn, q),
                 (thin, shape(EDGE, TILE)),
-                scalars=1,
                 flops=10**9,
             )
             edge, arrived = lax.optimization_barrier((edge, arrived))
@@ -398,29 +416,28 @@
             arrived.append(moved(near, [(i, i - s) for i in uneven]))
             n = len(late)
             wf, ws, new, far, *q_adjusted = call(
-                lambda *refs: far_kernel(n, *refs),
-                (flags, ma, mb, u, logs, low, high, wn, q, *late),
+                lambda flags, *refs: far_kernel(n, flags, *refs),
+                base,
+                (table, ma, mb, u, logs, low, high, wn, q, *late),
                 (big, thin, coupled, state_shape) + (state_shape,) * (1 if n else 0),
-                scalars=1,
                 flops=4 * 10**9,
             )
             q = q_adjusted[0] if n else q
             new, arrived = lax.optimization_barrier((new, arrived))
             parts = (q, *arrived)
-            late = (moved(far, top_pairs if 4 * s == count else [(i, i + s) for i in uneven]),)
+            sent_late = [top_pairs if 4 * s == count else [(i, i + s) for i in uneven]]
             if any(i >= s for i in even):
-                late += (moved(far, [(i, i - s) for i in even if i >= s]),)
+                sent_late.append([(i, i - s) for i in even if i >= s])
             low = moved(new, [(i, i + s) for i in even])
             high = moved(new, [(i, i - s) for i in uneven])
-        kept.append((flags, s, (ma, mb, u, wn, wf, ws)))
+        kept.append((base, s, (ma, mb, u, wn, wf, ws)))
         n_parts = len(parts)
-        active = number(t == count - 1 if last else leaves(2 * s))
         ma, mb, u, logs = call(
             lambda *refs: factor_next_kernel(n_parts, *refs),
-            (active, *parts),
+            base + 2,
+            (table, *parts),
             FACTORS,
             WORK,
-            scalars=1,
             flops=4 * 10**9,
         )
         level += 1
@@ -430,13 +447,13 @@
     n_late = len(late)
     (state,) = call(
         lambda *refs: root_kernel(total, n_late, *refs),
-        (active, ma, mb, u, logs, whole_tip, whole_fixed, edge, q, *late),
+        2 * level_count,
+        (table, ma, mb, u, logs, whole_tip, whole_fixed, edge, q, *late),
         (shape(1, NODES + TILE),),
         ((NODES, TILE), (TILE, TILE)),
-        scalars=1,
         flops=10**8,
     )
-    for flags, s, factors in reversed(kept):
+    for base, s, factors in reversed(kept):
         leaving = [(2 * k + 1) * s - 1 for k in range(count // (2 * s))]
         if 2 * s < count:
             pairs = [(i - s, i) for i in leaving if i >= s]
@@ -447,9 +464,9 @@
             from_right = moved(state, top_pairs)
         (state,) = call(
             back_kernel,
-            (flags, from_left, from_right, state) + factors,
+            base,
+            (table, from_left, from_right, state) + factors,
             (shape(1, NODES + TILE),),
-            scalars=1,
             flops=10**7,
         )
     rows = lax.all_to_all(state[:, 0:NODES], "col", split_axis=1, concat_axis=0, tiled=True)

time: 531 us -> 528 us (level)
  starting transfers between devices: 60.5 us -> 50.5 us
  local copies, waits for them, and re-layouts: 30.5 us -> 38 us
    ppermute x50, starting transfers between devices: 48.2 us -> 38.3 us  [moved(): lax.ppermute(x, AXES, [(device_of(i), device_of(j)) for i, j in pairs])]
    unnamed x93 -> x115, local copies, waits for them, and re-layouts: 22.4 us -> 29.3 us
  transfers between devices with their start and end apart: 53 -> 53, of which waited for: 6 -> 7; matrix products, arithmetic and copies ran while one was open for 2% -> 1% of each run, Pallas kernels for 20% -> 17%
where the time goes in v5:
time: 528 us; the launch traced here: 518 us
  waiting for transfers between devices  286 us (54%)
  Pallas kernels  139 us (26%)
  starting transfers between devices  50.5 us (10%)
  local copies, waits for them, and re-layouts  38 us (7%)
    ppermute x50, waiting for transfers between devices, moved(): lax.ppermute(x, AXES, [(device_of(i), device_of(j)) for i, j in pairs])  265 us
    pallas_call x31, Pallas kernels, call(): pl.pallas_call(lambda table, *refs: kernel(Entries(table, base), *refs),...  139 us
    ppermute x50, starting transfers between devices, moved(): lax.ppermute(x, AXES, [(device_of(i), device_of(j)) for i, j in pairs])  38.3 us
    unnamed x115, local copies, waits for them, and re-layouts  29.3 us
    all_to_all x1, waiting for transfers between devices, per_device(): got = lax.all_to_all(sent, 'col', split_axis=0, concat_axis=0, tiled=True)  15 us
  transfers between devices with their start and end apart: 53, of which 7 were waited for; matrix products, arithmetic and copies ran while one was open for 1% of the time, Pallas kernels for 17%

profile of v5, /device:TPU:6, one launch (start us, length us, event | category | flops | bytes accessed | tf_op | source)
XLA Modules:
  0.0 518.3 jit_solution(16923279738161039097)
XLA Ops:
  0.7 1.3 constant_dynamic-update-slice_fusion.1
  3.3 5.4 %all-to-all-start = ((f32[4,576,128]{2,1,0:T(8,128)}), f32[4,576,128]{2,1,0:T(8,128)S(1)}, u32[]{:S(2)}, u32[]{:S(2)}) async-start(f32[4,576,128]{2,1,0:T(8,128)} %maximum_select_fusion), calls=%async_computation | async-start | bytes 2359296 | tf_op jit(solution)/shard_map/all_to_all | solution.py:358
  8.8 1.4 concatenate.17
  10.2 15.0 %all-to-all-done.refs_0_ = f32[4,576,128]{2,1,0:T(8,128)S(1)} async-done(((f32[4,576,128]{2,1,0:T(8,128)}), f32[4,576,128]{2,1,0:T(8,128)S(1)}, u32[]{:S(2)}, u32[]{:S(2)}) %all-to-all-start) | async-done | bytes 1179680 | tf_op jit(solution)/shard_map/all_to_all | solution.py:358
  26.2 3.6 all-to-all-start.1
  30.8 21.0 %shard_map.85 = (f32[256,256]{1,0:T(8,128)}, f32[256,256]{1,0:T(8,128)}, f32[256,256]{1,0:T(8,128)}, f32[8,128]{1,0:T(8,128)}, f32[1920,128]{1,0:T(8,128)}) custom-call(s32[18]{0:T(128)} %stack.107.table, f32[4,576,128]{2,1,0:T(8,128)} %copy-done.3, f32[4,512]{1,0:T(4,128)} %refs_1_.1), custom_call_target="tpu_custom_call" | custom-call | flops 4000000000 | bytes 2961480 | tf_op jit(solution)/shard_map/pallas_call | solution.py:320
  51.9 3.4 all-to-all-done.1.refs_0_
  55.3 1.3 copy-done
  56.6 3.5 shard_map.86
  60.1 6.6 %shard_map.87 = (f32[512,512]{1,0:T(8,128)}, f32[1280,128]{1,0:T(8,128)}) custom-call(s32[18]{0:T(128)} %stack.107.table, f32[256,256]{1,0:T(8,128)} %get-tuple-element.131.refs_0_.refs_3_, f32[256,256]{1,0:T(8,128)} %get-tuple-element.132.refs_1_.refs_4_, f32[256,256]{1,0:T(8,128)} %get-tuple-element.133.refs_2_.refs_5_, ...), custom_call_target="tpu_custom_call" | custom-call | flops 3000000000 | bytes 5242952 | tf_op jit(solution)/shard_map/pallas_call | solution.py:320
  66.7 1.3 collective-permute-start
  68.8 13.8 %shard_map.88 = (f32[512,512]{1,0:T(8,128)}, f32[512,128]{1,0:T(8,128)}, f32[2688,128]{1,0:T(8,128)}, f32[1920,128]{1,0:T(8,128)}) custom-call(s32[18]{0:T(128)} %stack.107.table, f32[256,256]{1,0:T(8,128)} %get-tuple-element.131.refs_0_.refs_3_, f32[256,256]{1,0:T(8,128)} %get-tuple-element.132.refs_1_.refs_4_, ...), custom_call_target="tpu_custom_call" | custom-call | flops 4000000000 | bytes 9244744 | tf_op jit(solution)/shard_map/pallas_call | solution.py:320
  83.4 1.4 collective-permute-start.2
  85.6 2.8 shard_map.89
  88.4 12.5 %collective-permute-done.2.refs_3_.refs_4_ = f32[2688,128]{1,0:T(8,128)S(1)} collective-permute-done((f32[2688,128]{1,0:T(8,128)}, f32[2688,128]{1,0:T(8,128)S(1)}, u32[]{:S(2)}, u32[]{:S(2)}) %collective-permute-start.2) | collective-permute-done | bytes 1376288 | tf_op jit(solution)/shard_map/ppermute | solution.py:339
  102.4 3.2 shard_map.90
  106.3 1.4 collective-permute-start.5
  109.1 10.4 %collective-permute-done.5.refs_9_ = f32[1920,128]{1,0:T(8,128)S(1)} collective-permute-done((f32[1920,128]{1,0:T(8,128)}, f32[1920,128]{1,0:T(8,128)S(1)}, u32[]{:S(2)}, u32[]{:S(2)}) %collective-permute-start.5) | collective-permute-done | bytes 983072 | tf_op jit(solution)/shard_map/ppermute | solution.py:339
  120.5 5.5 %shard_map.91 = (f32[512,512]{1,0:T(8,128)}, f32[512,128]{1,0:T(8,128)}, f32[2688,128]{1,0:T(8,128)}, f32[1920,128]{1,0:T(8,128)}, f32[1920,128]{1,0:T(8,128)}) custom-call(s32[18]{0:T(128)} %stack.107.table, f32[256,256]{1,0:T(8,128)} %get-tuple-element.143.refs_0_.refs_3_, f32[256,256]{1,0:T(8,128)} %get-tuple-element.144.refs_1_.refs_4_, ...), custom_call_target="tpu_custom_call" | custom-call | flops 4000000000 | bytes 12193864 | tf_op jit(solution)/shard_map/pallas_call | solution.py:320
  128.4 3.1 shard_map.92
  133.0 3.2 shard_map.93
  140.4 5.5 %shard_map.94 = (f32[512,512]{1,0:T(8,128)}, f32[512,128]{1,0:T(8,128)}, f32[2688,128]{1,0:T(8,128)}, f32[1920,128]{1,0:T(8,128)}, f32[1920,128]{1,0:T(8,128)}) custom-call(s32[18]{0:T(128)} %stack.107.table, f32[256,256]{1,0:T(8,128)} %get-tuple-element.157.refs_0_.refs_3_, f32[256,256]{1,0:T(8,128)} %get-tuple-element.158.refs_1_.refs_4_, ...), custom_call_target="tpu_custom_call" | custom-call | flops 4000000000 | bytes 12193864 | tf_op jit(solution)/shard_map/pallas_call | solution.py:320
  148.3 2.7 shard_map.95
  152.6 3.2 shard_map.96
  160.0 5.6 %shard_map.97 = (f32[512,512]{1,0:T(8,128)}, f32[512,128]{1,0:T(8,128)}, f32[2688,128]{1,0:T(8,128)}, f32[1920,128]{1,0:T(8,128)}, f32[1920,128]{1,0:T(8,128)}) custom-call(s32[18]{0:T(128)} %stack.107.table, f32[256,256]{1,0:T(8,128)} %get-tuple-element.171.refs_0_.refs_3_, f32[256,256]{1,0:T(8,128)} %get-tuple-element.172.refs_1_.refs_4_, ...), custom_call_target="tpu_custom_call" | custom-call | flops 4000000000 | bytes 12193864 | tf_op jit(solution)/shard_map/pallas_call | solution.py:320
  168.0 3.0 shard_map.98
  172.5 3.2 shard_map.99
  179.9 5.6 %shard_map.100 = (f32[512,512]{1,0:T(8,128)}, f32[512,128]{1,0:T(8,128)}, f32[2688,128]{1,0:T(8,128)}, f32[1920,128]{1,0:T(8,128)}, f32[1920,128]{1,0:T(8,128)}) custom-call(s32[18]{0:T(128)} %stack.107.table, f32[256,256]{1,0:T(8,128)} %get-tuple-element.185.refs_0_.refs_3_, f32[256,256]{1,0:T(8,128)} %get-tuple-element.186.refs_1_.refs_4_, ...), custom_call_target="tpu_custom_call" | custom-call | flops 4000000000 | bytes 12193864 | tf_op jit(solution)/shard_map/pallas_call | solution.py:320
  187.9 2.8 shard_map.101
  192.2 3.2 shard_map.102
  199.6 5.8 %shard_map.103 = (f32[512,512]{1,0:T(8,128)}, f32[512,128]{1,0:T(8,128)}, f32[2688,128]{1,0:T(8,128)}, f32[1920,128]{1,0:T(8,128)}, f32[1920,128]{1,0:T(8,128)}) custom-call(s32[18]{0:T(128)} %stack.107.table, f32[256,256]{1,0:T(8,128)} %get-tuple-element.199.refs_0_.refs_3_, f32[256,256]{1,0:T(8,128)} %get-tuple-element.200.refs_1_.refs_4_, ...), custom_call_target="tpu_custom_call" | custom-call | flops 4000000000 | bytes 12193864 | tf_op jit(solution)/shard_map/pallas_call | solution.py:320
  207.8 4.4 shard_map.104
  213.6 3.3 shard_map.105
  219.7 3.5 shard_map.106
  225.0 2.8 shard_map.107
  228.6 2.5 shard_map.108.refs_2_
  233.4 2.8 shard_map.109.refs_2_
  238.1 2.7 shard_map.110.refs_2_
  242.8 2.8 shard_map.111.refs_2_
  247.5 2.8 shard_map.112.refs_2_
  252.2 2.8 shard_map.113.refs_2_
  256.9 2.8 shard_map.114.refs_2_
  260.9 1.3 collective-permute-start.49
  262.2 235.7 %collective-permute-done.48.refs_0_ = f32[1,640]{1,0:T(1,128)S(1)} collective-permute-done((f32[1,640]{1,0:T(1,128)}, f32[1,640]{1,0:T(1,128)S(1)}, u32[]{:S(2)}, u32[]{:S(2)}) %collective-permute-start.48) | collective-permute-done | bytes 2592 | tf_op jit(solution)/shard_map/ppermute | solution.py:339
  497.9 6.5 %collective-permute-done.49.refs_1_ = f32[1,640]{1,0:T(1,128)S(1)} collective-permute-done((f32[1,640]{1,0:T(1,128)}, f32[1,640]{1,0:T(1,128)S(1)}, u32[]{:S(2)}, u32[]{:S(2)}) %collective-permute-start.49) | collective-permute-done | bytes 2592 | tf_op jit(solution)/shard_map/ppermute | solution.py:339
  505.0 2.8 shard_map.115
  509.0 3.2 all-to-all-start.2
  514.5 2.9 all-to-all-done.2
  (221 shorter events, 68.8 us)
Async XLA Ops:
  3.3 21.9 %all-to-all-start = ((f32[4,576,128]{2,1,0:T(8,128)}), f32[4,576,128]{2,1,0:T(8,128)S(1)}, u32[]{:S(2)}, u32[]{:S(2)}) async-start(f32[4,576,128]{2,1,0:T(8,128)} %maximum_select_fusion), calls=%async_computation | async-start | bytes 2359296 | tf_op jit(solution)/shard_map/all_to_all | solution.py:358
  26.2 29.1 %all-to-all-start.1 = ((f32[4,2,512,128]{3,2,1,0:T(8,128)}), f32[4,2,512,128]{3,2,1,0:T(8,128)S(1)}, u32[]{:S(2)}, u32[]{:S(2)}) async-start(f32[4,2,512,128]{3,2,1,0:T(8,128)} %bitcast.36), calls=%async_computation.1 | async-start | bytes 4194304 | tf_op jit(solution)/shard_map/all_to_all | solution.py:364
  66.7 15.8 %collective-permute-start = (f32[1280,128]{1,0:T(8,128)}, f32[1280,128]{1,0:T(8,128)S(1)}, u32[]{:S(2)}, u32[]{:S(2)}) collective-permute-start(f32[1280,128]{1,0:T(8,128)} %get-tuple-element.140), channel_id=1, source_target_pairs={{0,1},{6,7},{8,9},{14,15},{16,17},{22,23},{24,25},{30,31},{32,33},... | collective-permute-start | bytes 1966088 | tf_op jit(solution)/shard_map/ppermute | solution.py:339
  68.0 14.5 %collective-permute-start.1 = (f32[1280,128]{1,0:T(8,128)}, f32[1280,128]{1,0:T(8,128)S(1)}, u32[]{:S(2)}, u32[]{:S(2)}) collective-permute-start(f32[1280,128]{1,0:T(8,128)} %get-tuple-element.140), channel_id=1, source_target_pairs={{2,1},{4,7},{10,9},{12,15},{18,17},{20,23},{26,25},{28,31},{34,33}... | collective-permute-start | bytes 1966088 | tf_op jit(solution)/shard_map/ppermute | solution.py:339
  83.4 17.4 %collective-permute-start.2 = (f32[2688,128]{1,0:T(8,128)}, f32[2688,128]{1,0:T(8,128)S(1)}, u32[]{:S(2)}, u32[]{:S(2)}) collective-permute-start(f32[2688,128]{1,0:T(8,128)} %get-tuple-element.147), channel_id=1, source_target_pairs={{0,1},{6,7},{8,9},{14,15},{16,17},{22,23},{24,25},{30,31},{32,33},... | collective-permute-start | bytes 4128776 | tf_op jit(solution)/shard_map/ppermute | solution.py:339
  84.8 16.0 %collective-permute-start.3 = (f32[2688,128]{1,0:T(8,128)}, f32[2688,128]{1,0:T(8,128)S(1)}, u32[]{:S(2)}, u32[]{:S(2)}) collective-permute-start(f32[2688,128]{1,0:T(8,128)} %get-tuple-element.147), channel_id=1, source_target_pairs={{2,1},{4,7},{10,9},{12,15},{18,17},{20,23},{26,25},{28,31},{34,33}... | collective-permute-start | bytes 4128776 | tf_op jit(solution)/shard_map/ppermute | solution.py:339
  105.6 3.5 collective-permute-start.4
  106.3 13.2 %collective-permute-start.5 = (f32[1920,128]{1,0:T(8,128)}, f32[1920,128]{1,0:T(8,128)S(1)}, u32[]{:S(2)}, u32[]{:S(2)}) collective-permute-start(f32[1920,128]{1,0:T(8,128)} %get-tuple-element.151), channel_id=1, source_target_pairs={{6,3},{8,5},{14,11},{16,13},{22,19},{24,21},{30,27},{32,29},{38,35... | collective-permute-start | bytes 2949128 | tf_op jit(solution)/shard_map/ppermute | solution.py:339
  107.7 18.3 %collective-permute-start.6 = (f32[1280,128]{1,0:T(8,128)}, f32[1280,128]{1,0:T(8,128)S(1)}, u32[]{:S(2)}, u32[]{:S(2)}) collective-permute-start(f32[1280,128]{1,0:T(8,128)} %get-tuple-element.154), channel_id=1, source_target_pairs={{1,3},{9,11},{17,19},{25,27},{33,35},{41,43},{49,51},{57,59},{65,6... | collective-permute-start | bytes 1966088 | tf_op jit(solution)/shard_map/ppermute | solution.py:339
  108.4 17.6 %collective-permute-start.7 = (f32[1280,128]{1,0:T(8,128)}, f32[1280,128]{1,0:T(8,128)S(1)}, u32[]{:S(2)}, u32[]{:S(2)}) collective-permute-start(f32[1280,128]{1,0:T(8,128)} %get-tuple-element.154), channel_id=1, source_target_pairs={{7,3},{15,11},{23,19},{31,27},{39,35},{47,43},{55,51},{63,59},{71,... | collective-permute-start | bytes 1966088 | tf_op jit(solution)/shard_map/ppermute | solution.py:339
  126.9 4.6 collective-permute-start.8
  127.7 3.8 collective-permute-start.9
  136.2 2.9 collective-permute-start.10
  137.0 2.2 collective-permute-start.11
  137.7 8.2 %collective-permute-start.12 = (f32[1280,128]{1,0:T(8,128)}, f32[1280,128]{1,0:T(8,128)S(1)}, u32[]{:S(2)}, u32[]{:S(2)}) collective-permute-start(f32[1280,128]{1,0:T(8,128)} %get-tuple-element.168), channel_id=1, source_target_pairs={{3,5},{19,21},{35,37},{51,53},{67,69},{83,85},{99,101},{115,117}} | collective-permute-start | bytes 1966088 | tf_op jit(solution)/shard_map/ppermute | solution.py:339
  138.4 7.5 %collective-permute-start.13 = (f32[1280,128]{1,0:T(8,128)}, f32[1280,128]{1,0:T(8,128)S(1)}, u32[]{:S(2)}, u32[]{:S(2)}) collective-permute-start(f32[1280,128]{1,0:T(8,128)} %get-tuple-element.168), channel_id=1, source_target_pairs={{11,5},{27,21},{43,37},{59,53},{75,69},{91,85},{107,101},{123,117}} | collective-permute-start | bytes 1966088 | tf_op jit(solution)/shard_map/ppermute | solution.py:339
  146.8 4.3 collective-permute-start.14
  147.6 3.5 collective-permute-start.15
  155.8 2.9 collective-permute-start.16
  156.5 2.2 collective-permute-start.17
  157.3 8.3 %collective-permute-start.18 = (f32[1280,128]{1,0:T(8,128)}, f32[1280,128]{1,0:T(8,128)S(1)}, u32[]{:S(2)}, u32[]{:S(2)}) collective-permute-start(f32[1280,128]{1,0:T(8,128)} %get-tuple-element.182), channel_id=1, source_target_pairs={{5,13},{37,45},{69,77},{101,109}} | collective-permute-start | bytes 1966088 | tf_op jit(solution)/shard_map/ppermute | solution.py:339
  158.0 7.6 %collective-permute-start.19 = (f32[1280,128]{1,0:T(8,128)}, f32[1280,128]{1,0:T(8,128)S(1)}, u32[]{:S(2)}, u32[]{:S(2)}) collective-permute-start(f32[1280,128]{1,0:T(8,128)} %get-tuple-element.182), channel_id=1, source_target_pairs={{21,13},{53,45},{85,77},{117,109}} | collective-permute-start | bytes 1966088 | tf_op jit(solution)/shard_map/ppermute | solution.py:339
  166.5 4.5 collective-permute-start.20
  167.2 3.8 collective-permute-start.21
  175.7 2.9 collective-permute-start.22
  176.5 2.2 collective-permute-start.23
  177.2 8.3 %collective-permute-start.24 = (f32[1280,128]{1,0:T(8,128)}, f32[1280,128]{1,0:T(8,128)S(1)}, u32[]{:S(2)}, u32[]{:S(2)}) collective-permute-start(f32[1280,128]{1,0:T(8,128)} %get-tuple-element.196), channel_id=1, source_target_pairs={{13,29},{77,93}} | collective-permute-start | bytes 1966088 | tf_op jit(solution)/shard_map/ppermute | solution.py:339
  177.9 7.6 %collective-permute-start.25 = (f32[1280,128]{1,0:T(8,128)}, f32[1280,128]{1,0:T(8,128)S(1)}, u32[]{:S(2)}, u32[]{:S(2)}) collective-permute-start(f32[1280,128]{1,0:T(8,128)} %get-tuple-element.196), channel_id=1, source_target_pairs={{45,29},{109,93}} | collective-permute-start | bytes 1966088 | tf_op jit(solution)/shard_map/ppermute | solution.py:339
  186.4 4.3 collective-permute-start.26
  187.1 3.6 collective-permute-start.27
  195.4 2.9 collective-permute-start.28
  196.1 2.2 collective-permute-start.29
  196.9 8.5 %collective-permute-start.30 = (f32[1280,128]{1,0:T(8,128)}, f32[1280,128]{1,0:T(8,128)S(1)}, u32[]{:S(2)}, u32[]{:S(2)}) collective-permute-start(f32[1280,128]{1,0:T(8,128)} %get-tuple-element.210), channel_id=1, source_target_pairs={{29,61}} | collective-permute-start | bytes 1966088 | tf_op jit(solution)/shard_map/ppermute | solution.py:339
  197.6 7.8 %collective-permute-start.31 = (f32[1280,128]{1,0:T(8,128)}, f32[1280,128]{1,0:T(8,128)S(1)}, u32[]{:S(2)}, u32[]{:S(2)}) collective-permute-start(f32[1280,128]{1,0:T(8,128)} %get-tuple-element.210), channel_id=1, source_target_pairs={{93,61}} | collective-permute-start | bytes 1966088 | tf_op jit(solution)/shard_map/ppermute | solution.py:339
  206.2 5.9 %collective-permute-start.32 = (f32[2688,128]{1,0:T(8,128)}, f32[2688,128]{1,0:T(8,128)S(1)}, u32[]{:S(2)}, u32[]{:S(2)}) collective-permute-start(f32[2688,128]{1,0:T(8,128)} %get-tuple-element.217), channel_id=1, source_target_pairs={{29,61}} | collective-permute-start | bytes 4128776 | tf_op jit(solution)/shard_map/ppermute | solution.py:339
  207.0 5.2 collective-permute-start.33
  216.9 7.0 %collective-permute-start.35 = (f32[1920,128]{1,0:T(8,128)}, f32[1920,128]{1,0:T(8,128)S(1)}, u32[]{:S(2)}, u32[]{:S(2)}) collective-permute-start(f32[1920,128]{1,0:T(8,128)} %get-tuple-element.224), channel_id=1, source_target_pairs={{61,93},{125,61},{93,125}} | collective-permute-start | bytes 2949128 | tf_op jit(solution)/shard_map/ppermute | solution.py:339
  217.6 5.6 %collective-permute-start.34 = (f32[1280,128]{1,0:T(8,128)}, f32[1280,128]{1,0:T(8,128)S(1)}, u32[]{:S(2)}, u32[]{:S(2)}) collective-permute-start(f32[1280,128]{1,0:T(8,128)} %get-tuple-element.222), channel_id=1, source_target_pairs={{61,125}} | collective-permute-start | bytes 1966088 | tf_op jit(solution)/shard_map/ppermute | solution.py:339
  223.2 4.6 collective-permute-start.36
  236.1 1.3 collective-permute-start.38
  236.8 0.7 collective-permute-start.39
  240.8 1.3 collective-permute-start.40
  245.5 1.3 collective-permute-start.42
  250.2 1.3 collective-permute-start.44
  254.9 1.3 collective-permute-start.46
  259.6 238.2 %collective-permute-start.48 = (f32[1,640]{1,0:T(1,128)}, f32[1,640]{1,0:T(1,128)S(1)}, u32[]{:S(2)}, u32[]{:S(2)}) collective-permute-start(f32[1,640]{1,0:T(1,128)} %shard_map.114.refs_2_), channel_id=1, source_target_pairs={{1,2},{3,6},{7,4},{5,8},{9,10},{11,14},{15,12},{13,16},{17,18},{19... | collective-permute-start | bytes 7688 | tf_op jit(solution)/shard_map/ppermute | solution.py:339
  260.9 243.5 %collective-permute-start.49 = (f32[1,640]{1,0:T(1,128)}, f32[1,640]{1,0:T(1,128)S(1)}, u32[]{:S(2)}, u32[]{:S(2)}) collective-permute-start(f32[1,640]{1,0:T(1,128)} %shard_map.114.refs_2_), channel_id=1, source_target_pairs={{1,0},{3,2},{7,6},{5,4},{9,8},{11,10},{15,14},{13,12},{17,16},{19,... | collective-permute-start | bytes 7688 | tf_op jit(solution)/shard_map/ppermute | solution.py:339
  509.0 8.4 %all-to-all-start.2 = ((f32[1,4,128]{2,0,1:T(1,128)}), f32[1,4,128]{2,0,1:T(1,128)S(1)}, u32[]{:S(2)}, u32[]{:S(2)}) async-start(f32[1,4,128]{2,0,1:T(1,128)} %slice_bitcast_fusion), calls=%async_computation.2 | async-start | bytes 4096 | tf_op jit(solution)/shard_map/all_to_all | solution.py:472
  (62 other events, 100.2 us)
